TPU v7x, 32 devices: a whole 2x2x4 slice. The times are simulated.
32 devices in a mesh: group: 2 (over y), seq: 4 (over z), shard: 2 (over x), guide: 2 (over core).
Axes of the slice: x: 2, y: 2, z: 4, core: 2. Of those that a mesh axis runs over, the one named last changes fastest.
Arguments:
- queries: bfloat16 [2, 2, 512, 2560], P('guide', 'group', 'seq', 'shard'), parts along dimension 1, may hold values from -120 to 120
- key_vecs: bfloat16 [2, 2, 512, 2560], P('guide', 'group', 'seq', 'shard'), parts along dimension 1, may hold values from -4 to 4
- value_vecs: bfloat16 [2, 2, 512, 2560], P('guide', 'group', 'seq', 'shard'), parts along dimension 1, may hold values from -24 to 24
- residual: bfloat16 [2, 2, 512, 5120], P('guide', 'group', 'seq', 'shard'), parts along dimension 1, may hold values from -64 to 64
- w_out: bfloat16 [2560, 5120], P('shard', 'guide'), may hold values from -0.125 to 0.125
- attn_gate: float32 [2, 5120], P('group', 'shard'), parts along dimension 0, may hold values from 2 to 4
- norm_shift: float32 [2, 5120], P('group', 'shard'), parts along dimension 0, may hold values from -3 to 3
- norm_scale: float32 [2, 5120], P('group', 'shard'), parts along dimension 0, may hold values from -2.5 to 2.5
- w_head: bfloat16 [5120, 64], P('shard'), may hold values from -0.078125 to 0.078125
- noise: float32 [2, 4, 128, 64], P('group', 'seq', None, 'guide'), parts along dimension 0, may hold values from -6 to 6
- timesteps: int32 [2], P('group'), parts along dimension 0, may hold values from 100 to 980
- frame_owner: int32 [2, 4], P('group'), parts along dimension 0, may hold values from 0 to 3, each once within a row
Outputs:
- sds_grad: float32 [2, 4, 128, 64], P('group', 'seq', None, 'guide'), parts along dimension 0
There are 2 independent parts, one for each index of `group`. A program takes and returns all parts, laid end to end along the dimension named above; an argument that names none is the same for every part. Nothing has to cross between parts.
Inputs may be any that keep to these rules, and one draw needn't show every extreme that they name: `frame_owner`: each row names every owner index once.
All inputs are finite; a program needn't handle non-finite values.
Results may differ from a plain program's by a relative error of at most 0.003.
Values may be sent and summed in bfloat16 or wider, within the bound.
No kernel may reach another device: no remote copies, remote signals or barrier semaphores. Data moves between devices by JAX's collectives and lax.ppermute only.
A program may use at most 128 MiB of HBM per device.

v0:
```python
import functools

import jax
import jax.numpy as jnp
from jax import lax
from jax.experimental import pallas as pl
from jax.experimental.pallas import tpu as pltpu
from jax.sharding import PartitionSpec as P


HEAD_DIM = 128
LANES = 128
SUBLANES = 8
beta_low = 0.0001
beta_high = 0.02
guidance_scale = 3.0
norm_epsilon = 1e-06
LOG2E = 1.4426950408889634


F32 = jnp.float32
BF16 = jnp.bfloat16
VMEM_SPEC = pl.BlockSpec(memory_space=pltpu.VMEM)
SMEM_SPEC = pl.BlockSpec(memory_space=pltpu.SMEM)
HBM_SPEC = pl.BlockSpec(memory_space=pltpu.HBM)


def plan_weight(timesteps):
    steps_float = timesteps.astype(jnp.float32)
    exponent = (steps_float + 1.0) * beta_low + (beta_high - beta_low) * steps_float * (
        steps_float + 1.0
    ) / (2.0 * 999.0)
    return 1.0 - jnp.exp(-exponent)


def attend_all(query_split, keys_all, values_all):
    heads_local = query_split.shape[2]
    keys_split = keys_all.reshape(keys_all.shape[0], keys_all.shape[1], heads_local, HEAD_DIM)
    values_split = values_all.reshape(values_all.shape[0], values_all.shape[1], heads_local, HEAD_DIM)
    scores = jnp.einsum(
        "tqhd,tkhd->tqhk", query_split, keys_split, preferred_element_type=F32
    ) * HEAD_DIM ** (-0.5)
    expo = jnp.exp(scores - jnp.max(scores, axis=-1, keepdims=True))
    total = jnp.sum(expo, axis=-1)
    mixed = jnp.einsum("tqhk,tkhd->tqhd", expo.astype(BF16), values_split, preferred_element_type=F32)
    return (mixed / total[..., None]).astype(BF16)


def general_plan(
    queries, key_vecs, value_vecs, residual, w_out, attn_gate, norm_shift, norm_scale, w_head, noise,
    timesteps, frame_owner,
):
    query_local = queries[0]
    step_count, token_count, width_local = query_local.shape
    heads_local = width_local // HEAD_DIM
    attended = attend_all(
        query_local.reshape(step_count, token_count, heads_local, HEAD_DIM),
        lax.all_gather(key_vecs[0], "seq", axis=1, tiled=True),
        lax.all_gather(value_vecs[0], "seq", axis=1, tiled=True),
    )
    row_count = step_count * token_count
    both_rows = jnp.dot(
        lax.all_gather(attended.reshape(row_count, width_local), "guide", axis=0, tiled=True),
        w_out,
        preferred_element_type=F32,
    )
    half_width = w_out.shape[1]
    swapped = lax.all_to_all(
        both_rows.reshape(2, row_count, half_width), "guide", split_axis=0, concat_axis=2, tiled=True
    )
    projected = swapped.reshape(row_count, 2 * half_width)
    attn_out = lax.psum_scatter(projected, "shard", scatter_dimension=1, tiled=True)
    width_shard = attn_out.shape[1]
    width_model = width_shard * lax.axis_size("shard")
    hidden = residual[0].astype(F32) + attn_gate[:, None, :] * attn_out.reshape(
        step_count, token_count, width_shard
    )
    sum_first, sum_second = lax.psum((jnp.sum(hidden, axis=-1), jnp.sum(hidden * hidden, axis=-1)), "shard")
    mean_row = sum_first / width_model
    var_row = sum_second / width_model - mean_row * mean_row
    inv_std = lax.rsqrt(var_row + norm_epsilon)
    modulated = (hidden - mean_row[..., None]) * inv_std[..., None] * (
        1.0 + norm_scale[:, None, :]
    ) + norm_shift[:, None, :]
    partial_head = jnp.einsum(
        "tqd,dc->tqc", modulated, w_head.astype(F32), precision=lax.Precision.HIGHEST
    )
    predicted = lax.psum(partial_head, "shard")
    seq_count = lax.axis_size("seq")
    frame_group = token_count // seq_count
    frames_view = predicted.reshape(step_count, seq_count, frame_group, predicted.shape[-1])
    owner_table = (
        frame_owner[:, :, None] == jnp.arange(seq_count, dtype=jnp.int32)[None, None, :]
    ).astype(F32)
    by_owner = jnp.einsum("tfo,tfgc->togc", owner_table, frames_view, precision=lax.Precision.HIGHEST)
    arrived = lax.all_to_all(
        lax.all_to_all(by_owner[None], "seq", split_axis=2, concat_axis=3, tiled=True),
        "guide",
        split_axis=4,
        concat_axis=0,
        tiled=True,
    )
    guided = arrived[1] + guidance_scale * (arrived[0] - arrived[1])
    return plan_weight(timesteps)[:, None, None, None] * (guided - noise)


def pack_kernel(parts, half, count, *refs):
    source_refs, out_refs, sems = refs[:count], refs[count:-1], refs[-1]
    z = lax.axis_index("seq")
    copies = []
    for j in range(parts):
        cols = pl.ds(pl.multiple_of(lax.rem(z + j, parts) * half, LANES), half)
        for i in range(count):
            copies.append(
                pltpu.make_async_copy(source_refs[i].at[:, cols], out_refs[j].at[i], sems.at[j * count + i])
            )
    for copy in copies:
        copy.start()
    for copy in copies:
        copy.wait()


def attend_kernel(parts, *refs):
    q_refs = refs[:parts]
    kv_refs = refs[parts : 3 * parts]
    o_refs = refs[3 * parts : 4 * parts]
    score_scr, total_scr = refs[4 * parts :]
    heads = q_refs[0].shape[2] // HEAD_DIM
    rows = q_refs[0].shape[1]
    for i in range(heads):
        cols = slice(i * HEAD_DIM, (i + 1) * HEAD_DIM)
        q = jnp.concatenate([r[0, :, cols] for r in q_refs], axis=0)
        for b, kv_ref in enumerate(kv_refs):
            scores = lax.dot_general(q, kv_ref[0, :, cols], (((1,), (1,)), ((), ())), preferred_element_type=F32)
            score_scr[i, :, b * rows : (b + 1) * rows] = scores * (HEAD_DIM ** (-0.5) * LOG2E)
    for i in range(heads):
        scores = score_scr[i]
        expo = jnp.exp2(scores - jnp.max(scores, axis=1, keepdims=True))
        score_scr[i] = expo
        total_scr[i] = jnp.broadcast_to(jnp.sum(expo, axis=1, keepdims=True), total_scr.shape[1:])
    for i in range(heads):
        cols = slice(i * HEAD_DIM, (i + 1) * HEAD_DIM)
        values = jnp.concatenate([r[1, :, cols] for r in kv_refs], axis=0)
        mixed = jnp.dot(score_scr[i].astype(BF16), values, preferred_element_type=F32) / total_scr[i]
        for j in range(parts):
            o_refs[j][:, cols] = mixed[j * rows : (j + 1) * rows].astype(BF16)


def project(parts, half, o_refs, w_ref, cols):
    z = lax.axis_index("seq")
    total = None
    for j in range(parts):
        start = pl.multiple_of(lax.rem(z + j, parts) * half, LANES)
        term = jnp.dot(o_refs[j][...], w_ref[pl.ds(start, half), cols], preferred_element_type=F32)
        total = term if total is None else total + term
    return total


def send_kernel(parts, half, chunk, first, *refs):
    o_refs = refs[:parts]
    near_ref, far_ref, out_ref = refs[parts:]
    guide = lax.axis_index("guide")
    for value, w_ref in ((1, near_ref), (0, far_ref)):

        @pl.when(guide == value)
        def _():
            for t in range(out_ref.shape[1] // chunk):
                cols = slice(first + t * chunk, first + (t + 1) * chunk)
                out_ref[:, t * chunk : (t + 1) * chunk] = project(parts, half, o_refs, w_ref, cols).astype(BF16)


def keep_kernel(parts, half, chunk, *refs):
    o_refs = refs[:parts]
    near_ref, far_ref, gate_ref, out_ref = refs[parts:]
    guide = lax.axis_index("guide")
    for value, w_ref in ((0, near_ref), (1, far_ref)):

        @pl.when(guide == value)
        def _():
            for t in range(out_ref.shape[1] // chunk):
                cols = slice(t * chunk, (t + 1) * chunk)
                out_ref[:, cols] = gate_ref[:, cols] * project(parts, half, o_refs, w_ref, cols)


def split_dot(head_t, rows):
    dims = (((1,), (1,)), ((), ()))
    high = rows.astype(BF16)
    low = (rows - high.astype(F32)).astype(BF16)
    return lax.dot_general(head_t, high, dims, preferred_element_type=F32) + lax.dot_general(
        head_t, low, dims, preferred_element_type=F32
    )


def early_kernel(seq_count, scale_ref, shift_ref, head_ref, owner_ref, steps_ref, out_ref, chosen_ref, weight_ref):
    z = lax.axis_index("seq")
    for k in range(seq_count):
        for f in range(seq_count):
            here = jnp.where(owner_ref[0, f] == z ^ k, 1.0, 0.0)
            chosen_ref[k * seq_count + f : k * seq_count + f + 1, :] = jnp.full((1, LANES), here, F32)
    weight_ref[...] = plan_weight(jnp.full((SUBLANES, LANES), steps_ref[0], jnp.int32))
    width = scale_ref.shape[1]
    which = lax.broadcasted_iota(jnp.int32, (LANES, width), 0)
    rows = jnp.where(which == 0, 1.0 + scale_ref[...], shift_ref[...])
    high = rows.astype(BF16)
    rest = rows - high.astype(F32)
    mid = rest.astype(BF16)
    low = (rest - mid.astype(F32)).astype(BF16)
    dims = (((1,), (1,)), ((), ()))
    total = None
    for part in (high, mid, low):
        term = lax.dot_general(head_ref[...], part, dims, preferred_element_type=F32)
        total = term if total is None else total + term
    out_ref[...] = total


def head_kernel(first, last, chunk, start, *refs):
    res_ref, hid_ref, got_ref, gate_ref, scale_ref, head_ref = refs[:6]
    if first:
        out_refs = refs[6:]
    else:
        prev_refs, out_refs = refs[6:9], refs[9:]
    channels = head_ref.shape[0]
    rows = hid_ref.shape[0]
    acc_one = jnp.zeros((rows, LANES), F32) if first else prev_refs[1][...]
    acc_two = jnp.zeros((rows, LANES), F32) if first else prev_refs[2][...]
    acc_head = jnp.zeros((channels, rows), F32) if first else prev_refs[0][...]
    for t in range(got_ref.shape[1] // chunk):
        cols = slice(start + t * chunk, start + (t + 1) * chunk)
        arrived = got_ref[:, t * chunk : (t + 1) * chunk].astype(F32)
        hidden = res_ref[:, cols].astype(F32) + hid_ref[:, cols] + gate_ref[:, cols] * arrived
        for s in range(chunk // LANES):
            piece = hidden[:, s * LANES : (s + 1) * LANES]
            acc_one = acc_one + piece
            acc_two = acc_two + piece * piece
        acc_head = acc_head + split_dot(head_ref[:, cols], hidden * (1.0 + scale_ref[:, cols]))
    if last:
        out_ref = out_refs[0]
        out_ref[0:channels, :] = acc_head
        sum_one = jnp.sum(acc_one.T, axis=0, keepdims=True)
        sum_two = jnp.sum(acc_two.T, axis=0, keepdims=True)
        row = lax.broadcasted_iota(jnp.int32, (SUBLANES, rows), 0)
        out_ref[channels : channels + SUBLANES, :] = jnp.where(row == 0, sum_one, sum_two)
    else:
        out_refs[0][...] = acc_head
        out_refs[1][...] = acc_one
        out_refs[2][...] = acc_two


def norm_kernel(width_model, own_ref, got_ref, rows_own_ref, rows_got_ref, keep_ref, send_ref, eps_scr):
    channels = rows_own_ref.shape[0]
    half_channels = channels // 2
    guide = lax.axis_index("guide")
    head = own_ref[0:channels, :] + got_ref[0:channels, :]
    stats = own_ref[channels : channels + SUBLANES, :] + got_ref[channels : channels + SUBLANES, :]
    mean = stats[0:1] / width_model
    var = stats[1:2] / width_model - mean * mean
    inv_std = lax.rsqrt(var + norm_epsilon)
    scaled = rows_own_ref[:, 0:1] + rows_got_ref[:, 0:1]
    shifted = rows_own_ref[:, 1:2] + rows_got_ref[:, 1:2]
    eps_scr[...] = (head - mean * scaled) * inv_std + shifted
    keep_ref[...] = eps_scr[pl.ds(pl.multiple_of(guide * half_channels, SUBLANES), half_channels), :]
    send_ref[...] = eps_scr[pl.ds(pl.multiple_of((1 - guide) * half_channels, SUBLANES), half_channels), :]


def frame_kernel(seq_count, group, chosen_ref, keep_ref, got_ref, *out_refs):
    first = lax.axis_index("guide") == 0
    mine, other = keep_ref[...], got_ref[...]
    fold = LANES // group
    rows = mine.shape[0] // fold
    lane = lax.broadcasted_iota(jnp.int32, (rows, LANES), 1) // group
    for sub, block in enumerate((jnp.where(first, mine, other), jnp.where(first, other, mine))):
        packed = []
        for f in range(seq_count):
            frame = jnp.zeros((rows, LANES), F32)
            for j in range(fold):
                piece = block[j * rows : (j + 1) * rows]
                shift = (j - f) * group % LANES
                frame = jnp.where(lane == j, pltpu.roll(piece, shift, axis=1) if shift else piece, frame)
            packed.append(frame)
        for k in range(seq_count):
            frame = packed[0]
            for f in range(1, seq_count):
                frame = jnp.where(chosen_ref[k * seq_count + f : k * seq_count + f + 1, :] > 0.5, packed[f], frame)
            out_refs[k][sub * rows : (sub + 1) * rows, :] = frame


def final_kernel(seq_count, group, weight_ref, noise_ref, *refs):
    piece_refs, out_ref = refs[:seq_count], refs[seq_count]
    z = lax.axis_index("seq")
    parts = seq_count // 2
    fold = LANES // group
    rows = piece_refs[0].shape[0] // 2
    lane = lax.broadcasted_iota(jnp.int32, (rows, LANES), 1) // group
    for j in range(fold):
        eps_cond = jnp.zeros((rows, LANES), F32)
        eps_free = jnp.zeros((rows, LANES), F32)
        for k in range(seq_count):
            source = z ^ k
            branch, position = source // parts, lax.rem(source, parts)
            for sub in range(2):
                block = parts * sub + position
                shift = lax.rem((block - j) * group + LANES, LANES)
                rolled = pltpu.roll(piece_refs[k][sub * rows : (sub + 1) * rows], shift, axis=1)
                eps_cond = jnp.where((lane == block) & (branch == 0), rolled, eps_cond)
                eps_free = jnp.where((lane == block) & (branch == 1), rolled, eps_free)
        part = slice(j * rows, (j + 1) * rows)
        guided = eps_free + guidance_scale * (eps_cond - eps_free)
        out_ref[part, :] = weight_ref[0:1, :] * (guided - noise_ref[part, :])


def call(kernel, outs, args, specs=None, scratch=(), flops=0, moved=0, grant=16):
    shapes = [jax.ShapeDtypeStruct(s, d) for s, d in outs]
    return pl.pallas_call(
        kernel,
        out_shape=shapes,
        in_specs=specs or [VMEM_SPEC] * len(args),
        out_specs=[VMEM_SPEC] * len(outs),
        scratch_shapes=list(scratch),
        compiler_params=pltpu.CompilerParams(vmem_limit_bytes=grant << 20),
        cost_estimate=pl.CostEstimate(flops=flops, bytes_accessed=moved, transcendentals=0),
    )(*args)


def fast_plan(
    queries, key_vecs, value_vecs, residual, w_out, attn_gate, norm_shift, norm_scale, w_head, noise,
    timesteps, frame_owner,
):
    seq_count = lax.axis_size("seq")
    parts = seq_count // 2
    rows, width_local = queries.shape[2:]
    half = width_local // parts
    width_shard = residual.shape[3]
    channels = w_head.shape[1]
    group = rows // seq_count
    width_model = float(width_shard * lax.axis_size("shard"))
    both = [(0, 1), (1, 0)]
    axes = ("seq", "guide")

    crossed = [(x * 2 + c, x * 2 + (c + x) % 2) for x in range(2) for c in range(2)]
    straight = [(x * 2 + c, x * 2 + (c + x + 1) % 2) for x in range(2) for c in range(2)]

    def pack(*arrays):
        return call(
            functools.partial(pack_kernel, parts, half, len(arrays)),
            [((len(arrays), rows, half), BF16)] * parts,
            [pltpu.with_memory_space_constraint(array[0, 0], pltpu.HBM) for array in arrays],
            [HBM_SPEC] * len(arrays),
            [pltpu.SemaphoreType.DMA((parts * len(arrays),))],
            moved=4 * len(arrays) * rows * width_local,
        )

    kv_sent = pack(key_vecs, value_vecs)
    there = [
        [
            (z * 2 + c, (parts * c + (z + j) % parts) * 2 + z // parts)
            for z in range(seq_count)
            for c in range(2)
        ]
        for j in range(parts)
    ]
    inside = [[(z, z // parts * parts + (z - j) % parts) for z in range(seq_count)] for j in range(parts)]
    kv_own = [lax.ppermute(kv_sent[j], axes, there[j]) for j in range(parts)]
    q_sent = pack(queries)
    q_own = [lax.ppermute(q_sent[j], axes, there[j]) for j in range(parts)]
    near_w = lax.ppermute(w_out, ("shard", "guide"), crossed)
    far_w = lax.ppermute(w_out, ("shard", "guide"), straight)
    kv_other = [lax.ppermute(block, "guide", both) for block in kv_own]
    res_here = lax.ppermute(residual[0, 0], axes, there[0])

    head_t = w_head.T
    rows_own, chosen, weight = call(
        functools.partial(early_kernel, seq_count),
        [((channels, LANES), F32), ((seq_count * seq_count, LANES), F32), ((SUBLANES, LANES), F32)],
        [norm_scale, norm_shift, head_t, frame_owner, timesteps],
        [VMEM_SPEC] * 3 + [SMEM_SPEC] * 2,
        moved=4 * width_shard * LANES,
    )
    rows_got = lax.ppermute(rows_own, "shard", both)
    *q_own, rows_own = lax.optimization_barrier((*q_own, rows_own))

    mixed = call(
        functools.partial(attend_kernel, parts),
        [((rows, half), BF16)] * parts,
        q_own + kv_own + kv_other,
        scratch=[
            pltpu.VMEM((half // HEAD_DIM, rows * parts, 2 * parts * rows), F32),
            pltpu.VMEM((half // HEAD_DIM, rows * parts, HEAD_DIM), F32),
        ],
        flops=8 * rows * parts * rows * parts * half,
        moved=2 * rows * half * parts * 6,
    )
    mixed = [mixed[0]] + [lax.ppermute(mixed[j], "seq", inside[j]) for j in range(1, parts)]

    chunk = 128
    pieces = 4
    width_piece = width_shard // pieces
    got = []
    for i in range(pieces):
        partial = call(
            functools.partial(send_kernel, parts, half, chunk, i * width_piece),
            [((rows, width_piece), BF16)],
            mixed + [near_w, far_w],
            flops=2 * rows * width_local * width_piece,
            moved=2 * width_local * width_piece,
        )[0]
        got.append(lax.ppermute(partial, "shard", both))
    hidden = call(
        functools.partial(keep_kernel, parts, half, chunk),
        [((rows, width_shard), F32)],
        mixed + [near_w, far_w, attn_gate],
        flops=2 * rows * width_local * width_shard,
        moved=2 * width_local * width_shard,
    )[0]
    state = []
    for i in range(pieces):
        first, last = i == 0, i == pieces - 1
        state = call(
            functools.partial(head_kernel, first, last, chunk, i * width_piece),
            [((channels + SUBLANES, rows), F32)]
            if last
            else [((channels, rows), F32), ((rows, LANES), F32), ((rows, LANES), F32)],
            [res_here, hidden, got[i], attn_gate, norm_scale, head_t] + list(state),
            flops=4 * rows * channels * width_piece,
            moved=6 * rows * width_piece,
        )
    sums = state[0]
    sums_got = lax.ppermute(sums, "shard", both)
    keep, send = call(
        functools.partial(norm_kernel, width_model),
        [((channels // 2, rows), F32)] * 2,
        [sums, sums_got, rows_own, rows_got],
        scratch=[pltpu.VMEM((channels, rows), F32)],
    )
    eps_got = lax.ppermute(send, "guide", both)
    fold = LANES // group
    frames = call(
        functools.partial(frame_kernel, seq_count, group),
        [((channels // fold, LANES), F32)] * seq_count,
        [chosen, keep, eps_got],
    )
    arrived = [frames[0]] + [
        lax.ppermute(frames[k], "seq", [(z, z ^ k) for z in range(seq_count)])
        for k in range(1, seq_count)
    ]
    out = call(
        functools.partial(final_kernel, seq_count, group),
        [((channels // 2, rows), F32)],
        [weight, noise[0, 0].T] + arrived,
    )[0]
    return out.T[None, None]


def fast_fits(sizes, queries, residual, w_out, w_head):
    seq_count = sizes["seq"]
    step_count, rows, width_local = queries.shape[1:]
    channels = w_head.shape[1]
    if seq_count < 2 or sizes["guide"] != 2 or sizes["shard"] != 2 or seq_count & (seq_count - 1) or step_count != 1 or rows != LANES:
        return False
    if width_local % (seq_count // 2 * HEAD_DIM) or residual.shape[3] % (4 * LANES):
        return False
    if w_out.shape[1] != residual.shape[3] or channels % (2 * SUBLANES):
        return False
    group = rows // seq_count
    if rows % seq_count or LANES % group:
        return False
    fold = LANES // group
    return channels // 2 % (fold * SUBLANES) == 0


def solution(mesh):
    sizes = dict(mesh.shape)

    def on_device(queries, key_vecs, value_vecs, residual, w_out, attn_gate, norm_shift, norm_scale, w_head, *rest):
        fits = fast_fits(sizes, queries, residual, w_out, w_head)
        plan = fast_plan if fits else general_plan
        return plan(queries, key_vecs, value_vecs, residual, w_out, attn_gate, norm_shift, norm_scale, w_head, *rest)

    return jax.shard_map(
        on_device,
        mesh=mesh,
        in_specs=(
            P("guide", "group", "seq", "shard"),
            P("guide", "group", "seq", "shard"),
            P("guide", "group", "seq", "shard"),
            P("guide", "group", "seq", "shard"),
            P("shard", "guide"),
            P("group", "shard"),
            P("group", "shard"),
            P("group", "shard"),
            P("shard", None),
            P("group", "seq", None, "guide"),
            P("group"),
            P("group", None),
        ),
        out_specs=P("group", "seq", None, "guide"),
        check_vma=False,
    )
```

profile of v0, /device:TPU:0, one launch (start us, length us, event | category | flops | bytes accessed | tf_op | source)
XLA Modules:
  0.0 85.7 jit_solution(12975966595607200306)
XLA Ops:
  0.0 3.5 %collective-permute-start.8 = (bf16[1280,2560]{1,0:T(8,128)(2,1)}, bf16[1280,2560]{1,0:T(8,128)(2,1)S(1)}, u32[]{:S(2)}, u32[]{:S(2)}) collective-permute-start(bf16[1280,2560]{1,0:T(8,128)(2,1)} %param.16), channel_id=1, source_target_pairs={{0,0},{1,1},{2,3},{3,2},{4,4},{5,5},{6,7},{7,6},{8,8},{9,9},{10,11... | collective-permute-start | bytes 19660808 | tf_op jit(solution)/shard_map/ppermute | solution.py:365
  3.5 2.4 %collective-permute-start.9 = (bf16[1280,2560]{1,0:T(8,128)(2,1)}, bf16[1280,2560]{1,0:T(8,128)(2,1)S(1)}, u32[]{:S(2)}, u32[]{:S(2)}) collective-permute-start(bf16[1280,2560]{1,0:T(8,128)(2,1)} %param.16), channel_id=1, source_target_pairs={{0,1},{1,0},{2,2},{3,3},{4,5},{5,4},{6,6},{7,7},{8,9},{9,8},{10,10... | collective-permute-start | bytes 19660808 | tf_op jit(solution)/shard_map/ppermute | solution.py:366
  5.9 1.2 %shard_map.120 = (bf16[2,128,640]{2,1,0:T(8,128)(2,1)S(1)}, bf16[2,128,640]{2,1,0:T(8,128)(2,1)S(1)}) custom-call(bf16[128,1280]{1,0:T(8,128)(2,1)} %bitcast.17, bf16[128,1280]{1,0:T(8,128)(2,1)} %bitcast.18), custom_call_target="tpu_custom_call" | custom-call | bytes 1310720 | tf_op jit(solution)/shard_map/pallas_call | solution.py:313
  7.8 2.6 %collective-permute-start.4 = (bf16[2,128,640]{2,1,0:T(8,128)(2,1)S(1)}, bf16[2,128,640]{2,1,0:T(8,128)(2,1)S(1)}, u32[]{:S(2)}, u32[]{:S(2)}) collective-permute-start(bf16[2,128,640]{2,1,0:T(8,128)(2,1)S(1)} %get-tuple-element.40), channel_id=1, source_target_pairs={{0,4},{1,12},{4,0},{5,8},{8,5},{9,13},{12,1},{13,9},{2,6},{3,14},{... | collective-permute-start | bytes 983048 | tf_op jit(solution)/shard_map/ppermute | solution.py:362
  10.4 1.0 %shard_map.119 = (bf16[1,128,640]{2,1,0:T(8,128)(2,1)S(1)}, bf16[1,128,640]{2,1,0:T(8,128)(2,1)S(1)}) custom-call(bf16[128,1280]{1,0:T(8,128)(2,1)} %bitcast.19), custom_call_target="tpu_custom_call" | custom-call | bytes 655360 | tf_op jit(solution)/shard_map/pallas_call | solution.py:313
  12.2 22.9 %collective-permute-start.5 = (bf16[2,128,640]{2,1,0:T(8,128)(2,1)S(1)}, bf16[2,128,640]{2,1,0:T(8,128)(2,1)S(1)}, u32[]{:S(2)}, u32[]{:S(2)}) collective-permute-start(bf16[2,128,640]{2,1,0:T(8,128)(2,1)S(1)} %collective-permute-done.3.refs_2_), channel_id=1, source_target_pairs={{0,1},{1,0},{2,3},{3,2},{4,5},{5,4},{6,7},{7,6},{8,9},{9,8},{10,11... | collective-permute-start | bytes 983048 | tf_op jit(solution)/shard_map/ppermute | solution.py:367
  35.2 1.7 %collective-permute-start = (bf16[128,2560]{1,0:T(8,128)(2,1)}, bf16[128,2560]{1,0:T(8,128)(2,1)S(1)}, u32[]{:S(2)}, u32[]{:S(2)}) collective-permute-start(bf16[128,2560]{1,0:T(8,128)(2,1)} %bitcast.20), channel_id=1, source_target_pairs={{0,0},{1,8},{4,4},{5,12},{8,1},{9,9},{12,5},{13,13},{2,2},{3,10},{... | collective-permute-start | bytes 1966088 | tf_op jit(solution)/shard_map/ppermute | solution.py:368
  37.6 1.0 %copy-done = bf16[2560,64]{0,1:T(8,128)(2,1)S(1)} copy-done((bf16[2560,64]{0,1:T(8,128)(2,1)S(1)}, bf16[2560,64]{0,1:T(8,128)(2,1)}, u32[]{:S(2)}) %copy-start) | copy-done | bytes 327704
  40.6 1.3 %shard_map.118 = (f32[64,128]{1,0:T(8,128)S(1)}, f32[16,128]{1,0:T(8,128)S(1)}, f32[8,128]{1,0:T(8,128)S(1)}) custom-call(f32[1,2560]{1,0:T(1,128)S(1)} %copy-done.3, f32[1,2560]{1,0:T(1,128)S(1)} %copy-done.6, bf16[64,2560]{1,0:T(8,128)(2,1)S(1)} %bitcast.11, s32[1,4]{1,0:T(1,128)S(1)} %copy-done.7, s32[1]{0:T(128)S(6)} %copy.13.steps_ref), custom_call_target="tpu_custom_call" | custom-call | bytes 1310720 | tf_op jit(solution)/shard_map/pallas_call | solution.py:313
  42.0 1.2 %shard_map.121 = (bf16[128,640]{1,0:T(8,128)(2,1)S(1)}, bf16[128,640]{1,0:T(8,128)(2,1)S(1)}) custom-call(bf16[1,128,640]{2,1,0:T(8,128)(2,1)S(1)} %collective-permute-done.1.refs_0_, bf16[1,128,640]{2,1,0:T(8,128)(2,1)S(1)} %collective-permute-done.2.refs_1_, bf16[2,128,640]{2,1,0:T(8,128)(2,1)S(1)} %collective-permute-done.3.refs_2_, ...), custom_call_target="tpu_custom_call" | custom-call | flops 335544320 | bytes 1966080 | tf_op jit(solution)/shard_map/pallas_call | solution.py:313
  43.2 5.7 %collective-permute-done.7.refs_1_ = bf16[128,640]{1,0:T(8,128)(2,1)S(1)} collective-permute-done((bf16[128,640]{1,0:T(8,128)(2,1)S(1)}, bf16[128,640]{1,0:T(8,128)(2,1)S(1)}, u32[]{:S(2)}, u32[]{:S(2)}) %collective-permute-start.7) | collective-permute-done | bytes 163872 | tf_op jit(solution)/shard_map/ppermute | solution.py:392
  49.6 2.0 %collective-permute-start.13 = (bf16[128,640]{1,0:T(8,128)(2,1)S(1)}, bf16[128,640]{1,0:T(8,128)(2,1)S(1)}, u32[]{:S(2)}, u32[]{:S(2)}) collective-permute-start(bf16[128,640]{1,0:T(8,128)(2,1)S(1)} %shard_map.126), channel_id=1, source_target_pairs={{0,2},{2,0},{1,3},{3,1},{4,6},{6,4},{5,7},{7,5},{8,10},{10,8},{9,1... | collective-permute-start | bytes 491528 | tf_op jit(solution)/shard_map/ppermute | solution.py:406
  53.0 2.0 %collective-permute-start.11 = (bf16[128,640]{1,0:T(8,128)(2,1)S(1)}, bf16[128,640]{1,0:T(8,128)(2,1)S(1)}, u32[]{:S(2)}, u32[]{:S(2)}) collective-permute-start(bf16[128,640]{1,0:T(8,128)(2,1)S(1)} %shard_map.124), channel_id=1, source_target_pairs={{0,2},{2,0},{1,3},{3,1},{4,6},{6,4},{5,7},{7,5},{8,10},{10,8},{9,1... | collective-permute-start | bytes 491528 | tf_op jit(solution)/shard_map/ppermute | solution.py:406
  55.8 2.3 %shard_map.122.refs_1_ = f32[128,2560]{1,0:T(8,128)S(1)} custom-call(bf16[128,640]{1,0:T(8,128)(2,1)S(1)} %get-tuple-element.41.refs_0_, bf16[128,640]{1,0:T(8,128)(2,1)S(1)} %collective-permute-done.7.refs_1_, bf16[1280,2560]{1,0:T(8,128)(2,1)S(1)} %collective-permute-done.8.refs_2_, bf16[1280,2560]{1,0:T(8,128)(2,1)S(1)} %collective-permute-done.9.refs_3_, ...), custom_call_target="tpu_custom_call" | custom-call | flops 838860800 | bytes 6553600 | tf_op jit(solution)/shard_map/pallas_call | solution.py:313
  59.3 3.2 %collective-permute-done.11.refs_2_ = bf16[128,640]{1,0:T(8,128)(2,1)S(1)} collective-permute-done((bf16[128,640]{1,0:T(8,128)(2,1)S(1)}, bf16[128,640]{1,0:T(8,128)(2,1)S(1)}, u32[]{:S(2)}, u32[]{:S(2)}) %collective-permute-start.11) | collective-permute-done | bytes 163872 | tf_op jit(solution)/shard_map/ppermute | solution.py:406
  62.8 3.2 %collective-permute-done.10.refs_2_ = bf16[128,640]{1,0:T(8,128)(2,1)S(1)} collective-permute-done((bf16[128,640]{1,0:T(8,128)(2,1)S(1)}, bf16[128,640]{1,0:T(8,128)(2,1)S(1)}, u32[]{:S(2)}, u32[]{:S(2)}) %collective-permute-start.10) | collective-permute-done | bytes 163872 | tf_op jit(solution)/shard_map/ppermute | solution.py:406
  67.0 1.4 %collective-permute-start.15 = (f32[64,128]{1,0:T(8,128)S(1)}, f32[64,128]{1,0:T(8,128)S(1)}, u32[]{:S(2)}, u32[]{:S(2)}) collective-permute-start(f32[64,128]{1,0:T(8,128)S(1)} %get-tuple-element.52.rows_own_ref), channel_id=1, source_target_pairs={{0,2},{2,0},{1,3},{3,1},{4,6},{6,4},{5,7},{7,5},{8,10},{10,8},{9,1... | collective-permute-start | bytes 98312 | tf_op jit(solution)/shard_map/ppermute | solution.py:378
  68.4 2.5 %collective-permute-done.15.rows_got_ref = f32[64,128]{1,0:T(8,128)S(1)} collective-permute-done((f32[64,128]{1,0:T(8,128)S(1)}, f32[64,128]{1,0:T(8,128)S(1)}, u32[]{:S(2)}, u32[]{:S(2)}) %collective-permute-start.15) | collective-permute-done | bytes 32800 | tf_op jit(solution)/shard_map/ppermute | solution.py:378
  71.0 1.0 %collective-permute-start.16 = (f32[32,128]{1,0:T(8,128)S(1)}, f32[32,128]{1,0:T(8,128)S(1)}, u32[]{:S(2)}, u32[]{:S(2)}) collective-permute-start(f32[32,128]{1,0:T(8,128)S(1)} %get-tuple-element.54), channel_id=1, source_target_pairs={{0,1},{1,0},{2,3},{3,2},{4,5},{5,4},{6,7},{7,6},{8,9},{9,8},{10,11... | collective-permute-start | bytes 49160 | tf_op jit(solution)/shard_map/ppermute | solution.py:434
  72.0 0.8 collective-permute-done.16.got_ref
  73.0 1.0 %collective-permute-start.17 = (f32[16,128]{1,0:T(8,128)S(1)}, f32[16,128]{1,0:T(8,128)S(1)}, u32[]{:S(2)}, u32[]{:S(2)}) collective-permute-start(f32[16,128]{1,0:T(8,128)S(1)} %get-tuple-element.56), channel_id=1, source_target_pairs={{0,4},{4,0},{8,12},{12,8},{1,5},{5,1},{9,13},{13,9},{2,6},{6,2},{1... | collective-permute-start | bytes 24584 | tf_op jit(solution)/shard_map/ppermute | solution.py:442
  74.0 5.5 %collective-permute-start.18 = (f32[16,128]{1,0:T(8,128)S(1)}, f32[16,128]{1,0:T(8,128)S(1)}, u32[]{:S(2)}, u32[]{:S(2)}) collective-permute-start(f32[16,128]{1,0:T(8,128)S(1)} %get-tuple-element.57), channel_id=1, source_target_pairs={{0,8},{4,12},{8,0},{12,4},{1,9},{5,13},{9,1},{13,5},{2,10},{6,14},... | collective-permute-start | bytes 24584 | tf_op jit(solution)/shard_map/ppermute | solution.py:442
  79.5 1.6 %collective-permute-done.18.refs_2_ = f32[16,128]{1,0:T(8,128)S(1)} collective-permute-done((f32[16,128]{1,0:T(8,128)S(1)}, f32[16,128]{1,0:T(8,128)S(1)}, u32[]{:S(2)}, u32[]{:S(2)}) %collective-permute-start.18) | collective-permute-done | bytes 8224 | tf_op jit(solution)/shard_map/ppermute | solution.py:442
  81.2 3.8 %collective-permute-done.19.refs_3_ = f32[16,128]{1,0:T(8,128)S(1)} collective-permute-done((f32[16,128]{1,0:T(8,128)S(1)}, f32[16,128]{1,0:T(8,128)S(1)}, u32[]{:S(2)}, u32[]{:S(2)}) %collective-permute-start.19) | collective-permute-done | bytes 8224 | tf_op jit(solution)/shard_map/ppermute | solution.py:442
  (48 shorter events, 10.0 us)
Async XLA Ops:
  0.0 48.9 %collective-permute-start.8 = (bf16[1280,2560]{1,0:T(8,128)(2,1)}, bf16[1280,2560]{1,0:T(8,128)(2,1)S(1)}, u32[]{:S(2)}, u32[]{:S(2)}) collective-permute-start(bf16[1280,2560]{1,0:T(8,128)(2,1)} %param.16), channel_id=1, source_target_pairs={{0,0},{1,1},{2,3},{3,2},{4,4},{5,5},{6,7},{7,6},{8,8},{9,9},{10,11... | collective-permute-start | bytes 19660808 | tf_op jit(solution)/shard_map/ppermute | solution.py:365
  3.5 45.4 %collective-permute-start.9 = (bf16[1280,2560]{1,0:T(8,128)(2,1)}, bf16[1280,2560]{1,0:T(8,128)(2,1)S(1)}, u32[]{:S(2)}, u32[]{:S(2)}) collective-permute-start(bf16[1280,2560]{1,0:T(8,128)(2,1)} %param.16), channel_id=1, source_target_pairs={{0,1},{1,0},{2,2},{3,3},{4,5},{5,4},{6,6},{7,7},{8,9},{9,8},{10,10... | collective-permute-start | bytes 19660808 | tf_op jit(solution)/shard_map/ppermute | solution.py:366
  7.1 5.1 %collective-permute-start.3 = (bf16[2,128,640]{2,1,0:T(8,128)(2,1)S(1)}, bf16[2,128,640]{2,1,0:T(8,128)(2,1)S(1)}, u32[]{:S(2)}, u32[]{:S(2)}) collective-permute-start(bf16[2,128,640]{2,1,0:T(8,128)(2,1)S(1)} %get-tuple-element.39), channel_id=1, source_target_pairs={{0,0},{1,8},{4,4},{5,12},{8,1},{9,9},{12,5},{13,13},{2,2},{3,10},{... | collective-permute-start | bytes 983048 | tf_op jit(solution)/shard_map/ppermute | solution.py:362
  7.8 27.3 %collective-permute-start.4 = (bf16[2,128,640]{2,1,0:T(8,128)(2,1)S(1)}, bf16[2,128,640]{2,1,0:T(8,128)(2,1)S(1)}, u32[]{:S(2)}, u32[]{:S(2)}) collective-permute-start(bf16[2,128,640]{2,1,0:T(8,128)(2,1)S(1)} %get-tuple-element.40), channel_id=1, source_target_pairs={{0,4},{1,12},{4,0},{5,8},{8,5},{9,13},{12,1},{13,9},{2,6},{3,14},{... | collective-permute-start | bytes 983048 | tf_op jit(solution)/shard_map/ppermute | solution.py:362
  11.5 0.7 collective-permute-start.1
  12.1 23.0 %collective-permute-start.2 = (bf16[1,128,640]{2,1,0:T(8,128)(2,1)S(1)}, bf16[1,128,640]{2,1,0:T(8,128)(2,1)S(1)}, u32[]{:S(2)}, u32[]{:S(2)}) collective-permute-start(bf16[1,128,640]{2,1,0:T(8,128)(2,1)S(1)} %get-tuple-element.35), channel_id=1, source_target_pairs={{0,4},{1,12},{4,0},{5,8},{8,5},{9,13},{12,1},{13,9},{2,6},{3,14},{... | collective-permute-start | bytes 491528 | tf_op jit(solution)/shard_map/ppermute | solution.py:364
  12.2 29.7 %collective-permute-start.5 = (bf16[2,128,640]{2,1,0:T(8,128)(2,1)S(1)}, bf16[2,128,640]{2,1,0:T(8,128)(2,1)S(1)}, u32[]{:S(2)}, u32[]{:S(2)}) collective-permute-start(bf16[2,128,640]{2,1,0:T(8,128)(2,1)S(1)} %collective-permute-done.3.refs_2_), channel_id=1, source_target_pairs={{0,1},{1,0},{2,3},{3,2},{4,5},{5,4},{6,7},{7,6},{8,9},{9,8},{10,11... | collective-permute-start | bytes 983048 | tf_op jit(solution)/shard_map/ppermute | solution.py:367
  35.1 6.8 %collective-permute-start.6 = (bf16[2,128,640]{2,1,0:T(8,128)(2,1)S(1)}, bf16[2,128,640]{2,1,0:T(8,128)(2,1)S(1)}, u32[]{:S(2)}, u32[]{:S(2)}) collective-permute-start(bf16[2,128,640]{2,1,0:T(8,128)(2,1)S(1)} %collective-permute-done.4.refs_3_), channel_id=1, source_target_pairs={{0,1},{1,0},{2,3},{3,2},{4,5},{5,4},{6,7},{7,6},{8,9},{9,8},{10,11... | collective-permute-start | bytes 983048 | tf_op jit(solution)/shard_map/ppermute | solution.py:367
  35.2 22.9 %collective-permute-start = (bf16[128,2560]{1,0:T(8,128)(2,1)}, bf16[128,2560]{1,0:T(8,128)(2,1)S(1)}, u32[]{:S(2)}, u32[]{:S(2)}) collective-permute-start(bf16[128,2560]{1,0:T(8,128)(2,1)} %bitcast.20), channel_id=1, source_target_pairs={{0,0},{1,8},{4,4},{5,12},{8,1},{9,9},{12,5},{13,13},{2,2},{3,10},{... | collective-permute-start | bytes 1966088 | tf_op jit(solution)/shard_map/ppermute | solution.py:368
  43.2 5.7 %collective-permute-start.7 = (bf16[128,640]{1,0:T(8,128)(2,1)S(1)}, bf16[128,640]{1,0:T(8,128)(2,1)S(1)}, u32[]{:S(2)}, u32[]{:S(2)}) collective-permute-start(bf16[128,640]{1,0:T(8,128)(2,1)S(1)} %get-tuple-element.42), channel_id=1, source_target_pairs={{0,4},{4,0},{8,12},{12,8},{1,5},{5,1},{9,13},{13,9},{2,6},{6,2},{1... | collective-permute-start | bytes 491528 | tf_op jit(solution)/shard_map/ppermute | solution.py:392
  49.6 8.5 %collective-permute-start.13 = (bf16[128,640]{1,0:T(8,128)(2,1)S(1)}, bf16[128,640]{1,0:T(8,128)(2,1)S(1)}, u32[]{:S(2)}, u32[]{:S(2)}) collective-permute-start(bf16[128,640]{1,0:T(8,128)(2,1)S(1)} %shard_map.126), channel_id=1, source_target_pairs={{0,2},{2,0},{1,3},{3,1},{4,6},{6,4},{5,7},{7,5},{8,10},{10,8},{9,1... | collective-permute-start | bytes 491528 | tf_op jit(solution)/shard_map/ppermute | solution.py:406
  52.2 6.8 %collective-permute-start.12 = (bf16[128,640]{1,0:T(8,128)(2,1)S(1)}, bf16[128,640]{1,0:T(8,128)(2,1)S(1)}, u32[]{:S(2)}, u32[]{:S(2)}) collective-permute-start(bf16[128,640]{1,0:T(8,128)(2,1)S(1)} %shard_map.125), channel_id=1, source_target_pairs={{0,2},{2,0},{1,3},{3,1},{4,6},{6,4},{5,7},{7,5},{8,10},{10,8},{9,1... | collective-permute-start | bytes 491528 | tf_op jit(solution)/shard_map/ppermute | solution.py:406
  53.0 2.8 %copy-start.2 = (f32[1,2560]{1,0:T(1,128)S(1)}, f32[1,2560]{1,0:T(1,128)}, u32[]{:S(2)}) copy-start(f32[1,2560]{1,0:T(1,128)} %refs_3_.7) | copy-start | bytes 30724
  53.0 9.4 %collective-permute-start.11 = (bf16[128,640]{1,0:T(8,128)(2,1)S(1)}, bf16[128,640]{1,0:T(8,128)(2,1)S(1)}, u32[]{:S(2)}, u32[]{:S(2)}) collective-permute-start(bf16[128,640]{1,0:T(8,128)(2,1)S(1)} %shard_map.124), channel_id=1, source_target_pairs={{0,2},{2,0},{1,3},{3,1},{4,6},{6,4},{5,7},{7,5},{8,10},{10,8},{9,1... | collective-permute-start | bytes 491528 | tf_op jit(solution)/shard_map/ppermute | solution.py:406
  55.6 2.5 %copy-start.1 = (bf16[2560,64]{0,1:T(8,128)(2,1)S(1)}, bf16[2560,64]{0,1:T(8,128)(2,1)}, u32[]{:S(2)}) copy-start(bf16[2560,64]{0,1:T(8,128)(2,1)} %param.20) | copy-start | bytes 983044
  55.6 2.5 %copy-start.4 = (f32[1,2560]{1,0:T(1,128)S(1)}, f32[1,2560]{1,0:T(1,128)}, u32[]{:S(2)}) copy-start(f32[1,2560]{1,0:T(1,128)} %refs_4_.9) | copy-start | bytes 30724
  55.6 10.3 %collective-permute-start.10 = (bf16[128,640]{1,0:T(8,128)(2,1)S(1)}, bf16[128,640]{1,0:T(8,128)(2,1)S(1)}, u32[]{:S(2)}, u32[]{:S(2)}) collective-permute-start(bf16[128,640]{1,0:T(8,128)(2,1)S(1)} %shard_map.123), channel_id=1, source_target_pairs={{0,2},{2,0},{1,3},{3,1},{4,6},{6,4},{5,7},{7,5},{8,10},{10,8},{9,1... | collective-permute-start | bytes 491528 | tf_op jit(solution)/shard_map/ppermute | solution.py:406
  58.1 26.9 %copy-start.5 = (f32[1,1,128,32]{2,3,1,0:T(8,128)S(1)}, f32[1,1,128,32]{2,3,1,0:T(8,128)}, u32[]{:S(2)}) copy-start(f32[1,1,128,32]{2,3,1,0:T(8,128)} %param.21) | copy-start | bytes 49156
  66.3 4.6 %collective-permute-start.14 = (f32[72,128]{1,0:T(8,128)S(1)}, f32[72,128]{1,0:T(8,128)S(1)}, u32[]{:S(2)}, u32[]{:S(2)}) collective-permute-start(f32[72,128]{1,0:T(8,128)S(1)} %shard_map.130.own_ref), channel_id=1, source_target_pairs={{0,2},{2,0},{1,3},{3,1},{4,6},{6,4},{5,7},{7,5},{8,10},{10,8},{9,1... | collective-permute-start | bytes 110600 | tf_op jit(solution)/shard_map/ppermute | solution.py:427
  67.0 3.9 %collective-permute-start.15 = (f32[64,128]{1,0:T(8,128)S(1)}, f32[64,128]{1,0:T(8,128)S(1)}, u32[]{:S(2)}, u32[]{:S(2)}) collective-permute-start(f32[64,128]{1,0:T(8,128)S(1)} %get-tuple-element.52.rows_own_ref), channel_id=1, source_target_pairs={{0,2},{2,0},{1,3},{3,1},{4,6},{6,4},{5,7},{7,5},{8,10},{10,8},{9,1... | collective-permute-start | bytes 98312 | tf_op jit(solution)/shard_map/ppermute | solution.py:378
  71.0 1.9 %collective-permute-start.16 = (f32[32,128]{1,0:T(8,128)S(1)}, f32[32,128]{1,0:T(8,128)S(1)}, u32[]{:S(2)}, u32[]{:S(2)}) collective-permute-start(f32[32,128]{1,0:T(8,128)S(1)} %get-tuple-element.54), channel_id=1, source_target_pairs={{0,1},{1,0},{2,3},{3,2},{4,5},{5,4},{6,7},{7,6},{8,9},{9,8},{10,11... | collective-permute-start | bytes 49160 | tf_op jit(solution)/shard_map/ppermute | solution.py:434
  73.0 6.6 %collective-permute-start.17 = (f32[16,128]{1,0:T(8,128)S(1)}, f32[16,128]{1,0:T(8,128)S(1)}, u32[]{:S(2)}, u32[]{:S(2)}) collective-permute-start(f32[16,128]{1,0:T(8,128)S(1)} %get-tuple-element.56), channel_id=1, source_target_pairs={{0,4},{4,0},{8,12},{12,8},{1,5},{5,1},{9,13},{13,9},{2,6},{6,2},{1... | collective-permute-start | bytes 24584 | tf_op jit(solution)/shard_map/ppermute | solution.py:442
  74.0 7.2 %collective-permute-start.18 = (f32[16,128]{1,0:T(8,128)S(1)}, f32[16,128]{1,0:T(8,128)S(1)}, u32[]{:S(2)}, u32[]{:S(2)}) collective-permute-start(f32[16,128]{1,0:T(8,128)S(1)} %get-tuple-element.57), channel_id=1, source_target_pairs={{0,8},{4,12},{8,0},{12,4},{1,9},{5,13},{9,1},{13,5},{2,10},{6,14},... | collective-permute-start | bytes 24584 | tf_op jit(solution)/shard_map/ppermute | solution.py:442
  79.5 5.4 %collective-permute-start.19 = (f32[16,128]{1,0:T(8,128)S(1)}, f32[16,128]{1,0:T(8,128)S(1)}, u32[]{:S(2)}, u32[]{:S(2)}) collective-permute-start(f32[16,128]{1,0:T(8,128)S(1)} %get-tuple-element.58), channel_id=1, source_target_pairs={{0,12},{4,8},{8,4},{12,0},{1,13},{5,9},{9,5},{13,1},{2,14},{6,10},... | collective-permute-start | bytes 24584 | tf_op jit(solution)/shard_map/ppermute | solution.py:442
  (4 other events, 3.0 us)
where the time goes:
time: 86.1 us; the launch traced here: 85.7 us
  starting transfers between devices  48.7 us (57%)
  waiting for transfers between devices  21.3 us (25%)
  Pallas kernels  11.8 us (14%)
  local copies, waits for them, and re-layouts  3.05 us (4%)
  between operations  0.91 us (1%)
    ppermute x2, starting transfers between devices, fast_plan(): kv_other = [lax.ppermute(block, 'guide', both) for block in kv_own]  22.9 us
    pallas_call x16, Pallas kernels, call(): pl.pallas_call(kernel, out_shape=shapes, in_specs=specs or [VMEM_SPEC] *...  11.8 us
    ppermute x4, waiting for transfers between devices, fast_plan(): got.append(lax.ppermute(partial, 'shard', both))  6.75 us
    ppermute x3, starting transfers between devices, fast_plan(): lax.ppermute(frames[k], 'seq', [(z, z ^ k) for z in range(seq_count)])  6.58 us
    ppermute x1, waiting for transfers between devices, fast_plan(): lax.ppermute(mixed[j], 'seq', inside[j])  5.67 us
    ppermute x3, waiting for transfers between devices, fast_plan(): lax.ppermute(frames[k], 'seq', [(z, z ^ k) for z in range(seq_count)])  5.44 us
    ppermute x4, starting transfers between devices, fast_plan(): got.append(lax.ppermute(partial, 'shard', both))  4.32 us
    ppermute x1, starting transfers between devices, fast_plan(): near_w = lax.ppermute(w_out, ('shard', 'guide'), crossed)  3.51 us
  transfers between devices with their start and end apart: 20, of which 8 were waited for; matrix products, arithmetic and copies ran while one was open for 0% of the time, Pallas kernels for 12%

commit v1 on v0

--- a/solution.py
+++ b/solution.py
@@ -191,13 +191,26 @@
     )
 
 
-def early_kernel(seq_count, scale_ref, shift_ref, head_ref, owner_ref, steps_ref, out_ref, chosen_ref, weight_ref):
+def early_kernel(
+    seq_count, scale_hbm, shift_hbm, head_hbm, owner_ref, steps_ref, out_ref, chosen_ref, weight_ref,
+    scale_ref, shift_ref, head_ref, sems,
+):
+    copies = [
+        pltpu.make_async_copy(source, target, sems.at[i])
+        for i, (source, target) in enumerate(
+            ((scale_hbm, scale_ref), (shift_hbm, shift_ref), (head_hbm, head_ref))
+        )
+    ]
+    for copy in copies:
+        copy.start()
     z = lax.axis_index("seq")
     for k in range(seq_count):
         for f in range(seq_count):
             here = jnp.where(owner_ref[0, f] == z ^ k, 1.0, 0.0)
             chosen_ref[k * seq_count + f : k * seq_count + f + 1, :] = jnp.full((1, LANES), here, F32)
     weight_ref[...] = plan_weight(jnp.full((SUBLANES, LANES), steps_ref[0], jnp.int32))
+    for copy in copies:
+        copy.wait()
     width = scale_ref.shape[1]
     which = lax.broadcasted_iota(jnp.int32, (LANES, width), 0)
     rows = jnp.where(which == 0, 1.0 + scale_ref[...], shift_ref[...])
@@ -321,6 +334,10 @@
     )(*args)
 
 
+def in_hbm(array):
+    return pltpu.with_memory_space_constraint(array, pltpu.HBM)
+
+
 def fast_plan(
     queries, key_vecs, value_vecs, residual, w_out, attn_gate, norm_shift, norm_scale, w_head, noise,
     timesteps, frame_owner,
@@ -343,7 +360,7 @@
         return call(
             functools.partial(pack_kernel, parts, half, len(arrays)),
             [((len(arrays), rows, half), BF16)] * parts,
-            [pltpu.with_memory_space_constraint(array[0, 0], pltpu.HBM) for array in arrays],
+            [in_hbm(array[0, 0]) for array in arrays],
             [HBM_SPEC] * len(arrays),
             [pltpu.SemaphoreType.DMA((parts * len(arrays),))],
             moved=4 * len(arrays) * rows * width_local,
@@ -371,8 +388,14 @@
     rows_own, chosen, weight = call(
         functools.partial(early_kernel, seq_count),
         [((channels, LANES), F32), ((seq_count * seq_count, LANES), F32), ((SUBLANES, LANES), F32)],
-        [norm_scale, norm_shift, head_t, frame_owner, timesteps],
-        [VMEM_SPEC] * 3 + [SMEM_SPEC] * 2,
+        [in_hbm(norm_scale), in_hbm(norm_shift), in_hbm(head_t), frame_owner, timesteps],
+        [HBM_SPEC] * 3 + [SMEM_SPEC] * 2,
+        [
+            pltpu.VMEM(norm_scale.shape, F32),
+            pltpu.VMEM(norm_shift.shape, F32),
+            pltpu.VMEM(head_t.shape, BF16),
+            pltpu.SemaphoreType.DMA((3,)),
+        ],
         moved=4 * width_shard * LANES,
     )
     rows_got = lax.ppermute(rows_own, "shard", both)

time: 86.1 us -> 80.7 us (0.937)
  waiting for transfers between devices: 21.3 us -> 18.1 us
  local copies, waits for them, and re-layouts: 3.05 us -> 0.68 us
  Pallas kernels: 11.8 us -> 12.8 us
    unnamed x16 -> x10, local copies, waits for them, and re-layouts: 3.05 us -> 0.68 us
    ppermute x3, starting transfers between devices: 6.58 us -> 4.75 us  [fast_plan(): lax.ppermute(frames[k], 'seq', [(z, z ^ k) for z in range(seq_count)])]
    ppermute x3, waiting for transfers between devices: 5.44 us -> 3.91 us  [fast_plan(): lax.ppermute(frames[k], 'seq', [(z, z ^ k) for z in range(seq_count)])]
    ppermute x4, waiting for transfers between devices: 6.75 us -> 5.48 us  [fast_plan(): got.append(lax.ppermute(partial, 'shard', both))]
    pallas_call x16, Pallas kernels: 11.8 us -> 12.8 us  [call(): pl.pallas_call(kernel, out_shape=shapes, in_specs=specs or [VMEM_SPEC] *...]
    ppermute x1, starting transfers between devices: 1.02 us -> 1.98 us  [fast_plan(): eps_got = lax.ppermute(send, 'guide', both)]
  transfers between devices with their start and end apart: 20 -> 20, of which waited for: 8 -> 7; matrix products, arithmetic and copies ran while one was open for 0% -> 0% of each run, Pallas kernels for 12% -> 14%
where the time goes in v1:
time: 80.7 us; the launch traced here: 80.3 us
  starting transfers between devices  47.9 us (59%)
  waiting for transfers between devices  18.1 us (22%)
  Pallas kernels  12.8 us (16%)
  between operations  0.91 us (1%)
    ppermute x2, starting transfers between devices, fast_plan(): kv_other = [lax.ppermute(block, 'guide', both) for block in kv_own]  22.9 us
    pallas_call x16, Pallas kernels, call(): pl.pallas_call(kernel, out_shape=shapes, in_specs=specs or [VMEM_SPEC] *...  12.8 us
    ppermute x4, waiting for transfers between devices, fast_plan(): got.append(lax.ppermute(partial, 'shard', both))  5.48 us
    ppermute x1, waiting for transfers between devices, fast_plan(): lax.ppermute(mixed[j], 'seq', inside[j])  5.31 us
    ppermute x3, starting transfers between devices, fast_plan(): lax.ppermute(frames[k], 'seq', [(z, z ^ k) for z in range(seq_count)])  4.75 us
    ppermute x4, starting transfers between devices, fast_plan(): got.append(lax.ppermute(partial, 'shard', both))  4.31 us
    ppermute x3, waiting for transfers between devices, fast_plan(): lax.ppermute(frames[k], 'seq', [(z, z ^ k) for z in range(seq_count)])  3.91 us
    ppermute x1, starting transfers between devices, fast_plan(): near_w = lax.ppermute(w_out, ('shard', 'guide'), crossed)  3.51 us
  transfers between devices with their start and end apart: 20, of which 7 were waited for; matrix products, arithmetic and copies ran while one was open for 0% of the time, Pallas kernels for 14%

profile of v1, /device:TPU:0, one launch (start us, length us, event | category | flops | bytes accessed | tf_op | source)
XLA Modules:
  0.0 80.3 jit_solution(8233373130670688993)
XLA Ops:
  0.0 3.5 %collective-permute-start.8 = (bf16[1280,2560]{1,0:T(8,128)(2,1)}, bf16[1280,2560]{1,0:T(8,128)(2,1)S(1)}, u32[]{:S(2)}, u32[]{:S(2)}) collective-permute-start(bf16[1280,2560]{1,0:T(8,128)(2,1)} %param.16), channel_id=1, source_target_pairs={{0,0},{1,1},{2,3},{3,2},{4,4},{5,5},{6,7},{7,6},{8,8},{9,9},{10,11... | collective-permute-start | bytes 19660808 | tf_op jit(solution)/shard_map/ppermute | solution.py:382
  3.5 2.4 %collective-permute-start.9 = (bf16[1280,2560]{1,0:T(8,128)(2,1)}, bf16[1280,2560]{1,0:T(8,128)(2,1)S(1)}, u32[]{:S(2)}, u32[]{:S(2)}) collective-permute-start(bf16[1280,2560]{1,0:T(8,128)(2,1)} %param.16), channel_id=1, source_target_pairs={{0,1},{1,0},{2,2},{3,3},{4,5},{5,4},{6,6},{7,7},{8,9},{9,8},{10,10... | collective-permute-start | bytes 19660808 | tf_op jit(solution)/shard_map/ppermute | solution.py:383
  5.9 1.2 %shard_map.120 = (bf16[2,128,640]{2,1,0:T(8,128)(2,1)S(1)}, bf16[2,128,640]{2,1,0:T(8,128)(2,1)S(1)}) custom-call(bf16[128,1280]{1,0:T(8,128)(2,1)} %bitcast.17, bf16[128,1280]{1,0:T(8,128)(2,1)} %bitcast.18), custom_call_target="tpu_custom_call" | custom-call | bytes 1310720 | tf_op jit(solution)/shard_map/pallas_call | solution.py:326
  7.8 2.6 %collective-permute-start.4 = (bf16[2,128,640]{2,1,0:T(8,128)(2,1)S(1)}, bf16[2,128,640]{2,1,0:T(8,128)(2,1)S(1)}, u32[]{:S(2)}, u32[]{:S(2)}) collective-permute-start(bf16[2,128,640]{2,1,0:T(8,128)(2,1)S(1)} %get-tuple-element.40), channel_id=1, source_target_pairs={{0,4},{1,12},{4,0},{5,8},{8,5},{9,13},{12,1},{13,9},{2,6},{3,14},{... | collective-permute-start | bytes 983048 | tf_op jit(solution)/shard_map/ppermute | solution.py:379
  10.4 1.0 %shard_map.119 = (bf16[1,128,640]{2,1,0:T(8,128)(2,1)S(1)}, bf16[1,128,640]{2,1,0:T(8,128)(2,1)S(1)}) custom-call(bf16[128,1280]{1,0:T(8,128)(2,1)} %bitcast.19), custom_call_target="tpu_custom_call" | custom-call | bytes 655360 | tf_op jit(solution)/shard_map/pallas_call | solution.py:326
  12.2 22.9 %collective-permute-start.5 = (bf16[2,128,640]{2,1,0:T(8,128)(2,1)S(1)}, bf16[2,128,640]{2,1,0:T(8,128)(2,1)S(1)}, u32[]{:S(2)}, u32[]{:S(2)}) collective-permute-start(bf16[2,128,640]{2,1,0:T(8,128)(2,1)S(1)} %collective-permute-done.3.refs_2_), channel_id=1, source_target_pairs={{0,1},{1,0},{2,3},{3,2},{4,5},{5,4},{6,7},{7,6},{8,9},{9,8},{10,11... | collective-permute-start | bytes 983048 | tf_op jit(solution)/shard_map/ppermute | solution.py:384
  35.2 1.7 %collective-permute-start = (bf16[128,2560]{1,0:T(8,128)(2,1)}, bf16[128,2560]{1,0:T(8,128)(2,1)S(1)}, u32[]{:S(2)}, u32[]{:S(2)}) collective-permute-start(bf16[128,2560]{1,0:T(8,128)(2,1)} %bitcast.20), channel_id=1, source_target_pairs={{0,0},{1,8},{4,4},{5,12},{8,1},{9,9},{12,5},{13,13},{2,2},{3,10},{... | collective-permute-start | bytes 1966088 | tf_op jit(solution)/shard_map/ppermute | solution.py:385
  38.2 2.4 %shard_map.118 = (f32[64,128]{1,0:T(8,128)S(1)}, f32[16,128]{1,0:T(8,128)S(1)}, f32[8,128]{1,0:T(8,128)S(1)}) custom-call(f32[1,2560]{1,0:T(1,128)} %refs_4_.9, f32[1,2560]{1,0:T(1,128)} %shift_hbm.1, bf16[64,2560]{1,0:T(8,128)(2,1)} %bitcast.11, s32[1,4]{1,0:T(1,128)S(1)} %copy-done.4, s32[1]{0:T(128)S(6)} %copy.13.steps_ref), custom_call_target="tpu_custom_call" | custom-call | bytes 1310720 | tf_op jit(solution)/shard_map/pallas_call | solution.py:326
  40.6 1.2 %shard_map.121 = (bf16[128,640]{1,0:T(8,128)(2,1)S(1)}, bf16[128,640]{1,0:T(8,128)(2,1)S(1)}) custom-call(bf16[1,128,640]{2,1,0:T(8,128)(2,1)S(1)} %collective-permute-done.1.refs_0_, bf16[1,128,640]{2,1,0:T(8,128)(2,1)S(1)} %collective-permute-done.2.refs_1_, bf16[2,128,640]{2,1,0:T(8,128)(2,1)S(1)} %collective-permute-done.3.refs_2_, ...), custom_call_target="tpu_custom_call" | custom-call | flops 335544320 | bytes 1966080 | tf_op jit(solution)/shard_map/pallas_call | solution.py:326
  41.9 5.3 %collective-permute-done.7.refs_1_ = bf16[128,640]{1,0:T(8,128)(2,1)S(1)} collective-permute-done((bf16[128,640]{1,0:T(8,128)(2,1)S(1)}, bf16[128,640]{1,0:T(8,128)(2,1)S(1)}, u32[]{:S(2)}, u32[]{:S(2)}) %collective-permute-start.7) | collective-permute-done | bytes 163872 | tf_op jit(solution)/shard_map/ppermute | solution.py:415
  47.9 1.7 %collective-permute-start.13 = (bf16[128,640]{1,0:T(8,128)(2,1)S(1)}, bf16[128,640]{1,0:T(8,128)(2,1)S(1)}, u32[]{:S(2)}, u32[]{:S(2)}) collective-permute-start(bf16[128,640]{1,0:T(8,128)(2,1)S(1)} %shard_map.126), channel_id=1, source_target_pairs={{0,2},{2,0},{1,3},{3,1},{4,6},{6,4},{5,7},{7,5},{8,10},{10,8},{9,1... | collective-permute-start | bytes 491528 | tf_op jit(solution)/shard_map/ppermute | solution.py:429
  51.3 1.7 %collective-permute-start.11 = (bf16[128,640]{1,0:T(8,128)(2,1)S(1)}, bf16[128,640]{1,0:T(8,128)(2,1)S(1)}, u32[]{:S(2)}, u32[]{:S(2)}) collective-permute-start(bf16[128,640]{1,0:T(8,128)(2,1)S(1)} %shard_map.124), channel_id=1, source_target_pairs={{0,2},{2,0},{1,3},{3,1},{4,6},{6,4},{5,7},{7,5},{8,10},{10,8},{9,1... | collective-permute-start | bytes 491528 | tf_op jit(solution)/shard_map/ppermute | solution.py:429
  54.1 2.3 %shard_map.122.refs_1_ = f32[128,2560]{1,0:T(8,128)S(1)} custom-call(bf16[128,640]{1,0:T(8,128)(2,1)S(1)} %get-tuple-element.41.refs_0_, bf16[128,640]{1,0:T(8,128)(2,1)S(1)} %collective-permute-done.7.refs_1_, bf16[1280,2560]{1,0:T(8,128)(2,1)S(1)} %collective-permute-done.8.refs_2_, bf16[1280,2560]{1,0:T(8,128)(2,1)S(1)} %collective-permute-done.9.refs_3_, ...), custom_call_target="tpu_custom_call" | custom-call | flops 838860800 | bytes 6553600 | tf_op jit(solution)/shard_map/pallas_call | solution.py:326
  57.2 2.3 %collective-permute-done.11.refs_2_ = bf16[128,640]{1,0:T(8,128)(2,1)S(1)} collective-permute-done((bf16[128,640]{1,0:T(8,128)(2,1)S(1)}, bf16[128,640]{1,0:T(8,128)(2,1)S(1)}, u32[]{:S(2)}, u32[]{:S(2)}) %collective-permute-start.11) | collective-permute-done | bytes 163872 | tf_op jit(solution)/shard_map/ppermute | solution.py:429
  59.8 3.2 %collective-permute-done.10.refs_2_ = bf16[128,640]{1,0:T(8,128)(2,1)S(1)} collective-permute-done((bf16[128,640]{1,0:T(8,128)(2,1)S(1)}, bf16[128,640]{1,0:T(8,128)(2,1)S(1)}, u32[]{:S(2)}, u32[]{:S(2)}) %collective-permute-start.10) | collective-permute-done | bytes 163872 | tf_op jit(solution)/shard_map/ppermute | solution.py:429
  64.0 1.4 %collective-permute-start.15 = (f32[64,128]{1,0:T(8,128)S(1)}, f32[64,128]{1,0:T(8,128)S(1)}, u32[]{:S(2)}, u32[]{:S(2)}) collective-permute-start(f32[64,128]{1,0:T(8,128)S(1)} %get-tuple-element.52.rows_own_ref), channel_id=1, source_target_pairs={{0,2},{2,0},{1,3},{3,1},{4,6},{6,4},{5,7},{7,5},{8,10},{10,8},{9,1... | collective-permute-start | bytes 98312 | tf_op jit(solution)/shard_map/ppermute | solution.py:401
  65.4 2.5 %collective-permute-done.15.rows_got_ref = f32[64,128]{1,0:T(8,128)S(1)} collective-permute-done((f32[64,128]{1,0:T(8,128)S(1)}, f32[64,128]{1,0:T(8,128)S(1)}, u32[]{:S(2)}, u32[]{:S(2)}) %collective-permute-start.15) | collective-permute-done | bytes 32800 | tf_op jit(solution)/shard_map/ppermute | solution.py:401
  68.0 2.0 %collective-permute-start.16 = (f32[32,128]{1,0:T(8,128)S(1)}, f32[32,128]{1,0:T(8,128)S(1)}, u32[]{:S(2)}, u32[]{:S(2)}) collective-permute-start(f32[32,128]{1,0:T(8,128)S(1)} %get-tuple-element.54), channel_id=1, source_target_pairs={{0,1},{1,0},{2,3},{3,2},{4,5},{5,4},{6,7},{7,6},{8,9},{9,8},{10,11... | collective-permute-start | bytes 49160 | tf_op jit(solution)/shard_map/ppermute | solution.py:457
  70.0 0.8 %collective-permute-done.16.got_ref = f32[32,128]{1,0:T(8,128)S(1)} collective-permute-done((f32[32,128]{1,0:T(8,128)S(1)}, f32[32,128]{1,0:T(8,128)S(1)}, u32[]{:S(2)}, u32[]{:S(2)}) %collective-permute-start.16) | collective-permute-done | bytes 16416 | tf_op jit(solution)/shard_map/ppermute | solution.py:457
  70.9 2.3 %collective-permute-start.17 = (f32[16,128]{1,0:T(8,128)S(1)}, f32[16,128]{1,0:T(8,128)S(1)}, u32[]{:S(2)}, u32[]{:S(2)}) collective-permute-start(f32[16,128]{1,0:T(8,128)S(1)} %get-tuple-element.56), channel_id=1, source_target_pairs={{0,4},{4,0},{8,12},{12,8},{1,5},{5,1},{9,13},{13,9},{2,6},{6,2},{1... | collective-permute-start | bytes 24584 | tf_op jit(solution)/shard_map/ppermute | solution.py:465
  73.3 0.9 %collective-permute-start.18 = (f32[16,128]{1,0:T(8,128)S(1)}, f32[16,128]{1,0:T(8,128)S(1)}, u32[]{:S(2)}, u32[]{:S(2)}) collective-permute-start(f32[16,128]{1,0:T(8,128)S(1)} %get-tuple-element.57), channel_id=1, source_target_pairs={{0,8},{4,12},{8,0},{12,4},{1,9},{5,13},{9,1},{13,5},{2,10},{6,14},... | collective-permute-start | bytes 24584 | tf_op jit(solution)/shard_map/ppermute | solution.py:465
  74.2 1.5 %collective-permute-start.19 = (f32[16,128]{1,0:T(8,128)S(1)}, f32[16,128]{1,0:T(8,128)S(1)}, u32[]{:S(2)}, u32[]{:S(2)}) collective-permute-start(f32[16,128]{1,0:T(8,128)S(1)} %get-tuple-element.58), channel_id=1, source_target_pairs={{0,12},{4,8},{8,4},{12,0},{1,13},{5,9},{9,5},{13,1},{2,14},{6,10},... | collective-permute-start | bytes 24584 | tf_op jit(solution)/shard_map/ppermute | solution.py:465
  75.7 2.2 %collective-permute-done.18.refs_2_ = f32[16,128]{1,0:T(8,128)S(1)} collective-permute-done((f32[16,128]{1,0:T(8,128)S(1)}, f32[16,128]{1,0:T(8,128)S(1)}, u32[]{:S(2)}, u32[]{:S(2)}) %collective-permute-start.18) | collective-permute-done | bytes 8224 | tf_op jit(solution)/shard_map/ppermute | solution.py:465
  77.9 1.7 %collective-permute-done.19.refs_3_ = f32[16,128]{1,0:T(8,128)S(1)} collective-permute-done((f32[16,128]{1,0:T(8,128)S(1)}, f32[16,128]{1,0:T(8,128)S(1)}, u32[]{:S(2)}, u32[]{:S(2)}) %collective-permute-start.19) | collective-permute-done | bytes 8224 | tf_op jit(solution)/shard_map/ppermute | solution.py:465
  (42 shorter events, 8.8 us)
Async XLA Ops:
  0.0 47.2 %collective-permute-start.8 = (bf16[1280,2560]{1,0:T(8,128)(2,1)}, bf16[1280,2560]{1,0:T(8,128)(2,1)S(1)}, u32[]{:S(2)}, u32[]{:S(2)}) collective-permute-start(bf16[1280,2560]{1,0:T(8,128)(2,1)} %param.16), channel_id=1, source_target_pairs={{0,0},{1,1},{2,3},{3,2},{4,4},{5,5},{6,7},{7,6},{8,8},{9,9},{10,11... | collective-permute-start | bytes 19660808 | tf_op jit(solution)/shard_map/ppermute | solution.py:382
  3.5 43.7 %collective-permute-start.9 = (bf16[1280,2560]{1,0:T(8,128)(2,1)}, bf16[1280,2560]{1,0:T(8,128)(2,1)S(1)}, u32[]{:S(2)}, u32[]{:S(2)}) collective-permute-start(bf16[1280,2560]{1,0:T(8,128)(2,1)} %param.16), channel_id=1, source_target_pairs={{0,1},{1,0},{2,2},{3,3},{4,5},{5,4},{6,6},{7,7},{8,9},{9,8},{10,10... | collective-permute-start | bytes 19660808 | tf_op jit(solution)/shard_map/ppermute | solution.py:383
  7.1 5.1 %collective-permute-start.3 = (bf16[2,128,640]{2,1,0:T(8,128)(2,1)S(1)}, bf16[2,128,640]{2,1,0:T(8,128)(2,1)S(1)}, u32[]{:S(2)}, u32[]{:S(2)}) collective-permute-start(bf16[2,128,640]{2,1,0:T(8,128)(2,1)S(1)} %get-tuple-element.39), channel_id=1, source_target_pairs={{0,0},{1,8},{4,4},{5,12},{8,1},{9,9},{12,5},{13,13},{2,2},{3,10},{... | collective-permute-start | bytes 983048 | tf_op jit(solution)/shard_map/ppermute | solution.py:379
  7.8 27.3 %collective-permute-start.4 = (bf16[2,128,640]{2,1,0:T(8,128)(2,1)S(1)}, bf16[2,128,640]{2,1,0:T(8,128)(2,1)S(1)}, u32[]{:S(2)}, u32[]{:S(2)}) collective-permute-start(bf16[2,128,640]{2,1,0:T(8,128)(2,1)S(1)} %get-tuple-element.40), channel_id=1, source_target_pairs={{0,4},{1,12},{4,0},{5,8},{8,5},{9,13},{12,1},{13,9},{2,6},{3,14},{... | collective-permute-start | bytes 983048 | tf_op jit(solution)/shard_map/ppermute | solution.py:379
  11.5 0.7 collective-permute-start.1
  12.1 23.0 %collective-permute-start.2 = (bf16[1,128,640]{2,1,0:T(8,128)(2,1)S(1)}, bf16[1,128,640]{2,1,0:T(8,128)(2,1)S(1)}, u32[]{:S(2)}, u32[]{:S(2)}) collective-permute-start(bf16[1,128,640]{2,1,0:T(8,128)(2,1)S(1)} %get-tuple-element.35), channel_id=1, source_target_pairs={{0,4},{1,12},{4,0},{5,8},{8,5},{9,13},{12,1},{13,9},{2,6},{3,14},{... | collective-permute-start | bytes 491528 | tf_op jit(solution)/shard_map/ppermute | solution.py:381
  12.2 28.4 %collective-permute-start.5 = (bf16[2,128,640]{2,1,0:T(8,128)(2,1)S(1)}, bf16[2,128,640]{2,1,0:T(8,128)(2,1)S(1)}, u32[]{:S(2)}, u32[]{:S(2)}) collective-permute-start(bf16[2,128,640]{2,1,0:T(8,128)(2,1)S(1)} %collective-permute-done.3.refs_2_), channel_id=1, source_target_pairs={{0,1},{1,0},{2,3},{3,2},{4,5},{5,4},{6,7},{7,6},{8,9},{9,8},{10,11... | collective-permute-start | bytes 983048 | tf_op jit(solution)/shard_map/ppermute | solution.py:384
  35.1 5.5 %collective-permute-start.6 = (bf16[2,128,640]{2,1,0:T(8,128)(2,1)S(1)}, bf16[2,128,640]{2,1,0:T(8,128)(2,1)S(1)}, u32[]{:S(2)}, u32[]{:S(2)}) collective-permute-start(bf16[2,128,640]{2,1,0:T(8,128)(2,1)S(1)} %collective-permute-done.4.refs_3_), channel_id=1, source_target_pairs={{0,1},{1,0},{2,3},{3,2},{4,5},{5,4},{6,7},{7,6},{8,9},{9,8},{10,11... | collective-permute-start | bytes 983048 | tf_op jit(solution)/shard_map/ppermute | solution.py:384
  35.2 21.2 %collective-permute-start = (bf16[128,2560]{1,0:T(8,128)(2,1)}, bf16[128,2560]{1,0:T(8,128)(2,1)S(1)}, u32[]{:S(2)}, u32[]{:S(2)}) collective-permute-start(bf16[128,2560]{1,0:T(8,128)(2,1)} %bitcast.20), channel_id=1, source_target_pairs={{0,0},{1,8},{4,4},{5,12},{8,1},{9,9},{12,5},{13,13},{2,2},{3,10},{... | collective-permute-start | bytes 1966088 | tf_op jit(solution)/shard_map/ppermute | solution.py:385
  41.8 5.4 %collective-permute-start.7 = (bf16[128,640]{1,0:T(8,128)(2,1)S(1)}, bf16[128,640]{1,0:T(8,128)(2,1)S(1)}, u32[]{:S(2)}, u32[]{:S(2)}) collective-permute-start(bf16[128,640]{1,0:T(8,128)(2,1)S(1)} %get-tuple-element.42), channel_id=1, source_target_pairs={{0,4},{4,0},{8,12},{12,8},{1,5},{5,1},{9,13},{13,9},{2,6},{6,2},{1... | collective-permute-start | bytes 491528 | tf_op jit(solution)/shard_map/ppermute | solution.py:415
  47.9 8.6 %collective-permute-start.13 = (bf16[128,640]{1,0:T(8,128)(2,1)S(1)}, bf16[128,640]{1,0:T(8,128)(2,1)S(1)}, u32[]{:S(2)}, u32[]{:S(2)}) collective-permute-start(bf16[128,640]{1,0:T(8,128)(2,1)S(1)} %shard_map.126), channel_id=1, source_target_pairs={{0,2},{2,0},{1,3},{3,1},{4,6},{6,4},{5,7},{7,5},{8,10},{10,8},{9,1... | collective-permute-start | bytes 491528 | tf_op jit(solution)/shard_map/ppermute | solution.py:429
  50.1 6.6 %collective-permute-start.12 = (bf16[128,640]{1,0:T(8,128)(2,1)S(1)}, bf16[128,640]{1,0:T(8,128)(2,1)S(1)}, u32[]{:S(2)}, u32[]{:S(2)}) collective-permute-start(bf16[128,640]{1,0:T(8,128)(2,1)S(1)} %shard_map.125), channel_id=1, source_target_pairs={{0,2},{2,0},{1,3},{3,1},{4,6},{6,4},{5,7},{7,5},{8,10},{10,8},{9,1... | collective-permute-start | bytes 491528 | tf_op jit(solution)/shard_map/ppermute | solution.py:429
  51.3 2.8 %copy-start.1 = (f32[1,2560]{1,0:T(1,128)S(1)}, f32[1,2560]{1,0:T(1,128)}, u32[]{:S(2)}) copy-start(f32[1,2560]{1,0:T(1,128)} %refs_3_.7) | copy-start | bytes 30724
  51.3 8.2 %collective-permute-start.11 = (bf16[128,640]{1,0:T(8,128)(2,1)S(1)}, bf16[128,640]{1,0:T(8,128)(2,1)S(1)}, u32[]{:S(2)}, u32[]{:S(2)}) collective-permute-start(bf16[128,640]{1,0:T(8,128)(2,1)S(1)} %shard_map.124), channel_id=1, source_target_pairs={{0,2},{2,0},{1,3},{3,1},{4,6},{6,4},{5,7},{7,5},{8,10},{10,8},{9,1... | collective-permute-start | bytes 491528 | tf_op jit(solution)/shard_map/ppermute | solution.py:429
  53.6 2.8 %copy-start = (bf16[2560,64]{0,1:T(8,128)(2,1)S(1)}, bf16[2560,64]{0,1:T(8,128)(2,1)}, u32[]{:S(2)}) copy-start(bf16[2560,64]{0,1:T(8,128)(2,1)} %param.20) | copy-start | bytes 983044
  53.6 2.8 %copy-start.2 = (f32[1,2560]{1,0:T(1,128)S(1)}, f32[1,2560]{1,0:T(1,128)}, u32[]{:S(2)}) copy-start(f32[1,2560]{1,0:T(1,128)} %refs_4_.9) | copy-start | bytes 30724
  53.6 9.4 %collective-permute-start.10 = (bf16[128,640]{1,0:T(8,128)(2,1)S(1)}, bf16[128,640]{1,0:T(8,128)(2,1)S(1)}, u32[]{:S(2)}, u32[]{:S(2)}) collective-permute-start(bf16[128,640]{1,0:T(8,128)(2,1)S(1)} %shard_map.123), channel_id=1, source_target_pairs={{0,2},{2,0},{1,3},{3,1},{4,6},{6,4},{5,7},{7,5},{8,10},{10,8},{9,1... | collective-permute-start | bytes 491528 | tf_op jit(solution)/shard_map/ppermute | solution.py:429
  56.4 23.2 %copy-start.3 = (f32[1,1,128,32]{2,3,1,0:T(8,128)S(1)}, f32[1,1,128,32]{2,3,1,0:T(8,128)}, u32[]{:S(2)}) copy-start(f32[1,1,128,32]{2,3,1,0:T(8,128)} %param.21) | copy-start | bytes 49156
  63.3 4.6 %collective-permute-start.14 = (f32[72,128]{1,0:T(8,128)S(1)}, f32[72,128]{1,0:T(8,128)S(1)}, u32[]{:S(2)}, u32[]{:S(2)}) collective-permute-start(f32[72,128]{1,0:T(8,128)S(1)} %shard_map.130.own_ref), channel_id=1, source_target_pairs={{0,2},{2,0},{1,3},{3,1},{4,6},{6,4},{5,7},{7,5},{8,10},{10,8},{9,1... | collective-permute-start | bytes 110600 | tf_op jit(solution)/shard_map/ppermute | solution.py:450
  64.0 3.9 %collective-permute-start.15 = (f32[64,128]{1,0:T(8,128)S(1)}, f32[64,128]{1,0:T(8,128)S(1)}, u32[]{:S(2)}, u32[]{:S(2)}) collective-permute-start(f32[64,128]{1,0:T(8,128)S(1)} %get-tuple-element.52.rows_own_ref), channel_id=1, source_target_pairs={{0,2},{2,0},{1,3},{3,1},{4,6},{6,4},{5,7},{7,5},{8,10},{10,8},{9,1... | collective-permute-start | bytes 98312 | tf_op jit(solution)/shard_map/ppermute | solution.py:401
  68.0 2.8 %collective-permute-start.16 = (f32[32,128]{1,0:T(8,128)S(1)}, f32[32,128]{1,0:T(8,128)S(1)}, u32[]{:S(2)}, u32[]{:S(2)}) collective-permute-start(f32[32,128]{1,0:T(8,128)S(1)} %get-tuple-element.54), channel_id=1, source_target_pairs={{0,1},{1,0},{2,3},{3,2},{4,5},{5,4},{6,7},{7,6},{8,9},{9,8},{10,11... | collective-permute-start | bytes 49160 | tf_op jit(solution)/shard_map/ppermute | solution.py:457
  70.9 4.8 %collective-permute-start.17 = (f32[16,128]{1,0:T(8,128)S(1)}, f32[16,128]{1,0:T(8,128)S(1)}, u32[]{:S(2)}, u32[]{:S(2)}) collective-permute-start(f32[16,128]{1,0:T(8,128)S(1)} %get-tuple-element.56), channel_id=1, source_target_pairs={{0,4},{4,0},{8,12},{12,8},{1,5},{5,1},{9,13},{13,9},{2,6},{6,2},{1... | collective-permute-start | bytes 24584 | tf_op jit(solution)/shard_map/ppermute | solution.py:465
  73.3 4.6 %collective-permute-start.18 = (f32[16,128]{1,0:T(8,128)S(1)}, f32[16,128]{1,0:T(8,128)S(1)}, u32[]{:S(2)}, u32[]{:S(2)}) collective-permute-start(f32[16,128]{1,0:T(8,128)S(1)} %get-tuple-element.57), channel_id=1, source_target_pairs={{0,8},{4,12},{8,0},{12,4},{1,9},{5,13},{9,1},{13,5},{2,10},{6,14},... | collective-permute-start | bytes 24584 | tf_op jit(solution)/shard_map/ppermute | solution.py:465
  74.2 5.4 %collective-permute-start.19 = (f32[16,128]{1,0:T(8,128)S(1)}, f32[16,128]{1,0:T(8,128)S(1)}, u32[]{:S(2)}, u32[]{:S(2)}) collective-permute-start(f32[16,128]{1,0:T(8,128)S(1)} %get-tuple-element.58), channel_id=1, source_target_pairs={{0,12},{4,8},{8,4},{12,0},{1,13},{5,9},{9,5},{13,1},{2,14},{6,10},... | collective-permute-start | bytes 24584 | tf_op jit(solution)/shard_map/ppermute | solution.py:465
  (1 other events, 0.7 us)

commit v2 on v1

--- a/solution.py
+++ b/solution.py
@@ -114,6 +114,19 @@
             copies.append(
                 pltpu.make_async_copy(source_refs[i].at[:, cols], out_refs[j].at[i], sems.at[j * count + i])
             )
+    for copy in copies:
+        copy.start()
+    for copy in copies:
+        copy.wait()
+
+
+def split_kernel(source_ref, *refs):
+    out_refs, sems = refs[:-1], refs[-1]
+    width = out_refs[0].shape[1]
+    copies = [
+        pltpu.make_async_copy(source_ref.at[:, pl.ds(i * width, width)], out_ref, sems.at[i])
+        for i, out_ref in enumerate(out_refs)
+    ]
     for copy in copies:
         copy.start()
     for copy in copies:
@@ -240,7 +253,8 @@
     for t in range(got_ref.shape[1] // chunk):
         cols = slice(start + t * chunk, start + (t + 1) * chunk)
         arrived = got_ref[:, t * chunk : (t + 1) * chunk].astype(F32)
-        hidden = res_ref[:, cols].astype(F32) + hid_ref[:, cols] + gate_ref[:, cols] * arrived
+        here = slice(cols.start % res_ref.shape[1], cols.start % res_ref.shape[1] + chunk)
+        hidden = res_ref[:, here].astype(F32) + hid_ref[:, cols] + gate_ref[:, cols] * arrived
         for s in range(chunk // LANES):
             piece = hidden[:, s * LANES : (s + 1) * LANES]
             acc_one = acc_one + piece
@@ -382,7 +396,15 @@
     near_w = lax.ppermute(w_out, ("shard", "guide"), crossed)
     far_w = lax.ppermute(w_out, ("shard", "guide"), straight)
     kv_other = [lax.ppermute(block, "guide", both) for block in kv_own]
-    res_here = lax.ppermute(residual[0, 0], axes, there[0])
+    res_sent = call(
+        split_kernel,
+        [((rows, width_shard // 2), BF16)] * 2,
+        [in_hbm(residual[0, 0])],
+        [HBM_SPEC],
+        [pltpu.SemaphoreType.DMA((2,))],
+        moved=4 * rows * width_shard,
+    )
+    res_here = [lax.ppermute(block, axes, there[0]) for block in res_sent]
 
     head_t = w_head.T
     rows_own, chosen, weight = call(
@@ -415,16 +437,16 @@
     mixed = [mixed[0]] + [lax.ppermute(mixed[j], "seq", inside[j]) for j in range(1, parts)]
 
     chunk = 128
-    pieces = 4
-    width_piece = width_shard // pieces
+    quarter = width_shard // 4
+    pieces = [(0, 2 * quarter), (2 * quarter, quarter), (3 * quarter, quarter)]
     got = []
-    for i in range(pieces):
+    for start, width in pieces:
         partial = call(
-            functools.partial(send_kernel, parts, half, chunk, i * width_piece),
-            [((rows, width_piece), BF16)],
+            functools.partial(send_kernel, parts, half, chunk, start),
+            [((rows, width), BF16)],
             mixed + [near_w, far_w],
-            flops=2 * rows * width_local * width_piece,
-            moved=2 * width_local * width_piece,
+            flops=2 * rows * width_local * width,
+            moved=2 * width_local * width,
         )[0]
         got.append(lax.ppermute(partial, "shard", both))
     hidden = call(
@@ -435,16 +457,16 @@
         moved=2 * width_local * width_shard,
     )[0]
     state = []
-    for i in range(pieces):
-        first, last = i == 0, i == pieces - 1
+    for i, (start, width) in enumerate(pieces):
+        first, last = i == 0, i == len(pieces) - 1
         state = call(
-            functools.partial(head_kernel, first, last, chunk, i * width_piece),
+            functools.partial(head_kernel, first, last, chunk, start),
             [((channels + SUBLANES, rows), F32)]
             if last
             else [((channels, rows), F32), ((rows, LANES), F32), ((rows, LANES), F32)],
-            [res_here, hidden, got[i], attn_gate, norm_scale, head_t] + list(state),
-            flops=4 * rows * channels * width_piece,
-            moved=6 * rows * width_piece,
+            [res_here[0 if first else 1], hidden, got[i], attn_gate, norm_scale, head_t] + list(state),
+            flops=4 * rows * channels * width,
+            moved=6 * rows * width,
         )
     sums = state[0]
     sums_got = lax.ppermute(sums, "shard", both)

time: 80.7 us -> 78.5 us (0.973)
  waiting for transfers between devices: 18.1 us -> 15.8 us
    ppermute x2, starting transfers between devices: 22.9 us -> 14.2 us  [fast_plan(): kv_other = [lax.ppermute(block, 'guide', both) for block in kv_own]]
    ppermute x2, starting transfers between devices: 0.77 us -> 4.9 us  [fast_plan(): q_own = [lax.ppermute(q_sent[j], axes, there[j]) for j in range(parts)]]
    ppermute x1, waiting for transfers between devices: 5.31 us -> 1.92 us  [fast_plan(): lax.ppermute(mixed[j], 'seq', inside[j])]
    ppermute x1, starting transfers between devices: 1.98 us -> 5.34 us  [fast_plan(): eps_got = lax.ppermute(send, 'guide', both)]
    ppermute x4 -> x3, waiting for transfers between devices: 5.48 us -> 3.83 us  [fast_plan(): got.append(lax.ppermute(partial, 'shard', both))]
    ppermute x1, starting transfers between devices: 0.07 us -> 1.68 us  [fast_plan(): lax.ppermute(mixed[j], 'seq', inside[j])]
    ppermute x3, waiting for transfers between devices: 3.91 us -> 5.37 us  [fast_plan(): lax.ppermute(frames[k], 'seq', [(z, z ^ k) for z in range(seq_count)])]
    ppermute x1, starting transfers between devices: 0.69 us -> 2.08 us  [fast_plan(): sums_got = lax.ppermute(sums, 'shard', both)]
  transfers between devices with their start and end apart: 20 -> 20, of which waited for: 7 -> 7; matrix products, arithmetic and copies ran while one was open for 0% -> 0% of each run, Pallas kernels for 14% -> 16%
where the time goes in v2:
time: 78.5 us; the launch traced here: 78.2 us
  starting transfers between devices  47.2 us (60%)
  waiting for transfers between devices  15.8 us (20%)
  Pallas kernels  13.5 us (17%)
  between operations  0.93 us (1%)
    ppermute x2, starting transfers between devices, fast_plan(): kv_other = [lax.ppermute(block, 'guide', both) for block in kv_own]  14.2 us
    pallas_call x15, Pallas kernels, call(): pl.pallas_call(kernel, out_shape=shapes, in_specs=specs or [VMEM_SPEC] *...  13.5 us
    ppermute x3, waiting for transfers between devices, fast_plan(): lax.ppermute(frames[k], 'seq', [(z, z ^ k) for z in range(seq_count)])  5.37 us
    ppermute x1, starting transfers between devices, fast_plan(): eps_got = lax.ppermute(send, 'guide', both)  5.34 us
    ppermute x2, starting transfers between devices, fast_plan(): q_own = [lax.ppermute(q_sent[j], axes, there[j]) for j in range(parts)]  4.9 us
    ppermute x3, starting transfers between devices, fast_plan(): lax.ppermute(frames[k], 'seq', [(z, z ^ k) for z in range(seq_count)])  4.44 us
    ppermute x3, starting transfers between devices, fast_plan(): got.append(lax.ppermute(partial, 'shard', both))  3.97 us
    ppermute x1, waiting for transfers between devices, fast_plan(): rows_got = lax.ppermute(rows_own, 'shard', both)  3.84 us
  transfers between devices with their start and end apart: 20, of which 7 were waited for; matrix products, arithmetic and copies ran while one was open for 0% of the time, Pallas kernels for 16%

profile of v2, /device:TPU:0, one launch (start us, length us, event | category | flops | bytes accessed | tf_op | source)
XLA Modules:
  0.0 78.2 jit_solution(13406272951423226715)
XLA Ops:
  0.0 3.5 %collective-permute-start.8 = (bf16[1280,2560]{1,0:T(8,128)(2,1)}, bf16[1280,2560]{1,0:T(8,128)(2,1)S(1)}, u32[]{:S(2)}, u32[]{:S(2)}) collective-permute-start(bf16[1280,2560]{1,0:T(8,128)(2,1)} %param.16), channel_id=1, source_target_pairs={{0,0},{1,1},{2,3},{3,2},{4,4},{5,5},{6,7},{7,6},{8,8},{9,9},{10,11... | collective-permute-start | bytes 19660808 | tf_op jit(solution)/shard_map/ppermute | solution.py:396
  3.5 2.4 %collective-permute-start.9 = (bf16[1280,2560]{1,0:T(8,128)(2,1)}, bf16[1280,2560]{1,0:T(8,128)(2,1)S(1)}, u32[]{:S(2)}, u32[]{:S(2)}) collective-permute-start(bf16[1280,2560]{1,0:T(8,128)(2,1)} %param.16), channel_id=1, source_target_pairs={{0,1},{1,0},{2,2},{3,3},{4,5},{5,4},{6,6},{7,7},{8,9},{9,8},{10,10... | collective-permute-start | bytes 19660808 | tf_op jit(solution)/shard_map/ppermute | solution.py:397
  5.9 1.2 %shard_map.121 = (bf16[2,128,640]{2,1,0:T(8,128)(2,1)S(1)}, bf16[2,128,640]{2,1,0:T(8,128)(2,1)S(1)}) custom-call(bf16[128,1280]{1,0:T(8,128)(2,1)} %bitcast.17, bf16[128,1280]{1,0:T(8,128)(2,1)} %bitcast.18), custom_call_target="tpu_custom_call" | custom-call | bytes 1310720 | tf_op jit(solution)/shard_map/pallas_call | solution.py:340
  7.8 2.6 %collective-permute-start.4 = (bf16[2,128,640]{2,1,0:T(8,128)(2,1)S(1)}, bf16[2,128,640]{2,1,0:T(8,128)(2,1)S(1)}, u32[]{:S(2)}, u32[]{:S(2)}) collective-permute-start(bf16[2,128,640]{2,1,0:T(8,128)(2,1)S(1)} %get-tuple-element.40), channel_id=1, source_target_pairs={{0,4},{1,12},{4,0},{5,8},{8,5},{9,13},{12,1},{13,9},{2,6},{3,14},{... | collective-permute-start | bytes 983048 | tf_op jit(solution)/shard_map/ppermute | solution.py:393
  10.4 1.0 %shard_map.120 = (bf16[1,128,640]{2,1,0:T(8,128)(2,1)S(1)}, bf16[1,128,640]{2,1,0:T(8,128)(2,1)S(1)}) custom-call(bf16[128,1280]{1,0:T(8,128)(2,1)} %bitcast.19), custom_call_target="tpu_custom_call" | custom-call | bytes 655360 | tf_op jit(solution)/shard_map/pallas_call | solution.py:340
  12.1 14.2 %collective-permute-start.5 = (bf16[2,128,640]{2,1,0:T(8,128)(2,1)S(1)}, bf16[2,128,640]{2,1,0:T(8,128)(2,1)S(1)}, u32[]{:S(2)}, u32[]{:S(2)}) collective-permute-start(bf16[2,128,640]{2,1,0:T(8,128)(2,1)S(1)} %collective-permute-done.3.refs_2_), channel_id=1, source_target_pairs={{0,1},{1,0},{2,3},{3,2},{4,5},{5,4},{6,7},{7,6},{8,9},{9,8},{10,11... | collective-permute-start | bytes 983048 | tf_op jit(solution)/shard_map/ppermute | solution.py:398
  26.3 4.2 %collective-permute-start.2 = (bf16[1,128,640]{2,1,0:T(8,128)(2,1)S(1)}, bf16[1,128,640]{2,1,0:T(8,128)(2,1)S(1)}, u32[]{:S(2)}, u32[]{:S(2)}) collective-permute-start(bf16[1,128,640]{2,1,0:T(8,128)(2,1)S(1)} %get-tuple-element.35), channel_id=1, source_target_pairs={{0,4},{1,12},{4,0},{5,8},{8,5},{9,13},{12,1},{13,9},{2,6},{3,14},{... | collective-permute-start | bytes 491528 | tf_op jit(solution)/shard_map/ppermute | solution.py:395
  31.8 2.4 %shard_map.118 = (f32[64,128]{1,0:T(8,128)S(1)}, f32[16,128]{1,0:T(8,128)S(1)}, f32[8,128]{1,0:T(8,128)S(1)}) custom-call(f32[1,2560]{1,0:T(1,128)} %refs_4_.7, f32[1,2560]{1,0:T(1,128)} %shift_hbm.1, bf16[64,2560]{1,0:T(8,128)(2,1)} %bitcast.11, s32[1,4]{1,0:T(1,128)S(1)} %copy-done.4, s32[1]{0:T(128)S(6)} %copy.13.steps_ref), custom_call_target="tpu_custom_call" | custom-call | bytes 1310720 | tf_op jit(solution)/shard_map/pallas_call | solution.py:340
  34.3 1.2 %shard_map.122 = (bf16[128,640]{1,0:T(8,128)(2,1)S(1)}, bf16[128,640]{1,0:T(8,128)(2,1)S(1)}) custom-call(bf16[1,128,640]{2,1,0:T(8,128)(2,1)S(1)} %collective-permute-done.1.refs_0_, bf16[1,128,640]{2,1,0:T(8,128)(2,1)S(1)} %collective-permute-done.2.refs_1_, bf16[2,128,640]{2,1,0:T(8,128)(2,1)S(1)} %collective-permute-done.3.refs_2_, ...), custom_call_target="tpu_custom_call" | custom-call | flops 335544320 | bytes 1966080 | tf_op jit(solution)/shard_map/pallas_call | solution.py:340
  35.4 1.7 %collective-permute-start.7 = (bf16[128,640]{1,0:T(8,128)(2,1)S(1)}, bf16[128,640]{1,0:T(8,128)(2,1)S(1)}, u32[]{:S(2)}, u32[]{:S(2)}) collective-permute-start(bf16[128,640]{1,0:T(8,128)(2,1)S(1)} %get-tuple-element.42), channel_id=1, source_target_pairs={{0,4},{4,0},{8,12},{12,8},{1,5},{5,1},{9,13},{13,9},{2,6},{6,2},{1... | collective-permute-start | bytes 491528 | tf_op jit(solution)/shard_map/ppermute | solution.py:437
  37.1 1.1 %shard_map.119 = (bf16[128,1280]{1,0:T(8,128)(2,1)S(1)}, bf16[128,1280]{1,0:T(8,128)(2,1)S(1)}) custom-call(bf16[128,2560]{1,0:T(8,128)(2,1)} %bitcast.16), custom_call_target="tpu_custom_call" | custom-call | bytes 1310720 | tf_op jit(solution)/shard_map/pallas_call | solution.py:340
  38.9 1.9 %collective-permute-done.7.refs_1_ = bf16[128,640]{1,0:T(8,128)(2,1)S(1)} collective-permute-done((bf16[128,640]{1,0:T(8,128)(2,1)S(1)}, bf16[128,640]{1,0:T(8,128)(2,1)S(1)}, u32[]{:S(2)}, u32[]{:S(2)}) %collective-permute-start.7) | collective-permute-done | bytes 163872 | tf_op jit(solution)/shard_map/ppermute | solution.py:437
  40.8 1.1 %shard_map.126 = bf16[128,1280]{1,0:T(8,128)(2,1)S(1)} custom-call(bf16[128,640]{1,0:T(8,128)(2,1)S(1)} %get-tuple-element.41.refs_0_, bf16[128,640]{1,0:T(8,128)(2,1)S(1)} %collective-permute-done.7.refs_1_, bf16[1280,2560]{1,0:T(8,128)(2,1)S(1)} %collective-permute-done.8.refs_2_, bf16[1280,2560]{1,0:T(8,128)(2,1)S(1)} %collective-permute-done.9.refs_3_), custom_call_target="tpu_custom_call" | custom-call | flops 419430400 | bytes 3276800 | tf_op jit(solution)/shard_map/pallas_call | solution.py:340
  42.0 1.8 %collective-permute-start.13 = (bf16[128,1280]{1,0:T(8,128)(2,1)S(1)}, bf16[128,1280]{1,0:T(8,128)(2,1)S(1)}, u32[]{:S(2)}, u32[]{:S(2)}) collective-permute-start(bf16[128,1280]{1,0:T(8,128)(2,1)S(1)} %shard_map.126), channel_id=1, source_target_pairs={{0,2},{2,0},{1,3},{3,1},{4,6},{6,4},{5,7},{7,5},{8,10},{10,8},{9,1... | collective-permute-start | bytes 983048 | tf_op jit(solution)/shard_map/ppermute | solution.py:451
  46.1 1.8 %collective-permute-start.10 = (bf16[128,640]{1,0:T(8,128)(2,1)S(1)}, bf16[128,640]{1,0:T(8,128)(2,1)S(1)}, u32[]{:S(2)}, u32[]{:S(2)}) collective-permute-start(bf16[128,640]{1,0:T(8,128)(2,1)S(1)} %shard_map.124), channel_id=1, source_target_pairs={{0,2},{2,0},{1,3},{3,1},{4,6},{6,4},{5,7},{7,5},{8,10},{10,8},{9,1... | collective-permute-start | bytes 491528 | tf_op jit(solution)/shard_map/ppermute | solution.py:451
  48.0 2.1 %shard_map.123.refs_1_ = f32[128,2560]{1,0:T(8,128)S(1)} custom-call(bf16[128,640]{1,0:T(8,128)(2,1)S(1)} %get-tuple-element.41.refs_0_, bf16[128,640]{1,0:T(8,128)(2,1)S(1)} %collective-permute-done.7.refs_1_, bf16[1280,2560]{1,0:T(8,128)(2,1)S(1)} %collective-permute-done.8.refs_2_, bf16[1280,2560]{1,0:T(8,128)(2,1)S(1)} %collective-permute-done.9.refs_3_, ...), custom_call_target="tpu_custom_call" | custom-call | flops 838860800 | bytes 6553600 | tf_op jit(solution)/shard_map/pallas_call | solution.py:340
  51.8 3.2 %collective-permute-done.10.refs_2_ = bf16[128,640]{1,0:T(8,128)(2,1)S(1)} collective-permute-done((bf16[128,640]{1,0:T(8,128)(2,1)S(1)}, bf16[128,640]{1,0:T(8,128)(2,1)S(1)}, u32[]{:S(2)}, u32[]{:S(2)}) %collective-permute-start.10) | collective-permute-done | bytes 163872 | tf_op jit(solution)/shard_map/ppermute | solution.py:451
  55.2 2.1 %collective-permute-start.14 = (f32[72,128]{1,0:T(8,128)S(1)}, f32[72,128]{1,0:T(8,128)S(1)}, u32[]{:S(2)}, u32[]{:S(2)}) collective-permute-start(f32[72,128]{1,0:T(8,128)S(1)} %shard_map.129.own_ref), channel_id=1, source_target_pairs={{0,2},{2,0},{1,3},{3,1},{4,6},{6,4},{5,7},{7,5},{8,10},{10,8},{9,1... | collective-permute-start | bytes 110600 | tf_op jit(solution)/shard_map/ppermute | solution.py:472
  57.4 3.8 %collective-permute-done.15.rows_got_ref = f32[64,128]{1,0:T(8,128)S(1)} collective-permute-done((f32[64,128]{1,0:T(8,128)S(1)}, f32[64,128]{1,0:T(8,128)S(1)}, u32[]{:S(2)}, u32[]{:S(2)}) %collective-permute-start.15) | collective-permute-done | bytes 32800 | tf_op jit(solution)/shard_map/ppermute | solution.py:423
  61.3 5.3 %collective-permute-start.16 = (f32[32,128]{1,0:T(8,128)S(1)}, f32[32,128]{1,0:T(8,128)S(1)}, u32[]{:S(2)}, u32[]{:S(2)}) collective-permute-start(f32[32,128]{1,0:T(8,128)S(1)} %get-tuple-element.52), channel_id=1, source_target_pairs={{0,1},{1,0},{2,3},{3,2},{4,5},{5,4},{6,7},{7,6},{8,9},{9,8},{10,11... | collective-permute-start | bytes 49160 | tf_op jit(solution)/shard_map/ppermute | solution.py:479
  66.7 0.8 %collective-permute-done.16.got_ref = f32[32,128]{1,0:T(8,128)S(1)} collective-permute-done((f32[32,128]{1,0:T(8,128)S(1)}, f32[32,128]{1,0:T(8,128)S(1)}, u32[]{:S(2)}, u32[]{:S(2)}) %collective-permute-start.16) | collective-permute-done | bytes 16416 | tf_op jit(solution)/shard_map/ppermute | solution.py:479
  67.7 4.3 %collective-permute-start.18 = (f32[16,128]{1,0:T(8,128)S(1)}, f32[16,128]{1,0:T(8,128)S(1)}, u32[]{:S(2)}, u32[]{:S(2)}) collective-permute-start(f32[16,128]{1,0:T(8,128)S(1)} %get-tuple-element.55), channel_id=1, source_target_pairs={{0,8},{4,12},{8,0},{12,4},{1,9},{5,13},{9,1},{13,5},{2,10},{6,14},... | collective-permute-start | bytes 24584 | tf_op jit(solution)/shard_map/ppermute | solution.py:487
  72.1 1.6 %collective-permute-done.18.refs_2_ = f32[16,128]{1,0:T(8,128)S(1)} collective-permute-done((f32[16,128]{1,0:T(8,128)S(1)}, f32[16,128]{1,0:T(8,128)S(1)}, u32[]{:S(2)}, u32[]{:S(2)}) %collective-permute-start.18) | collective-permute-done | bytes 8224 | tf_op jit(solution)/shard_map/ppermute | solution.py:487
  73.6 3.8 %collective-permute-done.19.refs_3_ = f32[16,128]{1,0:T(8,128)S(1)} collective-permute-done((f32[16,128]{1,0:T(8,128)S(1)}, f32[16,128]{1,0:T(8,128)S(1)}, u32[]{:S(2)}, u32[]{:S(2)}) %collective-permute-start.19) | collective-permute-done | bytes 8224 | tf_op jit(solution)/shard_map/ppermute | solution.py:487
  (41 shorter events, 8.1 us)
Async XLA Ops:
  0.0 40.8 %collective-permute-start.8 = (bf16[1280,2560]{1,0:T(8,128)(2,1)}, bf16[1280,2560]{1,0:T(8,128)(2,1)S(1)}, u32[]{:S(2)}, u32[]{:S(2)}) collective-permute-start(bf16[1280,2560]{1,0:T(8,128)(2,1)} %param.16), channel_id=1, source_target_pairs={{0,0},{1,1},{2,3},{3,2},{4,4},{5,5},{6,7},{7,6},{8,8},{9,9},{10,11... | collective-permute-start | bytes 19660808 | tf_op jit(solution)/shard_map/ppermute | solution.py:396
  3.5 37.3 %collective-permute-start.9 = (bf16[1280,2560]{1,0:T(8,128)(2,1)}, bf16[1280,2560]{1,0:T(8,128)(2,1)S(1)}, u32[]{:S(2)}, u32[]{:S(2)}) collective-permute-start(bf16[1280,2560]{1,0:T(8,128)(2,1)} %param.16), channel_id=1, source_target_pairs={{0,1},{1,0},{2,2},{3,3},{4,5},{5,4},{6,6},{7,7},{8,9},{9,8},{10,10... | collective-permute-start | bytes 19660808 | tf_op jit(solution)/shard_map/ppermute | solution.py:397
  7.1 5.0 %collective-permute-start.3 = (bf16[2,128,640]{2,1,0:T(8,128)(2,1)S(1)}, bf16[2,128,640]{2,1,0:T(8,128)(2,1)S(1)}, u32[]{:S(2)}, u32[]{:S(2)}) collective-permute-start(bf16[2,128,640]{2,1,0:T(8,128)(2,1)S(1)} %get-tuple-element.39), channel_id=1, source_target_pairs={{0,0},{1,8},{4,4},{5,12},{8,1},{9,9},{12,5},{13,13},{2,2},{3,10},{... | collective-permute-start | bytes 983048 | tf_op jit(solution)/shard_map/ppermute | solution.py:393
  7.8 18.5 %collective-permute-start.4 = (bf16[2,128,640]{2,1,0:T(8,128)(2,1)S(1)}, bf16[2,128,640]{2,1,0:T(8,128)(2,1)S(1)}, u32[]{:S(2)}, u32[]{:S(2)}) collective-permute-start(bf16[2,128,640]{2,1,0:T(8,128)(2,1)S(1)} %get-tuple-element.40), channel_id=1, source_target_pairs={{0,4},{1,12},{4,0},{5,8},{8,5},{9,13},{12,1},{13,9},{2,6},{3,14},{... | collective-permute-start | bytes 983048 | tf_op jit(solution)/shard_map/ppermute | solution.py:393
  11.5 14.9 %collective-permute-start.1 = (bf16[1,128,640]{2,1,0:T(8,128)(2,1)S(1)}, bf16[1,128,640]{2,1,0:T(8,128)(2,1)S(1)}, u32[]{:S(2)}, u32[]{:S(2)}) collective-permute-start(bf16[1,128,640]{2,1,0:T(8,128)(2,1)S(1)} %get-tuple-element.34), channel_id=1, source_target_pairs={{0,0},{1,8},{4,4},{5,12},{8,1},{9,9},{12,5},{13,13},{2,2},{3,10},{... | collective-permute-start | bytes 491528 | tf_op jit(solution)/shard_map/ppermute | solution.py:395
  12.1 22.1 %collective-permute-start.5 = (bf16[2,128,640]{2,1,0:T(8,128)(2,1)S(1)}, bf16[2,128,640]{2,1,0:T(8,128)(2,1)S(1)}, u32[]{:S(2)}, u32[]{:S(2)}) collective-permute-start(bf16[2,128,640]{2,1,0:T(8,128)(2,1)S(1)} %collective-permute-done.3.refs_2_), channel_id=1, source_target_pairs={{0,1},{1,0},{2,3},{3,2},{4,5},{5,4},{6,7},{7,6},{8,9},{9,8},{10,11... | collective-permute-start | bytes 983048 | tf_op jit(solution)/shard_map/ppermute | solution.py:398
  26.3 7.9 %collective-permute-start.6 = (bf16[2,128,640]{2,1,0:T(8,128)(2,1)S(1)}, bf16[2,128,640]{2,1,0:T(8,128)(2,1)S(1)}, u32[]{:S(2)}, u32[]{:S(2)}) collective-permute-start(bf16[2,128,640]{2,1,0:T(8,128)(2,1)S(1)} %collective-permute-done.4.refs_3_), channel_id=1, source_target_pairs={{0,1},{1,0},{2,3},{3,2},{4,5},{5,4},{6,7},{7,6},{8,9},{9,8},{10,11... | collective-permute-start | bytes 983048 | tf_op jit(solution)/shard_map/ppermute | solution.py:398
  26.3 7.9 %collective-permute-start.2 = (bf16[1,128,640]{2,1,0:T(8,128)(2,1)S(1)}, bf16[1,128,640]{2,1,0:T(8,128)(2,1)S(1)}, u32[]{:S(2)}, u32[]{:S(2)}) collective-permute-start(bf16[1,128,640]{2,1,0:T(8,128)(2,1)S(1)} %get-tuple-element.35), channel_id=1, source_target_pairs={{0,4},{1,12},{4,0},{5,8},{8,5},{9,13},{12,1},{13,9},{2,6},{3,14},{... | collective-permute-start | bytes 491528 | tf_op jit(solution)/shard_map/ppermute | solution.py:395
  35.4 5.4 %collective-permute-start.7 = (bf16[128,640]{1,0:T(8,128)(2,1)S(1)}, bf16[128,640]{1,0:T(8,128)(2,1)S(1)}, u32[]{:S(2)}, u32[]{:S(2)}) collective-permute-start(bf16[128,640]{1,0:T(8,128)(2,1)S(1)} %get-tuple-element.42), channel_id=1, source_target_pairs={{0,4},{4,0},{8,12},{12,8},{1,5},{5,1},{9,13},{13,9},{2,6},{6,2},{1... | collective-permute-start | bytes 491528 | tf_op jit(solution)/shard_map/ppermute | solution.py:437
  38.2 11.9 %collective-permute-start.12 = (bf16[128,1280]{1,0:T(8,128)(2,1)S(1)}, bf16[128,1280]{1,0:T(8,128)(2,1)S(1)}, u32[]{:S(2)}, u32[]{:S(2)}) collective-permute-start(bf16[128,1280]{1,0:T(8,128)(2,1)S(1)} %get-tuple-element.43), channel_id=1, source_target_pairs={{0,0},{1,8},{4,4},{5,12},{8,1},{9,9},{12,5},{13,13},{2,2},{3,10},{... | collective-permute-start | bytes 983048 | tf_op jit(solution)/shard_map/ppermute | solution.py:407
  42.0 8.1 %collective-permute-start.13 = (bf16[128,1280]{1,0:T(8,128)(2,1)S(1)}, bf16[128,1280]{1,0:T(8,128)(2,1)S(1)}, u32[]{:S(2)}, u32[]{:S(2)}) collective-permute-start(bf16[128,1280]{1,0:T(8,128)(2,1)S(1)} %shard_map.126), channel_id=1, source_target_pairs={{0,2},{2,0},{1,3},{3,1},{4,6},{6,4},{5,7},{7,5},{8,10},{10,8},{9,1... | collective-permute-start | bytes 983048 | tf_op jit(solution)/shard_map/ppermute | solution.py:451
  43.8 6.9 %collective-permute-start = (bf16[128,1280]{1,0:T(8,128)(2,1)S(1)}, bf16[128,1280]{1,0:T(8,128)(2,1)S(1)}, u32[]{:S(2)}, u32[]{:S(2)}) collective-permute-start(bf16[128,1280]{1,0:T(8,128)(2,1)S(1)} %get-tuple-element.33), channel_id=1, source_target_pairs={{0,0},{1,8},{4,4},{5,12},{8,1},{9,9},{12,5},{13,13},{2,2},{3,10},{... | collective-permute-start | bytes 983048 | tf_op jit(solution)/shard_map/ppermute | solution.py:407
  45.1 2.8 %copy-start.1 = (f32[1,2560]{1,0:T(1,128)S(1)}, f32[1,2560]{1,0:T(1,128)}, u32[]{:S(2)}) copy-start(f32[1,2560]{1,0:T(1,128)} %refs_3_.5) | copy-start | bytes 30724
  45.1 6.3 %collective-permute-start.11 = (bf16[128,640]{1,0:T(8,128)(2,1)S(1)}, bf16[128,640]{1,0:T(8,128)(2,1)S(1)}, u32[]{:S(2)}, u32[]{:S(2)}) collective-permute-start(bf16[128,640]{1,0:T(8,128)(2,1)S(1)} %shard_map.125), channel_id=1, source_target_pairs={{0,2},{2,0},{1,3},{3,1},{4,6},{6,4},{5,7},{7,5},{8,10},{10,8},{9,1... | collective-permute-start | bytes 491528 | tf_op jit(solution)/shard_map/ppermute | solution.py:451
  46.1 4.0 %copy-start = (bf16[2560,64]{0,1:T(8,128)(2,1)S(1)}, bf16[2560,64]{0,1:T(8,128)(2,1)}, u32[]{:S(2)}) copy-start(bf16[2560,64]{0,1:T(8,128)(2,1)} %param.20) | copy-start | bytes 983044
  46.1 4.0 %copy-start.2 = (f32[1,2560]{1,0:T(1,128)S(1)}, f32[1,2560]{1,0:T(1,128)}, u32[]{:S(2)}) copy-start(f32[1,2560]{1,0:T(1,128)} %refs_4_.7) | copy-start | bytes 30724
  46.1 8.8 %collective-permute-start.10 = (bf16[128,640]{1,0:T(8,128)(2,1)S(1)}, bf16[128,640]{1,0:T(8,128)(2,1)S(1)}, u32[]{:S(2)}, u32[]{:S(2)}) collective-permute-start(bf16[128,640]{1,0:T(8,128)(2,1)S(1)} %shard_map.124), channel_id=1, source_target_pairs={{0,2},{2,0},{1,3},{3,1},{4,6},{6,4},{5,7},{7,5},{8,10},{10,8},{9,1... | collective-permute-start | bytes 491528 | tf_op jit(solution)/shard_map/ppermute | solution.py:451
  50.1 27.4 %copy-start.3 = (f32[1,1,128,32]{2,3,1,0:T(8,128)S(1)}, f32[1,1,128,32]{2,3,1,0:T(8,128)}, u32[]{:S(2)}) copy-start(f32[1,1,128,32]{2,3,1,0:T(8,128)} %param.21) | copy-start | bytes 49156
  55.2 6.0 %collective-permute-start.14 = (f32[72,128]{1,0:T(8,128)S(1)}, f32[72,128]{1,0:T(8,128)S(1)}, u32[]{:S(2)}, u32[]{:S(2)}) collective-permute-start(f32[72,128]{1,0:T(8,128)S(1)} %shard_map.129.own_ref), channel_id=1, source_target_pairs={{0,2},{2,0},{1,3},{3,1},{4,6},{6,4},{5,7},{7,5},{8,10},{10,8},{9,1... | collective-permute-start | bytes 110600 | tf_op jit(solution)/shard_map/ppermute | solution.py:472
  57.3 3.9 %collective-permute-start.15 = (f32[64,128]{1,0:T(8,128)S(1)}, f32[64,128]{1,0:T(8,128)S(1)}, u32[]{:S(2)}, u32[]{:S(2)}) collective-permute-start(f32[64,128]{1,0:T(8,128)S(1)} %get-tuple-element.50.rows_own_ref), channel_id=1, source_target_pairs={{0,2},{2,0},{1,3},{3,1},{4,6},{6,4},{5,7},{7,5},{8,10},{10,8},{9,1... | collective-permute-start | bytes 98312 | tf_op jit(solution)/shard_map/ppermute | solution.py:423
  61.3 6.2 %collective-permute-start.16 = (f32[32,128]{1,0:T(8,128)S(1)}, f32[32,128]{1,0:T(8,128)S(1)}, u32[]{:S(2)}, u32[]{:S(2)}) collective-permute-start(f32[32,128]{1,0:T(8,128)S(1)} %get-tuple-element.52), channel_id=1, source_target_pairs={{0,1},{1,0},{2,3},{3,2},{4,5},{5,4},{6,7},{7,6},{8,9},{9,8},{10,11... | collective-permute-start | bytes 49160 | tf_op jit(solution)/shard_map/ppermute | solution.py:479
  67.6 4.5 %collective-permute-start.17 = (f32[16,128]{1,0:T(8,128)S(1)}, f32[16,128]{1,0:T(8,128)S(1)}, u32[]{:S(2)}, u32[]{:S(2)}) collective-permute-start(f32[16,128]{1,0:T(8,128)S(1)} %get-tuple-element.54), channel_id=1, source_target_pairs={{0,4},{4,0},{8,12},{12,8},{1,5},{5,1},{9,13},{13,9},{2,6},{6,2},{1... | collective-permute-start | bytes 24584 | tf_op jit(solution)/shard_map/ppermute | solution.py:487
  67.7 5.9 %collective-permute-start.18 = (f32[16,128]{1,0:T(8,128)S(1)}, f32[16,128]{1,0:T(8,128)S(1)}, u32[]{:S(2)}, u32[]{:S(2)}) collective-permute-start(f32[16,128]{1,0:T(8,128)S(1)} %get-tuple-element.55), channel_id=1, source_target_pairs={{0,8},{4,12},{8,0},{12,4},{1,9},{5,13},{9,1},{13,5},{2,10},{6,14},... | collective-permute-start | bytes 24584 | tf_op jit(solution)/shard_map/ppermute | solution.py:487
  72.0 5.4 %collective-permute-start.19 = (f32[16,128]{1,0:T(8,128)S(1)}, f32[16,128]{1,0:T(8,128)S(1)}, u32[]{:S(2)}, u32[]{:S(2)}) collective-permute-start(f32[16,128]{1,0:T(8,128)S(1)} %get-tuple-element.56), channel_id=1, source_target_pairs={{0,12},{4,8},{8,4},{12,0},{1,13},{5,9},{9,5},{13,1},{2,14},{6,10},... | collective-permute-start | bytes 24584 | tf_op jit(solution)/shard_map/ppermute | solution.py:487
  (1 other events, 0.7 us)

commit v3 on v2

--- a/solution.py
+++ b/solution.py
@@ -437,16 +437,16 @@
     mixed = [mixed[0]] + [lax.ppermute(mixed[j], "seq", inside[j]) for j in range(1, parts)]
 
     chunk = 128
-    quarter = width_shard // 4
-    pieces = [(0, 2 * quarter), (2 * quarter, quarter), (3 * quarter, quarter)]
+    pieces = 4
+    width_piece = width_shard // pieces
     got = []
-    for start, width in pieces:
+    for i in range(pieces):
         partial = call(
-            functools.partial(send_kernel, parts, half, chunk, start),
-            [((rows, width), BF16)],
+            functools.partial(send_kernel, parts, half, chunk, i * width_piece),
+            [((rows, width_piece), BF16)],
             mixed + [near_w, far_w],
-            flops=2 * rows * width_local * width,
-            moved=2 * width_local * width,
+            flops=2 * rows * width_local * width_piece,
+            moved=2 * width_local * width_piece,
         )[0]
         got.append(lax.ppermute(partial, "shard", both))
     hidden = call(
@@ -457,16 +457,16 @@
         moved=2 * width_local * width_shard,
     )[0]
     state = []
-    for i, (start, width) in enumerate(pieces):
-        first, last = i == 0, i == len(pieces) - 1
+    for i in range(pieces):
+        first, last = i == 0, i == pieces - 1
         state = call(
-            functools.partial(head_kernel, first, last, chunk, start),
+            functools.partial(head_kernel, first, last, chunk, i * width_piece),
             [((channels + SUBLANES, rows), F32)]
             if last
             else [((channels, rows), F32), ((rows, LANES), F32), ((rows, LANES), F32)],
-            [res_here[0 if first else 1], hidden, got[i], attn_gate, norm_scale, head_t] + list(state),
-            flops=4 * rows * channels * width,
-            moved=6 * rows * width,
+            [res_here[i * 2 // pieces], hidden, got[i], attn_gate, norm_scale, head_t] + list(state),
+            flops=4 * rows * channels * width_piece,
+            moved=6 * rows * width_piece,
         )
     sums = state[0]
     sums_got = lax.ppermute(sums, "shard", both)

time: 78.5 us -> 81 us (1.032)
  waiting for transfers between devices: 15.8 us -> 17.3 us
    ppermute x2, waiting for transfers between devices: 0.01 us -> 2.2 us  [fast_plan(): q_own = [lax.ppermute(q_sent[j], axes, there[j]) for j in range(parts)]]
    ppermute x1, waiting for transfers between devices: 1.92 us -> 4.04 us  [fast_plan(): lax.ppermute(mixed[j], 'seq', inside[j])]
    ppermute x1, starting transfers between devices: 2.08 us -> 0.43 us  [fast_plan(): sums_got = lax.ppermute(sums, 'shard', both)]
    ppermute x1, starting transfers between devices: 0.08 us -> 1.66 us  [fast_plan(): rows_got = lax.ppermute(rows_own, 'shard', both)]
    ppermute x3, waiting for transfers between devices: 5.37 us -> 4.06 us  [fast_plan(): lax.ppermute(frames[k], 'seq', [(z, z ^ k) for z in range(seq_count)])]
    ppermute x1, starting transfers between devices: 5.34 us -> 4.38 us  [fast_plan(): eps_got = lax.ppermute(send, 'guide', both)]
    ppermute x3, starting transfers between devices: 4.44 us -> 5.38 us  [fast_plan(): lax.ppermute(frames[k], 'seq', [(z, z ^ k) for z in range(seq_count)])]
    ppermute x3 -> x4, waiting for transfers between devices: 3.83 us -> 3.09 us  [fast_plan(): got.append(lax.ppermute(partial, 'shard', both))]
  transfers between devices with their start and end apart: 20 -> 21, of which waited for: 7 -> 7; matrix products, arithmetic and copies ran while one was open for 0% -> 0% of each run, Pallas kernels for 16% -> 16%
where the time goes in v3:
time: 81 us; the launch traced here: 80.7 us
  starting transfers between devices  47.9 us (59%)
  waiting for transfers between devices  17.3 us (21%)
  Pallas kernels  13.9 us (17%)
  between operations  0.94 us (1%)
    ppermute x2, starting transfers between devices, fast_plan(): kv_other = [lax.ppermute(block, 'guide', both) for block in kv_own]  14.2 us
    pallas_call x17, Pallas kernels, call(): pl.pallas_call(kernel, out_shape=shapes, in_specs=specs or [VMEM_SPEC] *...  13.9 us
    ppermute x3, starting transfers between devices, fast_plan(): lax.ppermute(frames[k], 'seq', [(z, z ^ k) for z in range(seq_count)])  5.38 us
    ppermute x2, starting transfers between devices, fast_plan(): q_own = [lax.ppermute(q_sent[j], axes, there[j]) for j in range(parts)]  4.9 us
    ppermute x1, starting transfers between devices, fast_plan(): eps_got = lax.ppermute(send, 'guide', both)  4.38 us
    ppermute x4, starting transfers between devices, fast_plan(): got.append(lax.ppermute(partial, 'shard', both))  4.31 us
    ppermute x3, waiting for transfers between devices, fast_plan(): lax.ppermute(frames[k], 'seq', [(z, z ^ k) for z in range(seq_count)])  4.06 us
    ppermute x1, waiting for transfers between devices, fast_plan(): lax.ppermute(mixed[j], 'seq', inside[j])  4.04 us
  transfers between devices with their start and end apart: 21, of which 7 were waited for; matrix products, arithmetic and copies ran while one was open for 0% of the time, Pallas kernels for 16%

profile of v3, /device:TPU:0, one launch (start us, length us, event | category | flops | bytes accessed | tf_op | source)
XLA Modules:
  0.0 80.7 jit_solution(6090808436319039132)
XLA Ops:
  0.0 3.5 %collective-permute-start.8 = (bf16[1280,2560]{1,0:T(8,128)(2,1)}, bf16[1280,2560]{1,0:T(8,128)(2,1)S(1)}, u32[]{:S(2)}, u32[]{:S(2)}) collective-permute-start(bf16[1280,2560]{1,0:T(8,128)(2,1)} %param.16), channel_id=1, source_target_pairs={{0,0},{1,1},{2,3},{3,2},{4,4},{5,5},{6,7},{7,6},{8,8},{9,9},{10,11... | collective-permute-start | bytes 19660808 | tf_op jit(solution)/shard_map/ppermute | solution.py:396
  3.5 2.4 %collective-permute-start.9 = (bf16[1280,2560]{1,0:T(8,128)(2,1)}, bf16[1280,2560]{1,0:T(8,128)(2,1)S(1)}, u32[]{:S(2)}, u32[]{:S(2)}) collective-permute-start(bf16[1280,2560]{1,0:T(8,128)(2,1)} %param.16), channel_id=1, source_target_pairs={{0,1},{1,0},{2,2},{3,3},{4,5},{5,4},{6,6},{7,7},{8,9},{9,8},{10,10... | collective-permute-start | bytes 19660808 | tf_op jit(solution)/shard_map/ppermute | solution.py:397
  5.9 1.2 %shard_map.121 = (bf16[2,128,640]{2,1,0:T(8,128)(2,1)S(1)}, bf16[2,128,640]{2,1,0:T(8,128)(2,1)S(1)}) custom-call(bf16[128,1280]{1,0:T(8,128)(2,1)} %bitcast.18, bf16[128,1280]{1,0:T(8,128)(2,1)} %bitcast.19), custom_call_target="tpu_custom_call" | custom-call | bytes 1310720 | tf_op jit(solution)/shard_map/pallas_call | solution.py:340
  7.8 2.6 %collective-permute-start.4 = (bf16[2,128,640]{2,1,0:T(8,128)(2,1)S(1)}, bf16[2,128,640]{2,1,0:T(8,128)(2,1)S(1)}, u32[]{:S(2)}, u32[]{:S(2)}) collective-permute-start(bf16[2,128,640]{2,1,0:T(8,128)(2,1)S(1)} %get-tuple-element.43), channel_id=1, source_target_pairs={{0,4},{1,12},{4,0},{5,8},{8,5},{9,13},{12,1},{13,9},{2,6},{3,14},{... | collective-permute-start | bytes 983048 | tf_op jit(solution)/shard_map/ppermute | solution.py:393
  12.1 14.2 %collective-permute-start.5 = (bf16[2,128,640]{2,1,0:T(8,128)(2,1)S(1)}, bf16[2,128,640]{2,1,0:T(8,128)(2,1)S(1)}, u32[]{:S(2)}, u32[]{:S(2)}) collective-permute-start(bf16[2,128,640]{2,1,0:T(8,128)(2,1)S(1)} %collective-permute-done.3.refs_2_), channel_id=1, source_target_pairs={{0,1},{1,0},{2,3},{3,2},{4,5},{5,4},{6,7},{7,6},{8,9},{9,8},{10,11... | collective-permute-start | bytes 983048 | tf_op jit(solution)/shard_map/ppermute | solution.py:398
  26.3 4.2 %collective-permute-start.2 = (bf16[1,128,640]{2,1,0:T(8,128)(2,1)S(1)}, bf16[1,128,640]{2,1,0:T(8,128)(2,1)S(1)}, u32[]{:S(2)}, u32[]{:S(2)}) collective-permute-start(bf16[1,128,640]{2,1,0:T(8,128)(2,1)S(1)} %get-tuple-element.38), channel_id=1, source_target_pairs={{0,4},{1,12},{4,0},{5,8},{8,5},{9,13},{12,1},{13,9},{2,6},{3,14},{... | collective-permute-start | bytes 491528 | tf_op jit(solution)/shard_map/ppermute | solution.py:395
  30.5 1.1 %shard_map.119 = (bf16[128,1280]{1,0:T(8,128)(2,1)S(1)}, bf16[128,1280]{1,0:T(8,128)(2,1)S(1)}) custom-call(bf16[128,2560]{1,0:T(8,128)(2,1)} %bitcast.17), custom_call_target="tpu_custom_call" | custom-call | bytes 1310720 | tf_op jit(solution)/shard_map/pallas_call | solution.py:340
  31.6 2.2 %collective-permute-done.2.refs_1_ = bf16[1,128,640]{2,1,0:T(8,128)(2,1)S(1)} collective-permute-done((bf16[1,128,640]{2,1,0:T(8,128)(2,1)S(1)}, bf16[1,128,640]{2,1,0:T(8,128)(2,1)S(1)}, u32[]{:S(2)}, u32[]{:S(2)}) %collective-permute-start.2) | collective-permute-done | bytes 163872 | tf_op jit(solution)/shard_map/ppermute | solution.py:395
  35.8 2.4 %shard_map.118 = (f32[64,128]{1,0:T(8,128)S(1)}, f32[16,128]{1,0:T(8,128)S(1)}, f32[8,128]{1,0:T(8,128)S(1)}) custom-call(f32[1,2560]{1,0:T(1,128)} %refs_4_.9, f32[1,2560]{1,0:T(1,128)} %shift_hbm.1, bf16[64,2560]{1,0:T(8,128)(2,1)} %bitcast.11, s32[1,4]{1,0:T(1,128)S(1)} %copy-done.4, s32[1]{0:T(128)S(6)} %copy.13.steps_ref), custom_call_target="tpu_custom_call" | custom-call | bytes 1310720 | tf_op jit(solution)/shard_map/pallas_call | solution.py:340
  38.2 1.2 %shard_map.122 = (bf16[128,640]{1,0:T(8,128)(2,1)S(1)}, bf16[128,640]{1,0:T(8,128)(2,1)S(1)}) custom-call(bf16[1,128,640]{2,1,0:T(8,128)(2,1)S(1)} %collective-permute-done.1.refs_0_, bf16[1,128,640]{2,1,0:T(8,128)(2,1)S(1)} %collective-permute-done.2.refs_1_, bf16[2,128,640]{2,1,0:T(8,128)(2,1)S(1)} %collective-permute-done.3.refs_2_, ...), custom_call_target="tpu_custom_call" | custom-call | flops 335544320 | bytes 1966080 | tf_op jit(solution)/shard_map/pallas_call | solution.py:340
  39.4 2.1 %collective-permute-start.7 = (bf16[128,640]{1,0:T(8,128)(2,1)S(1)}, bf16[128,640]{1,0:T(8,128)(2,1)S(1)}, u32[]{:S(2)}, u32[]{:S(2)}) collective-permute-start(bf16[128,640]{1,0:T(8,128)(2,1)S(1)} %get-tuple-element.45), channel_id=1, source_target_pairs={{0,4},{4,0},{8,12},{12,8},{1,5},{5,1},{9,13},{13,9},{2,6},{6,2},{1... | collective-permute-start | bytes 491528 | tf_op jit(solution)/shard_map/ppermute | solution.py:437
  42.2 4.0 %collective-permute-done.7.refs_1_ = bf16[128,640]{1,0:T(8,128)(2,1)S(1)} collective-permute-done((bf16[128,640]{1,0:T(8,128)(2,1)S(1)}, bf16[128,640]{1,0:T(8,128)(2,1)S(1)}, u32[]{:S(2)}, u32[]{:S(2)}) %collective-permute-start.7) | collective-permute-done | bytes 163872 | tf_op jit(solution)/shard_map/ppermute | solution.py:437
  46.9 1.5 %collective-permute-start.14 = (bf16[128,640]{1,0:T(8,128)(2,1)S(1)}, bf16[128,640]{1,0:T(8,128)(2,1)S(1)}, u32[]{:S(2)}, u32[]{:S(2)}) collective-permute-start(bf16[128,640]{1,0:T(8,128)(2,1)S(1)} %shard_map.127), channel_id=1, source_target_pairs={{0,2},{2,0},{1,3},{3,1},{4,6},{6,4},{5,7},{7,5},{8,10},{10,8},{9,1... | collective-permute-start | bytes 491528 | tf_op jit(solution)/shard_map/ppermute | solution.py:451
  50.3 1.5 %collective-permute-start.11 = (bf16[128,640]{1,0:T(8,128)(2,1)S(1)}, bf16[128,640]{1,0:T(8,128)(2,1)S(1)}, u32[]{:S(2)}, u32[]{:S(2)}) collective-permute-start(bf16[128,640]{1,0:T(8,128)(2,1)S(1)} %shard_map.125), channel_id=1, source_target_pairs={{0,2},{2,0},{1,3},{3,1},{4,6},{6,4},{5,7},{7,5},{8,10},{10,8},{9,1... | collective-permute-start | bytes 491528 | tf_op jit(solution)/shard_map/ppermute | solution.py:451
  53.1 2.3 %shard_map.123.refs_1_ = f32[128,2560]{1,0:T(8,128)S(1)} custom-call(bf16[128,640]{1,0:T(8,128)(2,1)S(1)} %get-tuple-element.44.refs_0_, bf16[128,640]{1,0:T(8,128)(2,1)S(1)} %collective-permute-done.7.refs_1_, bf16[1280,2560]{1,0:T(8,128)(2,1)S(1)} %collective-permute-done.8.refs_2_, bf16[1280,2560]{1,0:T(8,128)(2,1)S(1)} %collective-permute-done.9.refs_3_, ...), custom_call_target="tpu_custom_call" | custom-call | flops 838860800 | bytes 6553600 | tf_op jit(solution)/shard_map/pallas_call | solution.py:340
  56.6 3.1 %collective-permute-done.10.refs_2_ = bf16[128,640]{1,0:T(8,128)(2,1)S(1)} collective-permute-done((bf16[128,640]{1,0:T(8,128)(2,1)S(1)}, bf16[128,640]{1,0:T(8,128)(2,1)S(1)}, u32[]{:S(2)}, u32[]{:S(2)}) %collective-permute-start.10) | collective-permute-done | bytes 163872 | tf_op jit(solution)/shard_map/ppermute | solution.py:451
  60.4 1.7 %collective-permute-start.16 = (f32[64,128]{1,0:T(8,128)S(1)}, f32[64,128]{1,0:T(8,128)S(1)}, u32[]{:S(2)}, u32[]{:S(2)}) collective-permute-start(f32[64,128]{1,0:T(8,128)S(1)} %get-tuple-element.56.rows_own_ref), channel_id=1, source_target_pairs={{0,2},{2,0},{1,3},{3,1},{4,6},{6,4},{5,7},{7,5},{8,10},{10,8},{9,1... | collective-permute-start | bytes 98312 | tf_op jit(solution)/shard_map/ppermute | solution.py:423
  62.1 3.0 %collective-permute-done.16.rows_got_ref = f32[64,128]{1,0:T(8,128)S(1)} collective-permute-done((f32[64,128]{1,0:T(8,128)S(1)}, f32[64,128]{1,0:T(8,128)S(1)}, u32[]{:S(2)}, u32[]{:S(2)}) %collective-permute-start.16) | collective-permute-done | bytes 32800 | tf_op jit(solution)/shard_map/ppermute | solution.py:423
  65.2 4.4 %collective-permute-start.17 = (f32[32,128]{1,0:T(8,128)S(1)}, f32[32,128]{1,0:T(8,128)S(1)}, u32[]{:S(2)}, u32[]{:S(2)}) collective-permute-start(f32[32,128]{1,0:T(8,128)S(1)} %get-tuple-element.58), channel_id=1, source_target_pairs={{0,1},{1,0},{2,3},{3,2},{4,5},{5,4},{6,7},{7,6},{8,9},{9,8},{10,11... | collective-permute-start | bytes 49160 | tf_op jit(solution)/shard_map/ppermute | solution.py:479
  70.5 2.1 %collective-permute-start.18 = (f32[16,128]{1,0:T(8,128)S(1)}, f32[16,128]{1,0:T(8,128)S(1)}, u32[]{:S(2)}, u32[]{:S(2)}) collective-permute-start(f32[16,128]{1,0:T(8,128)S(1)} %get-tuple-element.60), channel_id=1, source_target_pairs={{0,4},{4,0},{8,12},{12,8},{1,5},{5,1},{9,13},{13,9},{2,6},{6,2},{1... | collective-permute-start | bytes 24584 | tf_op jit(solution)/shard_map/ppermute | solution.py:487
  72.6 1.9 %collective-permute-start.19 = (f32[16,128]{1,0:T(8,128)S(1)}, f32[16,128]{1,0:T(8,128)S(1)}, u32[]{:S(2)}, u32[]{:S(2)}) collective-permute-start(f32[16,128]{1,0:T(8,128)S(1)} %get-tuple-element.61), channel_id=1, source_target_pairs={{0,8},{4,12},{8,0},{12,4},{1,9},{5,13},{9,1},{13,5},{2,10},{6,14},... | collective-permute-start | bytes 24584 | tf_op jit(solution)/shard_map/ppermute | solution.py:487
  74.5 1.4 %collective-permute-start.20 = (f32[16,128]{1,0:T(8,128)S(1)}, f32[16,128]{1,0:T(8,128)S(1)}, u32[]{:S(2)}, u32[]{:S(2)}) collective-permute-start(f32[16,128]{1,0:T(8,128)S(1)} %get-tuple-element.62), channel_id=1, source_target_pairs={{0,12},{4,8},{8,4},{12,0},{1,13},{5,9},{9,5},{13,1},{2,14},{6,10},... | collective-permute-start | bytes 24584 | tf_op jit(solution)/shard_map/ppermute | solution.py:487
  75.9 1.2 %collective-permute-done.19.refs_2_ = f32[16,128]{1,0:T(8,128)S(1)} collective-permute-done((f32[16,128]{1,0:T(8,128)S(1)}, f32[16,128]{1,0:T(8,128)S(1)}, u32[]{:S(2)}, u32[]{:S(2)}) %collective-permute-start.19) | collective-permute-done | bytes 8224 | tf_op jit(solution)/shard_map/ppermute | solution.py:487
  77.2 2.8 %collective-permute-done.20.refs_3_ = f32[16,128]{1,0:T(8,128)S(1)} collective-permute-done((f32[16,128]{1,0:T(8,128)S(1)}, f32[16,128]{1,0:T(8,128)S(1)}, u32[]{:S(2)}, u32[]{:S(2)}) %collective-permute-start.20) | collective-permute-done | bytes 8224 | tf_op jit(solution)/shard_map/ppermute | solution.py:487
  (45 shorter events, 11.9 us)
Async XLA Ops:
  0.0 46.2 %collective-permute-start.8 = (bf16[1280,2560]{1,0:T(8,128)(2,1)}, bf16[1280,2560]{1,0:T(8,128)(2,1)S(1)}, u32[]{:S(2)}, u32[]{:S(2)}) collective-permute-start(bf16[1280,2560]{1,0:T(8,128)(2,1)} %param.16), channel_id=1, source_target_pairs={{0,0},{1,1},{2,3},{3,2},{4,4},{5,5},{6,7},{7,6},{8,8},{9,9},{10,11... | collective-permute-start | bytes 19660808 | tf_op jit(solution)/shard_map/ppermute | solution.py:396
  3.5 42.7 %collective-permute-start.9 = (bf16[1280,2560]{1,0:T(8,128)(2,1)}, bf16[1280,2560]{1,0:T(8,128)(2,1)S(1)}, u32[]{:S(2)}, u32[]{:S(2)}) collective-permute-start(bf16[1280,2560]{1,0:T(8,128)(2,1)} %param.16), channel_id=1, source_target_pairs={{0,1},{1,0},{2,2},{3,3},{4,5},{5,4},{6,6},{7,7},{8,9},{9,8},{10,10... | collective-permute-start | bytes 19660808 | tf_op jit(solution)/shard_map/ppermute | solution.py:397
  7.1 5.0 %collective-permute-start.3 = (bf16[2,128,640]{2,1,0:T(8,128)(2,1)S(1)}, bf16[2,128,640]{2,1,0:T(8,128)(2,1)S(1)}, u32[]{:S(2)}, u32[]{:S(2)}) collective-permute-start(bf16[2,128,640]{2,1,0:T(8,128)(2,1)S(1)} %get-tuple-element.42), channel_id=1, source_target_pairs={{0,0},{1,8},{4,4},{5,12},{8,1},{9,9},{12,5},{13,13},{2,2},{3,10},{... | collective-permute-start | bytes 983048 | tf_op jit(solution)/shard_map/ppermute | solution.py:393
  7.8 18.5 %collective-permute-start.4 = (bf16[2,128,640]{2,1,0:T(8,128)(2,1)S(1)}, bf16[2,128,640]{2,1,0:T(8,128)(2,1)S(1)}, u32[]{:S(2)}, u32[]{:S(2)}) collective-permute-start(bf16[2,128,640]{2,1,0:T(8,128)(2,1)S(1)} %get-tuple-element.43), channel_id=1, source_target_pairs={{0,4},{1,12},{4,0},{5,8},{8,5},{9,13},{12,1},{13,9},{2,6},{3,14},{... | collective-permute-start | bytes 983048 | tf_op jit(solution)/shard_map/ppermute | solution.py:393
  11.5 14.9 %collective-permute-start.1 = (bf16[1,128,640]{2,1,0:T(8,128)(2,1)S(1)}, bf16[1,128,640]{2,1,0:T(8,128)(2,1)S(1)}, u32[]{:S(2)}, u32[]{:S(2)}) collective-permute-start(bf16[1,128,640]{2,1,0:T(8,128)(2,1)S(1)} %get-tuple-element.37), channel_id=1, source_target_pairs={{0,0},{1,8},{4,4},{5,12},{8,1},{9,9},{12,5},{13,13},{2,2},{3,10},{... | collective-permute-start | bytes 491528 | tf_op jit(solution)/shard_map/ppermute | solution.py:395
  12.1 26.1 %collective-permute-start.5 = (bf16[2,128,640]{2,1,0:T(8,128)(2,1)S(1)}, bf16[2,128,640]{2,1,0:T(8,128)(2,1)S(1)}, u32[]{:S(2)}, u32[]{:S(2)}) collective-permute-start(bf16[2,128,640]{2,1,0:T(8,128)(2,1)S(1)} %collective-permute-done.3.refs_2_), channel_id=1, source_target_pairs={{0,1},{1,0},{2,3},{3,2},{4,5},{5,4},{6,7},{7,6},{8,9},{9,8},{10,11... | collective-permute-start | bytes 983048 | tf_op jit(solution)/shard_map/ppermute | solution.py:398
  26.3 11.9 %collective-permute-start.6 = (bf16[2,128,640]{2,1,0:T(8,128)(2,1)S(1)}, bf16[2,128,640]{2,1,0:T(8,128)(2,1)S(1)}, u32[]{:S(2)}, u32[]{:S(2)}) collective-permute-start(bf16[2,128,640]{2,1,0:T(8,128)(2,1)S(1)} %collective-permute-done.4.refs_3_), channel_id=1, source_target_pairs={{0,1},{1,0},{2,3},{3,2},{4,5},{5,4},{6,7},{7,6},{8,9},{9,8},{10,11... | collective-permute-start | bytes 983048 | tf_op jit(solution)/shard_map/ppermute | solution.py:398
  26.3 7.5 %collective-permute-start.2 = (bf16[1,128,640]{2,1,0:T(8,128)(2,1)S(1)}, bf16[1,128,640]{2,1,0:T(8,128)(2,1)S(1)}, u32[]{:S(2)}, u32[]{:S(2)}) collective-permute-start(bf16[1,128,640]{2,1,0:T(8,128)(2,1)S(1)} %get-tuple-element.38), channel_id=1, source_target_pairs={{0,4},{1,12},{4,0},{5,8},{8,5},{9,13},{12,1},{13,9},{2,6},{3,14},{... | collective-permute-start | bytes 491528 | tf_op jit(solution)/shard_map/ppermute | solution.py:395
  33.8 18.6 %collective-permute-start.12 = (bf16[128,1280]{1,0:T(8,128)(2,1)S(1)}, bf16[128,1280]{1,0:T(8,128)(2,1)S(1)}, u32[]{:S(2)}, u32[]{:S(2)}) collective-permute-start(bf16[128,1280]{1,0:T(8,128)(2,1)S(1)} %get-tuple-element.46), channel_id=1, source_target_pairs={{0,0},{1,8},{4,4},{5,12},{8,1},{9,9},{12,5},{13,13},{2,2},{3,10},{... | collective-permute-start | bytes 983048 | tf_op jit(solution)/shard_map/ppermute | solution.py:407
  39.4 6.8 %collective-permute-start.7 = (bf16[128,640]{1,0:T(8,128)(2,1)S(1)}, bf16[128,640]{1,0:T(8,128)(2,1)S(1)}, u32[]{:S(2)}, u32[]{:S(2)}) collective-permute-start(bf16[128,640]{1,0:T(8,128)(2,1)S(1)} %get-tuple-element.45), channel_id=1, source_target_pairs={{0,4},{4,0},{8,12},{12,8},{1,5},{5,1},{9,13},{13,9},{2,6},{6,2},{1... | collective-permute-start | bytes 491528 | tf_op jit(solution)/shard_map/ppermute | solution.py:437
  41.5 14.7 %collective-permute-start = (bf16[128,1280]{1,0:T(8,128)(2,1)S(1)}, bf16[128,1280]{1,0:T(8,128)(2,1)S(1)}, u32[]{:S(2)}, u32[]{:S(2)}) collective-permute-start(bf16[128,1280]{1,0:T(8,128)(2,1)S(1)} %get-tuple-element.36), channel_id=1, source_target_pairs={{0,0},{1,8},{4,4},{5,12},{8,1},{9,9},{12,5},{13,13},{2,2},{3,10},{... | collective-permute-start | bytes 983048 | tf_op jit(solution)/shard_map/ppermute | solution.py:407
  46.9 8.6 %collective-permute-start.14 = (bf16[128,640]{1,0:T(8,128)(2,1)S(1)}, bf16[128,640]{1,0:T(8,128)(2,1)S(1)}, u32[]{:S(2)}, u32[]{:S(2)}) collective-permute-start(bf16[128,640]{1,0:T(8,128)(2,1)S(1)} %shard_map.127), channel_id=1, source_target_pairs={{0,2},{2,0},{1,3},{3,1},{4,6},{6,4},{5,7},{7,5},{8,10},{10,8},{9,1... | collective-permute-start | bytes 491528 | tf_op jit(solution)/shard_map/ppermute | solution.py:451
  49.0 6.8 %collective-permute-start.13 = (bf16[128,640]{1,0:T(8,128)(2,1)S(1)}, bf16[128,640]{1,0:T(8,128)(2,1)S(1)}, u32[]{:S(2)}, u32[]{:S(2)}) collective-permute-start(bf16[128,640]{1,0:T(8,128)(2,1)S(1)} %shard_map.126), channel_id=1, source_target_pairs={{0,2},{2,0},{1,3},{3,1},{4,6},{6,4},{5,7},{7,5},{8,10},{10,8},{9,1... | collective-permute-start | bytes 491528 | tf_op jit(solution)/shard_map/ppermute | solution.py:451
  50.3 5.9 %collective-permute-start.11 = (bf16[128,640]{1,0:T(8,128)(2,1)S(1)}, bf16[128,640]{1,0:T(8,128)(2,1)S(1)}, u32[]{:S(2)}, u32[]{:S(2)}) collective-permute-start(bf16[128,640]{1,0:T(8,128)(2,1)S(1)} %shard_map.125), channel_id=1, source_target_pairs={{0,2},{2,0},{1,3},{3,1},{4,6},{6,4},{5,7},{7,5},{8,10},{10,8},{9,1... | collective-permute-start | bytes 491528 | tf_op jit(solution)/shard_map/ppermute | solution.py:451
  52.4 3.0 %copy-start = (bf16[2560,64]{0,1:T(8,128)(2,1)S(1)}, bf16[2560,64]{0,1:T(8,128)(2,1)}, u32[]{:S(2)}) copy-start(bf16[2560,64]{0,1:T(8,128)(2,1)} %param.20) | copy-start | bytes 983044
  52.4 3.0 %copy-start.2 = (f32[1,2560]{1,0:T(1,128)S(1)}, f32[1,2560]{1,0:T(1,128)}, u32[]{:S(2)}) copy-start(f32[1,2560]{1,0:T(1,128)} %refs_4_.9) | copy-start | bytes 30724
  52.5 7.2 %collective-permute-start.10 = (bf16[128,640]{1,0:T(8,128)(2,1)S(1)}, bf16[128,640]{1,0:T(8,128)(2,1)S(1)}, u32[]{:S(2)}, u32[]{:S(2)}) collective-permute-start(bf16[128,640]{1,0:T(8,128)(2,1)S(1)} %shard_map.124), channel_id=1, source_target_pairs={{0,2},{2,0},{1,3},{3,1},{4,6},{6,4},{5,7},{7,5},{8,10},{10,8},{9,1... | collective-permute-start | bytes 491528 | tf_op jit(solution)/shard_map/ppermute | solution.py:451
  55.4 24.6 %copy-start.3 = (f32[1,1,128,32]{2,3,1,0:T(8,128)S(1)}, f32[1,1,128,32]{2,3,1,0:T(8,128)}, u32[]{:S(2)}) copy-start(f32[1,1,128,32]{2,3,1,0:T(8,128)} %param.21) | copy-start | bytes 49156
  60.0 5.1 %collective-permute-start.15 = (f32[72,128]{1,0:T(8,128)S(1)}, f32[72,128]{1,0:T(8,128)S(1)}, u32[]{:S(2)}, u32[]{:S(2)}) collective-permute-start(f32[72,128]{1,0:T(8,128)S(1)} %shard_map.131.own_ref), channel_id=1, source_target_pairs={{0,2},{2,0},{1,3},{3,1},{4,6},{6,4},{5,7},{7,5},{8,10},{10,8},{9,1... | collective-permute-start | bytes 110600 | tf_op jit(solution)/shard_map/ppermute | solution.py:472
  60.4 4.7 %collective-permute-start.16 = (f32[64,128]{1,0:T(8,128)S(1)}, f32[64,128]{1,0:T(8,128)S(1)}, u32[]{:S(2)}, u32[]{:S(2)}) collective-permute-start(f32[64,128]{1,0:T(8,128)S(1)} %get-tuple-element.56.rows_own_ref), channel_id=1, source_target_pairs={{0,2},{2,0},{1,3},{3,1},{4,6},{6,4},{5,7},{7,5},{8,10},{10,8},{9,1... | collective-permute-start | bytes 98312 | tf_op jit(solution)/shard_map/ppermute | solution.py:423
  65.2 5.2 %collective-permute-start.17 = (f32[32,128]{1,0:T(8,128)S(1)}, f32[32,128]{1,0:T(8,128)S(1)}, u32[]{:S(2)}, u32[]{:S(2)}) collective-permute-start(f32[32,128]{1,0:T(8,128)S(1)} %get-tuple-element.58), channel_id=1, source_target_pairs={{0,1},{1,0},{2,3},{3,2},{4,5},{5,4},{6,7},{7,6},{8,9},{9,8},{10,11... | collective-permute-start | bytes 49160 | tf_op jit(solution)/shard_map/ppermute | solution.py:479
  70.5 5.4 %collective-permute-start.18 = (f32[16,128]{1,0:T(8,128)S(1)}, f32[16,128]{1,0:T(8,128)S(1)}, u32[]{:S(2)}, u32[]{:S(2)}) collective-permute-start(f32[16,128]{1,0:T(8,128)S(1)} %get-tuple-element.60), channel_id=1, source_target_pairs={{0,4},{4,0},{8,12},{12,8},{1,5},{5,1},{9,13},{13,9},{2,6},{6,2},{1... | collective-permute-start | bytes 24584 | tf_op jit(solution)/shard_map/ppermute | solution.py:487
  72.6 4.5 %collective-permute-start.19 = (f32[16,128]{1,0:T(8,128)S(1)}, f32[16,128]{1,0:T(8,128)S(1)}, u32[]{:S(2)}, u32[]{:S(2)}) collective-permute-start(f32[16,128]{1,0:T(8,128)S(1)} %get-tuple-element.61), channel_id=1, source_target_pairs={{0,8},{4,12},{8,0},{12,4},{1,9},{5,13},{9,1},{13,5},{2,10},{6,14},... | collective-permute-start | bytes 24584 | tf_op jit(solution)/shard_map/ppermute | solution.py:487
  74.5 5.4 %collective-permute-start.20 = (f32[16,128]{1,0:T(8,128)S(1)}, f32[16,128]{1,0:T(8,128)S(1)}, u32[]{:S(2)}, u32[]{:S(2)}) collective-permute-start(f32[16,128]{1,0:T(8,128)S(1)} %get-tuple-element.62), channel_id=1, source_target_pairs={{0,12},{4,8},{8,4},{12,0},{1,13},{5,9},{9,5},{13,1},{2,14},{6,10},... | collective-permute-start | bytes 24584 | tf_op jit(solution)/shard_map/ppermute | solution.py:487
  (2 other events, 3.5 us)

commit v4 on v3

--- a/solution.py
+++ b/solution.py
@@ -219,7 +219,7 @@
     z = lax.axis_index("seq")
     for k in range(seq_count):
         for f in range(seq_count):
-            here = jnp.where(owner_ref[0, f] == z ^ k, 1.0, 0.0)
+            here = jnp.where(owner_ref[0, f] == lax.rem(z + k, seq_count), 1.0, 0.0)
             chosen_ref[k * seq_count + f : k * seq_count + f + 1, :] = jnp.full((1, LANES), here, F32)
     weight_ref[...] = plan_weight(jnp.full((SUBLANES, LANES), steps_ref[0], jnp.int32))
     for copy in copies:
@@ -322,7 +322,7 @@
         eps_cond = jnp.zeros((rows, LANES), F32)
         eps_free = jnp.zeros((rows, LANES), F32)
         for k in range(seq_count):
-            source = z ^ k
+            source = lax.rem(z - k + seq_count, seq_count)
             branch, position = source // parts, lax.rem(source, parts)
             for sub in range(2):
                 block = parts * sub + position
@@ -484,7 +484,7 @@
         [chosen, keep, eps_got],
     )
     arrived = [frames[0]] + [
-        lax.ppermute(frames[k], "seq", [(z, z ^ k) for z in range(seq_count)])
+        lax.ppermute(frames[k], "seq", [(z, (z + k) % seq_count) for z in range(seq_count)])
         for k in range(1, seq_count)
     ]
     out = call(

time: 81 us -> 79.8 us (0.985)
  waiting for transfers between devices: 17.3 us -> 14.6 us
  starting transfers between devices: 47.9 us -> 49.3 us
    ppermute x3, waiting for transfers between devices: 4.06 us -> 1.37 us  [fast_plan(): lax.ppermute(frames[k], 'seq', [(z, (z + k) % seq_count) for z in range(s...]
    ppermute x3, starting transfers between devices: 5.38 us -> 6.83 us  [fast_plan(): lax.ppermute(frames[k], 'seq', [(z, (z + k) % seq_count) for z in range(s...]
  transfers between devices with their start and end apart: 21 -> 21, of which waited for: 7 -> 6; matrix products, arithmetic and copies ran while one was open for 0% -> 0% of each run, Pallas kernels for 16% -> 16%
where the time goes in v4:
time: 79.8 us; the launch traced here: 79.4 us
  starting transfers between devices  49.3 us (62%)
  waiting for transfers between devices  14.6 us (18%)
  Pallas kernels  13.9 us (17%)
  between operations  0.94 us (1%)
    ppermute x2, starting transfers between devices, fast_plan(): kv_other = [lax.ppermute(block, 'guide', both) for block in kv_own]  14.2 us
    pallas_call x17, Pallas kernels, call(): pl.pallas_call(kernel, out_shape=shapes, in_specs=specs or [VMEM_SPEC] *...  13.9 us
    ppermute x3, starting transfers between devices, fast_plan(): lax.ppermute(frames[k], 'seq', [(z, (z + k) % seq_count) for z in range(s...  6.83 us
    ppermute x2, starting transfers between devices, fast_plan(): q_own = [lax.ppermute(q_sent[j], axes, there[j]) for j in range(parts)]  4.9 us
    ppermute x1, starting transfers between devices, fast_plan(): eps_got = lax.ppermute(send, 'guide', both)  4.38 us
    ppermute x4, starting transfers between devices, fast_plan(): got.append(lax.ppermute(partial, 'shard', both))  4.31 us
    ppermute x1, waiting for transfers between devices, fast_plan(): lax.ppermute(mixed[j], 'seq', inside[j])  4.04 us
    ppermute x1, starting transfers between devices, fast_plan(): near_w = lax.ppermute(w_out, ('shard', 'guide'), crossed)  3.51 us
  transfers between devices with their start and end apart: 21, of which 6 were waited for; matrix products, arithmetic and copies ran while one was open for 0% of the time, Pallas kernels for 16%

profile of v4, /device:TPU:0, one launch (start us, length us, event | category | flops | bytes accessed | tf_op | source)
XLA Modules:
  0.0 79.4 jit_solution(4665785483672664525)
XLA Ops:
  0.0 3.5 %collective-permute-start.8 = (bf16[1280,2560]{1,0:T(8,128)(2,1)}, bf16[1280,2560]{1,0:T(8,128)(2,1)S(1)}, u32[]{:S(2)}, u32[]{:S(2)}) collective-permute-start(bf16[1280,2560]{1,0:T(8,128)(2,1)} %param.16), channel_id=1, source_target_pairs={{0,0},{1,1},{2,3},{3,2},{4,4},{5,5},{6,7},{7,6},{8,8},{9,9},{10,11... | collective-permute-start | bytes 19660808 | tf_op jit(solution)/shard_map/ppermute | solution.py:396
  3.5 2.4 %collective-permute-start.9 = (bf16[1280,2560]{1,0:T(8,128)(2,1)}, bf16[1280,2560]{1,0:T(8,128)(2,1)S(1)}, u32[]{:S(2)}, u32[]{:S(2)}) collective-permute-start(bf16[1280,2560]{1,0:T(8,128)(2,1)} %param.16), channel_id=1, source_target_pairs={{0,1},{1,0},{2,2},{3,3},{4,5},{5,4},{6,6},{7,7},{8,9},{9,8},{10,10... | collective-permute-start | bytes 19660808 | tf_op jit(solution)/shard_map/ppermute | solution.py:397
  5.9 1.2 %shard_map.121 = (bf16[2,128,640]{2,1,0:T(8,128)(2,1)S(1)}, bf16[2,128,640]{2,1,0:T(8,128)(2,1)S(1)}) custom-call(bf16[128,1280]{1,0:T(8,128)(2,1)} %bitcast.18, bf16[128,1280]{1,0:T(8,128)(2,1)} %bitcast.19), custom_call_target="tpu_custom_call" | custom-call | bytes 1310720 | tf_op jit(solution)/shard_map/pallas_call | solution.py:340
  7.8 2.6 %collective-permute-start.4 = (bf16[2,128,640]{2,1,0:T(8,128)(2,1)S(1)}, bf16[2,128,640]{2,1,0:T(8,128)(2,1)S(1)}, u32[]{:S(2)}, u32[]{:S(2)}) collective-permute-start(bf16[2,128,640]{2,1,0:T(8,128)(2,1)S(1)} %get-tuple-element.43), channel_id=1, source_target_pairs={{0,4},{1,12},{4,0},{5,8},{8,5},{9,13},{12,1},{13,9},{2,6},{3,14},{... | collective-permute-start | bytes 983048 | tf_op jit(solution)/shard_map/ppermute | solution.py:393
  10.4 1.0 %shard_map.120 = (bf16[1,128,640]{2,1,0:T(8,128)(2,1)S(1)}, bf16[1,128,640]{2,1,0:T(8,128)(2,1)S(1)}) custom-call(bf16[128,1280]{1,0:T(8,128)(2,1)} %bitcast.20), custom_call_target="tpu_custom_call" | custom-call | bytes 655360 | tf_op jit(solution)/shard_map/pallas_call | solution.py:340
  12.1 14.2 %collective-permute-start.5 = (bf16[2,128,640]{2,1,0:T(8,128)(2,1)S(1)}, bf16[2,128,640]{2,1,0:T(8,128)(2,1)S(1)}, u32[]{:S(2)}, u32[]{:S(2)}) collective-permute-start(bf16[2,128,640]{2,1,0:T(8,128)(2,1)S(1)} %collective-permute-done.3.refs_2_), channel_id=1, source_target_pairs={{0,1},{1,0},{2,3},{3,2},{4,5},{5,4},{6,7},{7,6},{8,9},{9,8},{10,11... | collective-permute-start | bytes 983048 | tf_op jit(solution)/shard_map/ppermute | solution.py:398
  26.3 4.2 %collective-permute-start.2 = (bf16[1,128,640]{2,1,0:T(8,128)(2,1)S(1)}, bf16[1,128,640]{2,1,0:T(8,128)(2,1)S(1)}, u32[]{:S(2)}, u32[]{:S(2)}) collective-permute-start(bf16[1,128,640]{2,1,0:T(8,128)(2,1)S(1)} %get-tuple-element.38), channel_id=1, source_target_pairs={{0,4},{1,12},{4,0},{5,8},{8,5},{9,13},{12,1},{13,9},{2,6},{3,14},{... | collective-permute-start | bytes 491528 | tf_op jit(solution)/shard_map/ppermute | solution.py:395
  30.5 1.1 %shard_map.119 = (bf16[128,1280]{1,0:T(8,128)(2,1)S(1)}, bf16[128,1280]{1,0:T(8,128)(2,1)S(1)}) custom-call(bf16[128,2560]{1,0:T(8,128)(2,1)} %bitcast.17), custom_call_target="tpu_custom_call" | custom-call | bytes 1310720 | tf_op jit(solution)/shard_map/pallas_call | solution.py:340
  31.6 2.2 %collective-permute-done.2.refs_1_ = bf16[1,128,640]{2,1,0:T(8,128)(2,1)S(1)} collective-permute-done((bf16[1,128,640]{2,1,0:T(8,128)(2,1)S(1)}, bf16[1,128,640]{2,1,0:T(8,128)(2,1)S(1)}, u32[]{:S(2)}, u32[]{:S(2)}) %collective-permute-start.2) | collective-permute-done | bytes 163872 | tf_op jit(solution)/shard_map/ppermute | solution.py:395
  35.8 2.4 %shard_map.118 = (f32[64,128]{1,0:T(8,128)S(1)}, f32[16,128]{1,0:T(8,128)S(1)}, f32[8,128]{1,0:T(8,128)S(1)}) custom-call(f32[1,2560]{1,0:T(1,128)} %refs_4_.9, f32[1,2560]{1,0:T(1,128)} %shift_hbm.1, bf16[64,2560]{1,0:T(8,128)(2,1)} %bitcast.11, s32[1,4]{1,0:T(1,128)S(1)} %copy-done.4, s32[1]{0:T(128)S(6)} %copy.13.steps_ref), custom_call_target="tpu_custom_call" | custom-call | bytes 1310720 | tf_op jit(solution)/shard_map/pallas_call | solution.py:340
  38.2 1.2 %shard_map.122 = (bf16[128,640]{1,0:T(8,128)(2,1)S(1)}, bf16[128,640]{1,0:T(8,128)(2,1)S(1)}) custom-call(bf16[1,128,640]{2,1,0:T(8,128)(2,1)S(1)} %collective-permute-done.1.refs_0_, bf16[1,128,640]{2,1,0:T(8,128)(2,1)S(1)} %collective-permute-done.2.refs_1_, bf16[2,128,640]{2,1,0:T(8,128)(2,1)S(1)} %collective-permute-done.3.refs_2_, ...), custom_call_target="tpu_custom_call" | custom-call | flops 335544320 | bytes 1966080 | tf_op jit(solution)/shard_map/pallas_call | solution.py:340
  39.4 2.1 %collective-permute-start.7 = (bf16[128,640]{1,0:T(8,128)(2,1)S(1)}, bf16[128,640]{1,0:T(8,128)(2,1)S(1)}, u32[]{:S(2)}, u32[]{:S(2)}) collective-permute-start(bf16[128,640]{1,0:T(8,128)(2,1)S(1)} %get-tuple-element.45), channel_id=1, source_target_pairs={{0,4},{4,0},{8,12},{12,8},{1,5},{5,1},{9,13},{13,9},{2,6},{6,2},{1... | collective-permute-start | bytes 491528 | tf_op jit(solution)/shard_map/ppermute | solution.py:437
  42.2 4.0 %collective-permute-done.7.refs_1_ = bf16[128,640]{1,0:T(8,128)(2,1)S(1)} collective-permute-done((bf16[128,640]{1,0:T(8,128)(2,1)S(1)}, bf16[128,640]{1,0:T(8,128)(2,1)S(1)}, u32[]{:S(2)}, u32[]{:S(2)}) %collective-permute-start.7) | collective-permute-done | bytes 163872 | tf_op jit(solution)/shard_map/ppermute | solution.py:437
  46.9 1.5 %collective-permute-start.14 = (bf16[128,640]{1,0:T(8,128)(2,1)S(1)}, bf16[128,640]{1,0:T(8,128)(2,1)S(1)}, u32[]{:S(2)}, u32[]{:S(2)}) collective-permute-start(bf16[128,640]{1,0:T(8,128)(2,1)S(1)} %shard_map.127), channel_id=1, source_target_pairs={{0,2},{2,0},{1,3},{3,1},{4,6},{6,4},{5,7},{7,5},{8,10},{10,8},{9,1... | collective-permute-start | bytes 491528 | tf_op jit(solution)/shard_map/ppermute | solution.py:451
  50.3 1.5 %collective-permute-start.11 = (bf16[128,640]{1,0:T(8,128)(2,1)S(1)}, bf16[128,640]{1,0:T(8,128)(2,1)S(1)}, u32[]{:S(2)}, u32[]{:S(2)}) collective-permute-start(bf16[128,640]{1,0:T(8,128)(2,1)S(1)} %shard_map.125), channel_id=1, source_target_pairs={{0,2},{2,0},{1,3},{3,1},{4,6},{6,4},{5,7},{7,5},{8,10},{10,8},{9,1... | collective-permute-start | bytes 491528 | tf_op jit(solution)/shard_map/ppermute | solution.py:451
  53.1 2.3 %shard_map.123.refs_1_ = f32[128,2560]{1,0:T(8,128)S(1)} custom-call(bf16[128,640]{1,0:T(8,128)(2,1)S(1)} %get-tuple-element.44.refs_0_, bf16[128,640]{1,0:T(8,128)(2,1)S(1)} %collective-permute-done.7.refs_1_, bf16[1280,2560]{1,0:T(8,128)(2,1)S(1)} %collective-permute-done.8.refs_2_, bf16[1280,2560]{1,0:T(8,128)(2,1)S(1)} %collective-permute-done.9.refs_3_, ...), custom_call_target="tpu_custom_call" | custom-call | flops 838860800 | bytes 6553600 | tf_op jit(solution)/shard_map/pallas_call | solution.py:340
  56.6 3.1 %collective-permute-done.10.refs_2_ = bf16[128,640]{1,0:T(8,128)(2,1)S(1)} collective-permute-done((bf16[128,640]{1,0:T(8,128)(2,1)S(1)}, bf16[128,640]{1,0:T(8,128)(2,1)S(1)}, u32[]{:S(2)}, u32[]{:S(2)}) %collective-permute-start.10) | collective-permute-done | bytes 163872 | tf_op jit(solution)/shard_map/ppermute | solution.py:451
  60.4 1.7 %collective-permute-start.16 = (f32[64,128]{1,0:T(8,128)S(1)}, f32[64,128]{1,0:T(8,128)S(1)}, u32[]{:S(2)}, u32[]{:S(2)}) collective-permute-start(f32[64,128]{1,0:T(8,128)S(1)} %get-tuple-element.56.rows_own_ref), channel_id=1, source_target_pairs={{0,2},{2,0},{1,3},{3,1},{4,6},{6,4},{5,7},{7,5},{8,10},{10,8},{9,1... | collective-permute-start | bytes 98312 | tf_op jit(solution)/shard_map/ppermute | solution.py:423
  62.1 3.0 %collective-permute-done.16.rows_got_ref = f32[64,128]{1,0:T(8,128)S(1)} collective-permute-done((f32[64,128]{1,0:T(8,128)S(1)}, f32[64,128]{1,0:T(8,128)S(1)}, u32[]{:S(2)}, u32[]{:S(2)}) %collective-permute-start.16) | collective-permute-done | bytes 32800 | tf_op jit(solution)/shard_map/ppermute | solution.py:423
  65.2 4.4 %collective-permute-start.17 = (f32[32,128]{1,0:T(8,128)S(1)}, f32[32,128]{1,0:T(8,128)S(1)}, u32[]{:S(2)}, u32[]{:S(2)}) collective-permute-start(f32[32,128]{1,0:T(8,128)S(1)} %get-tuple-element.58), channel_id=1, source_target_pairs={{0,1},{1,0},{2,3},{3,2},{4,5},{5,4},{6,7},{7,6},{8,9},{9,8},{10,11... | collective-permute-start | bytes 49160 | tf_op jit(solution)/shard_map/ppermute | solution.py:479
  70.5 2.1 %collective-permute-start.18 = (f32[16,128]{1,0:T(8,128)S(1)}, f32[16,128]{1,0:T(8,128)S(1)}, u32[]{:S(2)}, u32[]{:S(2)}) collective-permute-start(f32[16,128]{1,0:T(8,128)S(1)} %get-tuple-element.60), channel_id=1, source_target_pairs={{0,4},{4,8},{8,12},{12,0},{1,5},{5,9},{9,13},{13,1},{2,6},{6,10},{... | collective-permute-start | bytes 24584 | tf_op jit(solution)/shard_map/ppermute | solution.py:487
  72.6 1.9 %collective-permute-start.19 = (f32[16,128]{1,0:T(8,128)S(1)}, f32[16,128]{1,0:T(8,128)S(1)}, u32[]{:S(2)}, u32[]{:S(2)}) collective-permute-start(f32[16,128]{1,0:T(8,128)S(1)} %get-tuple-element.61), channel_id=1, source_target_pairs={{0,8},{4,12},{8,0},{12,4},{1,9},{5,13},{9,1},{13,5},{2,10},{6,14},... | collective-permute-start | bytes 24584 | tf_op jit(solution)/shard_map/ppermute | solution.py:487
  74.5 2.8 %collective-permute-start.20 = (f32[16,128]{1,0:T(8,128)S(1)}, f32[16,128]{1,0:T(8,128)S(1)}, u32[]{:S(2)}, u32[]{:S(2)}) collective-permute-start(f32[16,128]{1,0:T(8,128)S(1)} %get-tuple-element.62), channel_id=1, source_target_pairs={{0,12},{4,0},{8,4},{12,8},{1,13},{5,1},{9,5},{13,9},{2,14},{6,2},{... | collective-permute-start | bytes 24584 | tf_op jit(solution)/shard_map/ppermute | solution.py:487
  77.4 1.4 %collective-permute-done.20.refs_3_ = f32[16,128]{1,0:T(8,128)S(1)} collective-permute-done((f32[16,128]{1,0:T(8,128)S(1)}, f32[16,128]{1,0:T(8,128)S(1)}, u32[]{:S(2)}, u32[]{:S(2)}) %collective-permute-start.20) | collective-permute-done | bytes 8224 | tf_op jit(solution)/shard_map/ppermute | solution.py:487
  (45 shorter events, 10.9 us)
Async XLA Ops:
  0.0 46.2 %collective-permute-start.8 = (bf16[1280,2560]{1,0:T(8,128)(2,1)}, bf16[1280,2560]{1,0:T(8,128)(2,1)S(1)}, u32[]{:S(2)}, u32[]{:S(2)}) collective-permute-start(bf16[1280,2560]{1,0:T(8,128)(2,1)} %param.16), channel_id=1, source_target_pairs={{0,0},{1,1},{2,3},{3,2},{4,4},{5,5},{6,7},{7,6},{8,8},{9,9},{10,11... | collective-permute-start | bytes 19660808 | tf_op jit(solution)/shard_map/ppermute | solution.py:396
  3.5 42.7 %collective-permute-start.9 = (bf16[1280,2560]{1,0:T(8,128)(2,1)}, bf16[1280,2560]{1,0:T(8,128)(2,1)S(1)}, u32[]{:S(2)}, u32[]{:S(2)}) collective-permute-start(bf16[1280,2560]{1,0:T(8,128)(2,1)} %param.16), channel_id=1, source_target_pairs={{0,1},{1,0},{2,2},{3,3},{4,5},{5,4},{6,6},{7,7},{8,9},{9,8},{10,10... | collective-permute-start | bytes 19660808 | tf_op jit(solution)/shard_map/ppermute | solution.py:397
  7.1 5.0 %collective-permute-start.3 = (bf16[2,128,640]{2,1,0:T(8,128)(2,1)S(1)}, bf16[2,128,640]{2,1,0:T(8,128)(2,1)S(1)}, u32[]{:S(2)}, u32[]{:S(2)}) collective-permute-start(bf16[2,128,640]{2,1,0:T(8,128)(2,1)S(1)} %get-tuple-element.42), channel_id=1, source_target_pairs={{0,0},{1,8},{4,4},{5,12},{8,1},{9,9},{12,5},{13,13},{2,2},{3,10},{... | collective-permute-start | bytes 983048 | tf_op jit(solution)/shard_map/ppermute | solution.py:393
  7.8 18.5 %collective-permute-start.4 = (bf16[2,128,640]{2,1,0:T(8,128)(2,1)S(1)}, bf16[2,128,640]{2,1,0:T(8,128)(2,1)S(1)}, u32[]{:S(2)}, u32[]{:S(2)}) collective-permute-start(bf16[2,128,640]{2,1,0:T(8,128)(2,1)S(1)} %get-tuple-element.43), channel_id=1, source_target_pairs={{0,4},{1,12},{4,0},{5,8},{8,5},{9,13},{12,1},{13,9},{2,6},{3,14},{... | collective-permute-start | bytes 983048 | tf_op jit(solution)/shard_map/ppermute | solution.py:393
  11.5 14.9 %collective-permute-start.1 = (bf16[1,128,640]{2,1,0:T(8,128)(2,1)S(1)}, bf16[1,128,640]{2,1,0:T(8,128)(2,1)S(1)}, u32[]{:S(2)}, u32[]{:S(2)}) collective-permute-start(bf16[1,128,640]{2,1,0:T(8,128)(2,1)S(1)} %get-tuple-element.37), channel_id=1, source_target_pairs={{0,0},{1,8},{4,4},{5,12},{8,1},{9,9},{12,5},{13,13},{2,2},{3,10},{... | collective-permute-start | bytes 491528 | tf_op jit(solution)/shard_map/ppermute | solution.py:395
  12.1 26.1 %collective-permute-start.5 = (bf16[2,128,640]{2,1,0:T(8,128)(2,1)S(1)}, bf16[2,128,640]{2,1,0:T(8,128)(2,1)S(1)}, u32[]{:S(2)}, u32[]{:S(2)}) collective-permute-start(bf16[2,128,640]{2,1,0:T(8,128)(2,1)S(1)} %collective-permute-done.3.refs_2_), channel_id=1, source_target_pairs={{0,1},{1,0},{2,3},{3,2},{4,5},{5,4},{6,7},{7,6},{8,9},{9,8},{10,11... | collective-permute-start | bytes 983048 | tf_op jit(solution)/shard_map/ppermute | solution.py:398
  26.3 11.9 %collective-permute-start.6 = (bf16[2,128,640]{2,1,0:T(8,128)(2,1)S(1)}, bf16[2,128,640]{2,1,0:T(8,128)(2,1)S(1)}, u32[]{:S(2)}, u32[]{:S(2)}) collective-permute-start(bf16[2,128,640]{2,1,0:T(8,128)(2,1)S(1)} %collective-permute-done.4.refs_3_), channel_id=1, source_target_pairs={{0,1},{1,0},{2,3},{3,2},{4,5},{5,4},{6,7},{7,6},{8,9},{9,8},{10,11... | collective-permute-start | bytes 983048 | tf_op jit(solution)/shard_map/ppermute | solution.py:398
  26.3 7.5 %collective-permute-start.2 = (bf16[1,128,640]{2,1,0:T(8,128)(2,1)S(1)}, bf16[1,128,640]{2,1,0:T(8,128)(2,1)S(1)}, u32[]{:S(2)}, u32[]{:S(2)}) collective-permute-start(bf16[1,128,640]{2,1,0:T(8,128)(2,1)S(1)} %get-tuple-element.38), channel_id=1, source_target_pairs={{0,4},{1,12},{4,0},{5,8},{8,5},{9,13},{12,1},{13,9},{2,6},{3,14},{... | collective-permute-start | bytes 491528 | tf_op jit(solution)/shard_map/ppermute | solution.py:395
  33.8 18.6 %collective-permute-start.12 = (bf16[128,1280]{1,0:T(8,128)(2,1)S(1)}, bf16[128,1280]{1,0:T(8,128)(2,1)S(1)}, u32[]{:S(2)}, u32[]{:S(2)}) collective-permute-start(bf16[128,1280]{1,0:T(8,128)(2,1)S(1)} %get-tuple-element.46), channel_id=1, source_target_pairs={{0,0},{1,8},{4,4},{5,12},{8,1},{9,9},{12,5},{13,13},{2,2},{3,10},{... | collective-permute-start | bytes 983048 | tf_op jit(solution)/shard_map/ppermute | solution.py:407
  39.4 6.8 %collective-permute-start.7 = (bf16[128,640]{1,0:T(8,128)(2,1)S(1)}, bf16[128,640]{1,0:T(8,128)(2,1)S(1)}, u32[]{:S(2)}, u32[]{:S(2)}) collective-permute-start(bf16[128,640]{1,0:T(8,128)(2,1)S(1)} %get-tuple-element.45), channel_id=1, source_target_pairs={{0,4},{4,0},{8,12},{12,8},{1,5},{5,1},{9,13},{13,9},{2,6},{6,2},{1... | collective-permute-start | bytes 491528 | tf_op jit(solution)/shard_map/ppermute | solution.py:437
  41.5 14.7 %collective-permute-start = (bf16[128,1280]{1,0:T(8,128)(2,1)S(1)}, bf16[128,1280]{1,0:T(8,128)(2,1)S(1)}, u32[]{:S(2)}, u32[]{:S(2)}) collective-permute-start(bf16[128,1280]{1,0:T(8,128)(2,1)S(1)} %get-tuple-element.36), channel_id=1, source_target_pairs={{0,0},{1,8},{4,4},{5,12},{8,1},{9,9},{12,5},{13,13},{2,2},{3,10},{... | collective-permute-start | bytes 983048 | tf_op jit(solution)/shard_map/ppermute | solution.py:407
  46.9 8.6 %collective-permute-start.14 = (bf16[128,640]{1,0:T(8,128)(2,1)S(1)}, bf16[128,640]{1,0:T(8,128)(2,1)S(1)}, u32[]{:S(2)}, u32[]{:S(2)}) collective-permute-start(bf16[128,640]{1,0:T(8,128)(2,1)S(1)} %shard_map.127), channel_id=1, source_target_pairs={{0,2},{2,0},{1,3},{3,1},{4,6},{6,4},{5,7},{7,5},{8,10},{10,8},{9,1... | collective-permute-start | bytes 491528 | tf_op jit(solution)/shard_map/ppermute | solution.py:451
  49.0 6.8 %collective-permute-start.13 = (bf16[128,640]{1,0:T(8,128)(2,1)S(1)}, bf16[128,640]{1,0:T(8,128)(2,1)S(1)}, u32[]{:S(2)}, u32[]{:S(2)}) collective-permute-start(bf16[128,640]{1,0:T(8,128)(2,1)S(1)} %shard_map.126), channel_id=1, source_target_pairs={{0,2},{2,0},{1,3},{3,1},{4,6},{6,4},{5,7},{7,5},{8,10},{10,8},{9,1... | collective-permute-start | bytes 491528 | tf_op jit(solution)/shard_map/ppermute | solution.py:451
  50.3 5.9 %collective-permute-start.11 = (bf16[128,640]{1,0:T(8,128)(2,1)S(1)}, bf16[128,640]{1,0:T(8,128)(2,1)S(1)}, u32[]{:S(2)}, u32[]{:S(2)}) collective-permute-start(bf16[128,640]{1,0:T(8,128)(2,1)S(1)} %shard_map.125), channel_id=1, source_target_pairs={{0,2},{2,0},{1,3},{3,1},{4,6},{6,4},{5,7},{7,5},{8,10},{10,8},{9,1... | collective-permute-start | bytes 491528 | tf_op jit(solution)/shard_map/ppermute | solution.py:451
  52.4 3.0 %copy-start = (bf16[2560,64]{0,1:T(8,128)(2,1)S(1)}, bf16[2560,64]{0,1:T(8,128)(2,1)}, u32[]{:S(2)}) copy-start(bf16[2560,64]{0,1:T(8,128)(2,1)} %param.20) | copy-start | bytes 983044
  52.4 3.0 %copy-start.2 = (f32[1,2560]{1,0:T(1,128)S(1)}, f32[1,2560]{1,0:T(1,128)}, u32[]{:S(2)}) copy-start(f32[1,2560]{1,0:T(1,128)} %refs_4_.9) | copy-start | bytes 30724
  52.5 7.2 %collective-permute-start.10 = (bf16[128,640]{1,0:T(8,128)(2,1)S(1)}, bf16[128,640]{1,0:T(8,128)(2,1)S(1)}, u32[]{:S(2)}, u32[]{:S(2)}) collective-permute-start(bf16[128,640]{1,0:T(8,128)(2,1)S(1)} %shard_map.124), channel_id=1, source_target_pairs={{0,2},{2,0},{1,3},{3,1},{4,6},{6,4},{5,7},{7,5},{8,10},{10,8},{9,1... | collective-permute-start | bytes 491528 | tf_op jit(solution)/shard_map/ppermute | solution.py:451
  55.4 23.3 %copy-start.3 = (f32[1,1,128,32]{2,3,1,0:T(8,128)S(1)}, f32[1,1,128,32]{2,3,1,0:T(8,128)}, u32[]{:S(2)}) copy-start(f32[1,1,128,32]{2,3,1,0:T(8,128)} %param.21) | copy-start | bytes 49156
  60.0 5.1 %collective-permute-start.15 = (f32[72,128]{1,0:T(8,128)S(1)}, f32[72,128]{1,0:T(8,128)S(1)}, u32[]{:S(2)}, u32[]{:S(2)}) collective-permute-start(f32[72,128]{1,0:T(8,128)S(1)} %shard_map.131.own_ref), channel_id=1, source_target_pairs={{0,2},{2,0},{1,3},{3,1},{4,6},{6,4},{5,7},{7,5},{8,10},{10,8},{9,1... | collective-permute-start | bytes 110600 | tf_op jit(solution)/shard_map/ppermute | solution.py:472
  60.4 4.7 %collective-permute-start.16 = (f32[64,128]{1,0:T(8,128)S(1)}, f32[64,128]{1,0:T(8,128)S(1)}, u32[]{:S(2)}, u32[]{:S(2)}) collective-permute-start(f32[64,128]{1,0:T(8,128)S(1)} %get-tuple-element.56.rows_own_ref), channel_id=1, source_target_pairs={{0,2},{2,0},{1,3},{3,1},{4,6},{6,4},{5,7},{7,5},{8,10},{10,8},{9,1... | collective-permute-start | bytes 98312 | tf_op jit(solution)/shard_map/ppermute | solution.py:423
  65.2 5.2 %collective-permute-start.17 = (f32[32,128]{1,0:T(8,128)S(1)}, f32[32,128]{1,0:T(8,128)S(1)}, u32[]{:S(2)}, u32[]{:S(2)}) collective-permute-start(f32[32,128]{1,0:T(8,128)S(1)} %get-tuple-element.58), channel_id=1, source_target_pairs={{0,1},{1,0},{2,3},{3,2},{4,5},{5,4},{6,7},{7,6},{8,9},{9,8},{10,11... | collective-permute-start | bytes 49160 | tf_op jit(solution)/shard_map/ppermute | solution.py:479
  70.5 6.8 %collective-permute-start.18 = (f32[16,128]{1,0:T(8,128)S(1)}, f32[16,128]{1,0:T(8,128)S(1)}, u32[]{:S(2)}, u32[]{:S(2)}) collective-permute-start(f32[16,128]{1,0:T(8,128)S(1)} %get-tuple-element.60), channel_id=1, source_target_pairs={{0,4},{4,8},{8,12},{12,0},{1,5},{5,9},{9,13},{13,1},{2,6},{6,10},{... | collective-permute-start | bytes 24584 | tf_op jit(solution)/shard_map/ppermute | solution.py:487
  72.6 4.8 %collective-permute-start.19 = (f32[16,128]{1,0:T(8,128)S(1)}, f32[16,128]{1,0:T(8,128)S(1)}, u32[]{:S(2)}, u32[]{:S(2)}) collective-permute-start(f32[16,128]{1,0:T(8,128)S(1)} %get-tuple-element.61), channel_id=1, source_target_pairs={{0,8},{4,12},{8,0},{12,4},{1,9},{5,13},{9,1},{13,5},{2,10},{6,14},... | collective-permute-start | bytes 24584 | tf_op jit(solution)/shard_map/ppermute | solution.py:487
  74.5 4.2 %collective-permute-start.20 = (f32[16,128]{1,0:T(8,128)S(1)}, f32[16,128]{1,0:T(8,128)S(1)}, u32[]{:S(2)}, u32[]{:S(2)}) collective-permute-start(f32[16,128]{1,0:T(8,128)S(1)} %get-tuple-element.62), channel_id=1, source_target_pairs={{0,12},{4,0},{8,4},{12,8},{1,13},{5,1},{9,5},{13,9},{2,14},{6,2},{... | collective-permute-start | bytes 24584 | tf_op jit(solution)/shard_map/ppermute | solution.py:487
  (2 other events, 3.5 us)

commit v5 on v3

--- a/solution.py
+++ b/solution.py
@@ -122,13 +122,12 @@
 
 def split_kernel(source_ref, *refs):
     out_refs, sems = refs[:-1], refs[-1]
-    width = out_refs[0].shape[1]
-    copies = [
-        pltpu.make_async_copy(source_ref.at[:, pl.ds(i * width, width)], out_ref, sems.at[i])
-        for i, out_ref in enumerate(out_refs)
-    ]
-    for copy in copies:
-        copy.start()
+    copies, start = [], 0
+    for i, out_ref in enumerate(out_refs):
+        width = out_ref.shape[1]
+        copies.append(pltpu.make_async_copy(source_ref.at[:, pl.ds(start, width)], out_ref, sems.at[i]))
+        copies[-1].start()
+        start += width
     for copy in copies:
         copy.wait()
 
@@ -253,7 +252,8 @@
     for t in range(got_ref.shape[1] // chunk):
         cols = slice(start + t * chunk, start + (t + 1) * chunk)
         arrived = got_ref[:, t * chunk : (t + 1) * chunk].astype(F32)
-        here = slice(cols.start % res_ref.shape[1], cols.start % res_ref.shape[1] + chunk)
+        offset = cols.start - (hid_ref.shape[1] - res_ref.shape[1] if start else 0)
+        here = slice(offset, offset + chunk)
         hidden = res_ref[:, here].astype(F32) + hid_ref[:, cols] + gate_ref[:, cols] * arrived
         for s in range(chunk // LANES):
             piece = hidden[:, s * LANES : (s + 1) * LANES]
@@ -398,7 +398,7 @@
     kv_other = [lax.ppermute(block, "guide", both) for block in kv_own]
     res_sent = call(
         split_kernel,
-        [((rows, width_shard // 2), BF16)] * 2,
+        [((rows, width_shard // 4), BF16), ((rows, width_shard - width_shard // 4), BF16)],
         [in_hbm(residual[0, 0])],
         [HBM_SPEC],
         [pltpu.SemaphoreType.DMA((2,))],
@@ -464,7 +464,7 @@
             [((channels + SUBLANES, rows), F32)]
             if last
             else [((channels, rows), F32), ((rows, LANES), F32), ((rows, LANES), F32)],
-            [res_here[i * 2 // pieces], hidden, got[i], attn_gate, norm_scale, head_t] + list(state),
+            [res_here[0 if first else 1], hidden, got[i], attn_gate, norm_scale, head_t] + list(state),
             flops=4 * rows * channels * width_piece,
             moved=6 * rows * width_piece,
         )

time: 81 us -> 83.6 us (1.032)
  waiting for transfers between devices: 17.3 us -> 19.6 us
    ppermute x4, waiting for transfers between devices: 3.09 us -> 4.52 us  [fast_plan(): got.append(lax.ppermute(partial, 'shard', both))]
    ppermute x3, waiting for transfers between devices: 4.06 us -> 5.44 us  [fast_plan(): lax.ppermute(frames[k], 'seq', [(z, z ^ k) for z in range(seq_count)])]
    ppermute x3, starting transfers between devices: 5.38 us -> 6.52 us  [fast_plan(): lax.ppermute(frames[k], 'seq', [(z, z ^ k) for z in range(seq_count)])]
    ppermute x1, starting transfers between devices: 4.38 us -> 3.52 us  [fast_plan(): eps_got = lax.ppermute(send, 'guide', both)]
  transfers between devices with their start and end apart: 21 -> 21, of which waited for: 7 -> 8; matrix products, arithmetic and copies ran while one was open for 0% -> 0% of each run, Pallas kernels for 16% -> 15%
where the time goes in v5:
time: 83.6 us; the launch traced here: 83.3 us
  starting transfers between devices  48.1 us (58%)
  waiting for transfers between devices  19.6 us (23%)
  Pallas kernels  14 us (17%)
  between operations  0.93 us (1%)
    ppermute x2, starting transfers between devices, fast_plan(): kv_other = [lax.ppermute(block, 'guide', both) for block in kv_own]  14.2 us
    pallas_call x17, Pallas kernels, call(): pl.pallas_call(kernel, out_shape=shapes, in_specs=specs or [VMEM_SPEC] *...  14 us
    ppermute x3, starting transfers between devices, fast_plan(): lax.ppermute(frames[k], 'seq', [(z, z ^ k) for z in range(seq_count)])  6.52 us
    ppermute x3, waiting for transfers between devices, fast_plan(): lax.ppermute(frames[k], 'seq', [(z, z ^ k) for z in range(seq_count)])  5.44 us
    ppermute x2, starting transfers between devices, fast_plan(): q_own = [lax.ppermute(q_sent[j], axes, there[j]) for j in range(parts)]  4.9 us
    ppermute x4, waiting for transfers between devices, fast_plan(): got.append(lax.ppermute(partial, 'shard', both))  4.52 us
    ppermute x4, starting transfers between devices, fast_plan(): got.append(lax.ppermute(partial, 'shard', both))  4.31 us
    ppermute x1, waiting for transfers between devices, fast_plan(): lax.ppermute(mixed[j], 'seq', inside[j])  4.05 us
  transfers between devices with their start and end apart: 21, of which 8 were waited for; matrix products, arithmetic and copies ran while one was open for 0% of the time, Pallas kernels for 15%

profile of v5, /device:TPU:0, one launch (start us, length us, event | category | flops | bytes accessed | tf_op | source)
XLA Modules:
  0.0 83.3 jit_solution(10025527616108296390)
XLA Ops:
  0.0 3.5 %collective-permute-start.8 = (bf16[1280,2560]{1,0:T(8,128)(2,1)}, bf16[1280,2560]{1,0:T(8,128)(2,1)S(1)}, u32[]{:S(2)}, u32[]{:S(2)}) collective-permute-start(bf16[1280,2560]{1,0:T(8,128)(2,1)} %param.16), channel_id=1, source_target_pairs={{0,0},{1,1},{2,3},{3,2},{4,4},{5,5},{6,7},{7,6},{8,8},{9,9},{10,11... | collective-permute-start | bytes 19660808 | tf_op jit(solution)/shard_map/ppermute | solution.py:396
  3.5 2.4 %collective-permute-start.9 = (bf16[1280,2560]{1,0:T(8,128)(2,1)}, bf16[1280,2560]{1,0:T(8,128)(2,1)S(1)}, u32[]{:S(2)}, u32[]{:S(2)}) collective-permute-start(bf16[1280,2560]{1,0:T(8,128)(2,1)} %param.16), channel_id=1, source_target_pairs={{0,1},{1,0},{2,2},{3,3},{4,5},{5,4},{6,6},{7,7},{8,9},{9,8},{10,10... | collective-permute-start | bytes 19660808 | tf_op jit(solution)/shard_map/ppermute | solution.py:397
  5.9 1.2 %shard_map.121 = (bf16[2,128,640]{2,1,0:T(8,128)(2,1)S(1)}, bf16[2,128,640]{2,1,0:T(8,128)(2,1)S(1)}) custom-call(bf16[128,1280]{1,0:T(8,128)(2,1)} %bitcast.18, bf16[128,1280]{1,0:T(8,128)(2,1)} %bitcast.19), custom_call_target="tpu_custom_call" | custom-call | bytes 1310720 | tf_op jit(solution)/shard_map/pallas_call | solution.py:340
  7.8 2.6 %collective-permute-start.4 = (bf16[2,128,640]{2,1,0:T(8,128)(2,1)S(1)}, bf16[2,128,640]{2,1,0:T(8,128)(2,1)S(1)}, u32[]{:S(2)}, u32[]{:S(2)}) collective-permute-start(bf16[2,128,640]{2,1,0:T(8,128)(2,1)S(1)} %get-tuple-element.43), channel_id=1, source_target_pairs={{0,4},{1,12},{4,0},{5,8},{8,5},{9,13},{12,1},{13,9},{2,6},{3,14},{... | collective-permute-start | bytes 983048 | tf_op jit(solution)/shard_map/ppermute | solution.py:393
  12.1 14.2 %collective-permute-start.5 = (bf16[2,128,640]{2,1,0:T(8,128)(2,1)S(1)}, bf16[2,128,640]{2,1,0:T(8,128)(2,1)S(1)}, u32[]{:S(2)}, u32[]{:S(2)}) collective-permute-start(bf16[2,128,640]{2,1,0:T(8,128)(2,1)S(1)} %collective-permute-done.3.refs_2_), channel_id=1, source_target_pairs={{0,1},{1,0},{2,3},{3,2},{4,5},{5,4},{6,7},{7,6},{8,9},{9,8},{10,11... | collective-permute-start | bytes 983048 | tf_op jit(solution)/shard_map/ppermute | solution.py:398
  26.3 4.2 %collective-permute-start.2 = (bf16[1,128,640]{2,1,0:T(8,128)(2,1)S(1)}, bf16[1,128,640]{2,1,0:T(8,128)(2,1)S(1)}, u32[]{:S(2)}, u32[]{:S(2)}) collective-permute-start(bf16[1,128,640]{2,1,0:T(8,128)(2,1)S(1)} %get-tuple-element.38), channel_id=1, source_target_pairs={{0,4},{1,12},{4,0},{5,8},{8,5},{9,13},{12,1},{13,9},{2,6},{3,14},{... | collective-permute-start | bytes 491528 | tf_op jit(solution)/shard_map/ppermute | solution.py:395
  30.5 1.1 %shard_map.119 = (bf16[128,640]{1,0:T(8,128)(2,1)S(1)}, bf16[128,1920]{1,0:T(8,128)(2,1)S(1)}) custom-call(bf16[128,2560]{1,0:T(8,128)(2,1)} %bitcast.17), custom_call_target="tpu_custom_call" | custom-call | bytes 1310720 | tf_op jit(solution)/shard_map/pallas_call | solution.py:340
  31.7 2.2 %collective-permute-done.2.refs_1_ = bf16[1,128,640]{2,1,0:T(8,128)(2,1)S(1)} collective-permute-done((bf16[1,128,640]{2,1,0:T(8,128)(2,1)S(1)}, bf16[1,128,640]{2,1,0:T(8,128)(2,1)S(1)}, u32[]{:S(2)}, u32[]{:S(2)}) %collective-permute-start.2) | collective-permute-done | bytes 163872 | tf_op jit(solution)/shard_map/ppermute | solution.py:395
  35.8 2.4 %shard_map.118 = (f32[64,128]{1,0:T(8,128)S(1)}, f32[16,128]{1,0:T(8,128)S(1)}, f32[8,128]{1,0:T(8,128)S(1)}) custom-call(f32[1,2560]{1,0:T(1,128)} %refs_4_.9, f32[1,2560]{1,0:T(1,128)} %shift_hbm.1, bf16[64,2560]{1,0:T(8,128)(2,1)} %bitcast.11, s32[1,4]{1,0:T(1,128)S(1)} %copy-done.4, s32[1]{0:T(128)S(6)} %copy.13.steps_ref), custom_call_target="tpu_custom_call" | custom-call | bytes 1310720 | tf_op jit(solution)/shard_map/pallas_call | solution.py:340
  38.2 1.2 %shard_map.122 = (bf16[128,640]{1,0:T(8,128)(2,1)S(1)}, bf16[128,640]{1,0:T(8,128)(2,1)S(1)}) custom-call(bf16[1,128,640]{2,1,0:T(8,128)(2,1)S(1)} %collective-permute-done.1.refs_0_, bf16[1,128,640]{2,1,0:T(8,128)(2,1)S(1)} %collective-permute-done.2.refs_1_, bf16[2,128,640]{2,1,0:T(8,128)(2,1)S(1)} %collective-permute-done.3.refs_2_, ...), custom_call_target="tpu_custom_call" | custom-call | flops 335544320 | bytes 1966080 | tf_op jit(solution)/shard_map/pallas_call | solution.py:340
  39.4 2.1 %collective-permute-start.7 = (bf16[128,640]{1,0:T(8,128)(2,1)S(1)}, bf16[128,640]{1,0:T(8,128)(2,1)S(1)}, u32[]{:S(2)}, u32[]{:S(2)}) collective-permute-start(bf16[128,640]{1,0:T(8,128)(2,1)S(1)} %get-tuple-element.45), channel_id=1, source_target_pairs={{0,4},{4,0},{8,12},{12,8},{1,5},{5,1},{9,13},{13,9},{2,6},{6,2},{1... | collective-permute-start | bytes 491528 | tf_op jit(solution)/shard_map/ppermute | solution.py:437
  42.2 4.0 %collective-permute-done.7.refs_1_ = bf16[128,640]{1,0:T(8,128)(2,1)S(1)} collective-permute-done((bf16[128,640]{1,0:T(8,128)(2,1)S(1)}, bf16[128,640]{1,0:T(8,128)(2,1)S(1)}, u32[]{:S(2)}, u32[]{:S(2)}) %collective-permute-start.7) | collective-permute-done | bytes 163872 | tf_op jit(solution)/shard_map/ppermute | solution.py:437
  46.9 1.7 %collective-permute-start.14 = (bf16[128,640]{1,0:T(8,128)(2,1)S(1)}, bf16[128,640]{1,0:T(8,128)(2,1)S(1)}, u32[]{:S(2)}, u32[]{:S(2)}) collective-permute-start(bf16[128,640]{1,0:T(8,128)(2,1)S(1)} %shard_map.127), channel_id=1, source_target_pairs={{0,2},{2,0},{1,3},{3,1},{4,6},{6,4},{5,7},{7,5},{8,10},{10,8},{9,1... | collective-permute-start | bytes 491528 | tf_op jit(solution)/shard_map/ppermute | solution.py:451
  50.3 1.7 %collective-permute-start.11 = (bf16[128,640]{1,0:T(8,128)(2,1)S(1)}, bf16[128,640]{1,0:T(8,128)(2,1)S(1)}, u32[]{:S(2)}, u32[]{:S(2)}) collective-permute-start(bf16[128,640]{1,0:T(8,128)(2,1)S(1)} %shard_map.125), channel_id=1, source_target_pairs={{0,2},{2,0},{1,3},{3,1},{4,6},{6,4},{5,7},{7,5},{8,10},{10,8},{9,1... | collective-permute-start | bytes 491528 | tf_op jit(solution)/shard_map/ppermute | solution.py:451
  53.1 2.3 %shard_map.123.refs_1_ = f32[128,2560]{1,0:T(8,128)S(1)} custom-call(bf16[128,640]{1,0:T(8,128)(2,1)S(1)} %get-tuple-element.44.refs_0_, bf16[128,640]{1,0:T(8,128)(2,1)S(1)} %collective-permute-done.7.refs_1_, bf16[1280,2560]{1,0:T(8,128)(2,1)S(1)} %collective-permute-done.8.refs_2_, bf16[1280,2560]{1,0:T(8,128)(2,1)S(1)} %collective-permute-done.9.refs_3_, ...), custom_call_target="tpu_custom_call" | custom-call | flops 838860800 | bytes 6553600 | tf_op jit(solution)/shard_map/pallas_call | solution.py:340
  56.2 1.4 %collective-permute-done.11.refs_2_ = bf16[128,640]{1,0:T(8,128)(2,1)S(1)} collective-permute-done((bf16[128,640]{1,0:T(8,128)(2,1)S(1)}, bf16[128,640]{1,0:T(8,128)(2,1)S(1)}, u32[]{:S(2)}, u32[]{:S(2)}) %collective-permute-start.11) | collective-permute-done | bytes 163872 | tf_op jit(solution)/shard_map/ppermute | solution.py:451
  57.9 3.2 %collective-permute-done.10.refs_2_ = bf16[128,640]{1,0:T(8,128)(2,1)S(1)} collective-permute-done((bf16[128,640]{1,0:T(8,128)(2,1)S(1)}, bf16[128,640]{1,0:T(8,128)(2,1)S(1)}, u32[]{:S(2)}, u32[]{:S(2)}) %collective-permute-start.10) | collective-permute-done | bytes 163872 | tf_op jit(solution)/shard_map/ppermute | solution.py:451
  62.1 1.4 %collective-permute-start.16 = (f32[64,128]{1,0:T(8,128)S(1)}, f32[64,128]{1,0:T(8,128)S(1)}, u32[]{:S(2)}, u32[]{:S(2)}) collective-permute-start(f32[64,128]{1,0:T(8,128)S(1)} %get-tuple-element.56.rows_own_ref), channel_id=1, source_target_pairs={{0,2},{2,0},{1,3},{3,1},{4,6},{6,4},{5,7},{7,5},{8,10},{10,8},{9,1... | collective-permute-start | bytes 98312 | tf_op jit(solution)/shard_map/ppermute | solution.py:423
  63.5 2.5 %collective-permute-done.16.rows_got_ref = f32[64,128]{1,0:T(8,128)S(1)} collective-permute-done((f32[64,128]{1,0:T(8,128)S(1)}, f32[64,128]{1,0:T(8,128)S(1)}, u32[]{:S(2)}, u32[]{:S(2)}) %collective-permute-start.16) | collective-permute-done | bytes 32800 | tf_op jit(solution)/shard_map/ppermute | solution.py:423
  66.1 3.5 %collective-permute-start.17 = (f32[32,128]{1,0:T(8,128)S(1)}, f32[32,128]{1,0:T(8,128)S(1)}, u32[]{:S(2)}, u32[]{:S(2)}) collective-permute-start(f32[32,128]{1,0:T(8,128)S(1)} %get-tuple-element.58), channel_id=1, source_target_pairs={{0,1},{1,0},{2,3},{3,2},{4,5},{5,4},{6,7},{7,6},{8,9},{9,8},{10,11... | collective-permute-start | bytes 49160 | tf_op jit(solution)/shard_map/ppermute | solution.py:479
  70.6 2.0 %collective-permute-start.18 = (f32[16,128]{1,0:T(8,128)S(1)}, f32[16,128]{1,0:T(8,128)S(1)}, u32[]{:S(2)}, u32[]{:S(2)}) collective-permute-start(f32[16,128]{1,0:T(8,128)S(1)} %get-tuple-element.60), channel_id=1, source_target_pairs={{0,4},{4,0},{8,12},{12,8},{1,5},{5,1},{9,13},{13,9},{2,6},{6,2},{1... | collective-permute-start | bytes 24584 | tf_op jit(solution)/shard_map/ppermute | solution.py:487
  72.5 4.5 %collective-permute-start.19 = (f32[16,128]{1,0:T(8,128)S(1)}, f32[16,128]{1,0:T(8,128)S(1)}, u32[]{:S(2)}, u32[]{:S(2)}) collective-permute-start(f32[16,128]{1,0:T(8,128)S(1)} %get-tuple-element.61), channel_id=1, source_target_pairs={{0,8},{4,12},{8,0},{12,4},{1,9},{5,13},{9,1},{13,5},{2,10},{6,14},... | collective-permute-start | bytes 24584 | tf_op jit(solution)/shard_map/ppermute | solution.py:487
  77.1 1.6 %collective-permute-done.19.refs_2_ = f32[16,128]{1,0:T(8,128)S(1)} collective-permute-done((f32[16,128]{1,0:T(8,128)S(1)}, f32[16,128]{1,0:T(8,128)S(1)}, u32[]{:S(2)}, u32[]{:S(2)}) %collective-permute-start.19) | collective-permute-done | bytes 8224 | tf_op jit(solution)/shard_map/ppermute | solution.py:487
  78.7 3.8 %collective-permute-done.20.refs_3_ = f32[16,128]{1,0:T(8,128)S(1)} collective-permute-done((f32[16,128]{1,0:T(8,128)S(1)}, f32[16,128]{1,0:T(8,128)S(1)}, u32[]{:S(2)}, u32[]{:S(2)}) %collective-permute-start.20) | collective-permute-done | bytes 8224 | tf_op jit(solution)/shard_map/ppermute | solution.py:487
  (45 shorter events, 11.7 us)
Async XLA Ops:
  0.0 46.2 %collective-permute-start.8 = (bf16[1280,2560]{1,0:T(8,128)(2,1)}, bf16[1280,2560]{1,0:T(8,128)(2,1)S(1)}, u32[]{:S(2)}, u32[]{:S(2)}) collective-permute-start(bf16[1280,2560]{1,0:T(8,128)(2,1)} %param.16), channel_id=1, source_target_pairs={{0,0},{1,1},{2,3},{3,2},{4,4},{5,5},{6,7},{7,6},{8,8},{9,9},{10,11... | collective-permute-start | bytes 19660808 | tf_op jit(solution)/shard_map/ppermute | solution.py:396
  3.5 42.7 %collective-permute-start.9 = (bf16[1280,2560]{1,0:T(8,128)(2,1)}, bf16[1280,2560]{1,0:T(8,128)(2,1)S(1)}, u32[]{:S(2)}, u32[]{:S(2)}) collective-permute-start(bf16[1280,2560]{1,0:T(8,128)(2,1)} %param.16), channel_id=1, source_target_pairs={{0,1},{1,0},{2,2},{3,3},{4,5},{5,4},{6,6},{7,7},{8,9},{9,8},{10,10... | collective-permute-start | bytes 19660808 | tf_op jit(solution)/shard_map/ppermute | solution.py:397
  7.1 5.0 %collective-permute-start.3 = (bf16[2,128,640]{2,1,0:T(8,128)(2,1)S(1)}, bf16[2,128,640]{2,1,0:T(8,128)(2,1)S(1)}, u32[]{:S(2)}, u32[]{:S(2)}) collective-permute-start(bf16[2,128,640]{2,1,0:T(8,128)(2,1)S(1)} %get-tuple-element.42), channel_id=1, source_target_pairs={{0,0},{1,8},{4,4},{5,12},{8,1},{9,9},{12,5},{13,13},{2,2},{3,10},{... | collective-permute-start | bytes 983048 | tf_op jit(solution)/shard_map/ppermute | solution.py:393
  7.8 18.5 %collective-permute-start.4 = (bf16[2,128,640]{2,1,0:T(8,128)(2,1)S(1)}, bf16[2,128,640]{2,1,0:T(8,128)(2,1)S(1)}, u32[]{:S(2)}, u32[]{:S(2)}) collective-permute-start(bf16[2,128,640]{2,1,0:T(8,128)(2,1)S(1)} %get-tuple-element.43), channel_id=1, source_target_pairs={{0,4},{1,12},{4,0},{5,8},{8,5},{9,13},{12,1},{13,9},{2,6},{3,14},{... | collective-permute-start | bytes 983048 | tf_op jit(solution)/shard_map/ppermute | solution.py:393
  11.5 14.9 %collective-permute-start.1 = (bf16[1,128,640]{2,1,0:T(8,128)(2,1)S(1)}, bf16[1,128,640]{2,1,0:T(8,128)(2,1)S(1)}, u32[]{:S(2)}, u32[]{:S(2)}) collective-permute-start(bf16[1,128,640]{2,1,0:T(8,128)(2,1)S(1)} %get-tuple-element.37), channel_id=1, source_target_pairs={{0,0},{1,8},{4,4},{5,12},{8,1},{9,9},{12,5},{13,13},{2,2},{3,10},{... | collective-permute-start | bytes 491528 | tf_op jit(solution)/shard_map/ppermute | solution.py:395
  12.1 26.1 %collective-permute-start.5 = (bf16[2,128,640]{2,1,0:T(8,128)(2,1)S(1)}, bf16[2,128,640]{2,1,0:T(8,128)(2,1)S(1)}, u32[]{:S(2)}, u32[]{:S(2)}) collective-permute-start(bf16[2,128,640]{2,1,0:T(8,128)(2,1)S(1)} %collective-permute-done.3.refs_2_), channel_id=1, source_target_pairs={{0,1},{1,0},{2,3},{3,2},{4,5},{5,4},{6,7},{7,6},{8,9},{9,8},{10,11... | collective-permute-start | bytes 983048 | tf_op jit(solution)/shard_map/ppermute | solution.py:398
  26.3 11.9 %collective-permute-start.6 = (bf16[2,128,640]{2,1,0:T(8,128)(2,1)S(1)}, bf16[2,128,640]{2,1,0:T(8,128)(2,1)S(1)}, u32[]{:S(2)}, u32[]{:S(2)}) collective-permute-start(bf16[2,128,640]{2,1,0:T(8,128)(2,1)S(1)} %collective-permute-done.4.refs_3_), channel_id=1, source_target_pairs={{0,1},{1,0},{2,3},{3,2},{4,5},{5,4},{6,7},{7,6},{8,9},{9,8},{10,11... | collective-permute-start | bytes 983048 | tf_op jit(solution)/shard_map/ppermute | solution.py:398
  26.3 7.5 %collective-permute-start.2 = (bf16[1,128,640]{2,1,0:T(8,128)(2,1)S(1)}, bf16[1,128,640]{2,1,0:T(8,128)(2,1)S(1)}, u32[]{:S(2)}, u32[]{:S(2)}) collective-permute-start(bf16[1,128,640]{2,1,0:T(8,128)(2,1)S(1)} %get-tuple-element.38), channel_id=1, source_target_pairs={{0,4},{1,12},{4,0},{5,8},{8,5},{9,13},{12,1},{13,9},{2,6},{3,14},{... | collective-permute-start | bytes 491528 | tf_op jit(solution)/shard_map/ppermute | solution.py:395
  33.8 22.0 %collective-permute-start = (bf16[128,1920]{1,0:T(8,128)(2,1)S(1)}, bf16[128,1920]{1,0:T(8,128)(2,1)S(1)}, u32[]{:S(2)}, u32[]{:S(2)}) collective-permute-start(bf16[128,1920]{1,0:T(8,128)(2,1)S(1)} %get-tuple-element.36), channel_id=1, source_target_pairs={{0,0},{1,8},{4,4},{5,12},{8,1},{9,9},{12,5},{13,13},{2,2},{3,10},{... | collective-permute-start | bytes 1474568 | tf_op jit(solution)/shard_map/ppermute | solution.py:407
  39.4 6.8 %collective-permute-start.7 = (bf16[128,640]{1,0:T(8,128)(2,1)S(1)}, bf16[128,640]{1,0:T(8,128)(2,1)S(1)}, u32[]{:S(2)}, u32[]{:S(2)}) collective-permute-start(bf16[128,640]{1,0:T(8,128)(2,1)S(1)} %get-tuple-element.45), channel_id=1, source_target_pairs={{0,4},{4,0},{8,12},{12,8},{1,5},{5,1},{9,13},{13,9},{2,6},{6,2},{1... | collective-permute-start | bytes 491528 | tf_op jit(solution)/shard_map/ppermute | solution.py:437
  41.5 11.2 %collective-permute-start.13 = (bf16[128,640]{1,0:T(8,128)(2,1)S(1)}, bf16[128,640]{1,0:T(8,128)(2,1)S(1)}, u32[]{:S(2)}, u32[]{:S(2)}) collective-permute-start(bf16[128,640]{1,0:T(8,128)(2,1)S(1)} %get-tuple-element.46), channel_id=1, source_target_pairs={{0,0},{1,8},{4,4},{5,12},{8,1},{9,9},{12,5},{13,13},{2,2},{3,10},{... | collective-permute-start | bytes 491528 | tf_op jit(solution)/shard_map/ppermute | solution.py:407
  46.9 8.6 %collective-permute-start.14 = (bf16[128,640]{1,0:T(8,128)(2,1)S(1)}, bf16[128,640]{1,0:T(8,128)(2,1)S(1)}, u32[]{:S(2)}, u32[]{:S(2)}) collective-permute-start(bf16[128,640]{1,0:T(8,128)(2,1)S(1)} %shard_map.127), channel_id=1, source_target_pairs={{0,2},{2,0},{1,3},{3,1},{4,6},{6,4},{5,7},{7,5},{8,10},{10,8},{9,1... | collective-permute-start | bytes 491528 | tf_op jit(solution)/shard_map/ppermute | solution.py:451
  49.2 6.6 %collective-permute-start.12 = (bf16[128,640]{1,0:T(8,128)(2,1)S(1)}, bf16[128,640]{1,0:T(8,128)(2,1)S(1)}, u32[]{:S(2)}, u32[]{:S(2)}) collective-permute-start(bf16[128,640]{1,0:T(8,128)(2,1)S(1)} %shard_map.126), channel_id=1, source_target_pairs={{0,2},{2,0},{1,3},{3,1},{4,6},{6,4},{5,7},{7,5},{8,10},{10,8},{9,1... | collective-permute-start | bytes 491528 | tf_op jit(solution)/shard_map/ppermute | solution.py:451
  50.3 2.8 %copy-start.1 = (f32[1,2560]{1,0:T(1,128)S(1)}, f32[1,2560]{1,0:T(1,128)}, u32[]{:S(2)}) copy-start(f32[1,2560]{1,0:T(1,128)} %refs_3_.7) | copy-start | bytes 30724
  50.3 7.2 %collective-permute-start.11 = (bf16[128,640]{1,0:T(8,128)(2,1)S(1)}, bf16[128,640]{1,0:T(8,128)(2,1)S(1)}, u32[]{:S(2)}, u32[]{:S(2)}) collective-permute-start(bf16[128,640]{1,0:T(8,128)(2,1)S(1)} %shard_map.125), channel_id=1, source_target_pairs={{0,2},{2,0},{1,3},{3,1},{4,6},{6,4},{5,7},{7,5},{8,10},{10,8},{9,1... | collective-permute-start | bytes 491528 | tf_op jit(solution)/shard_map/ppermute | solution.py:451
  52.6 2.8 %copy-start = (bf16[2560,64]{0,1:T(8,128)(2,1)S(1)}, bf16[2560,64]{0,1:T(8,128)(2,1)}, u32[]{:S(2)}) copy-start(bf16[2560,64]{0,1:T(8,128)(2,1)} %param.20) | copy-start | bytes 983044
  52.7 8.4 %collective-permute-start.10 = (bf16[128,640]{1,0:T(8,128)(2,1)S(1)}, bf16[128,640]{1,0:T(8,128)(2,1)S(1)}, u32[]{:S(2)}, u32[]{:S(2)}) collective-permute-start(bf16[128,640]{1,0:T(8,128)(2,1)S(1)} %shard_map.124), channel_id=1, source_target_pairs={{0,2},{2,0},{1,3},{3,1},{4,6},{6,4},{5,7},{7,5},{8,10},{10,8},{9,1... | collective-permute-start | bytes 491528 | tf_op jit(solution)/shard_map/ppermute | solution.py:451
  55.4 27.1 %copy-start.3 = (f32[1,1,128,32]{2,3,1,0:T(8,128)S(1)}, f32[1,1,128,32]{2,3,1,0:T(8,128)}, u32[]{:S(2)}) copy-start(f32[1,1,128,32]{2,3,1,0:T(8,128)} %param.21) | copy-start | bytes 49156
  61.4 4.6 %collective-permute-start.15 = (f32[72,128]{1,0:T(8,128)S(1)}, f32[72,128]{1,0:T(8,128)S(1)}, u32[]{:S(2)}, u32[]{:S(2)}) collective-permute-start(f32[72,128]{1,0:T(8,128)S(1)} %shard_map.131.own_ref), channel_id=1, source_target_pairs={{0,2},{2,0},{1,3},{3,1},{4,6},{6,4},{5,7},{7,5},{8,10},{10,8},{9,1... | collective-permute-start | bytes 110600 | tf_op jit(solution)/shard_map/ppermute | solution.py:472
  62.1 3.9 %collective-permute-start.16 = (f32[64,128]{1,0:T(8,128)S(1)}, f32[64,128]{1,0:T(8,128)S(1)}, u32[]{:S(2)}, u32[]{:S(2)}) collective-permute-start(f32[64,128]{1,0:T(8,128)S(1)} %get-tuple-element.56.rows_own_ref), channel_id=1, source_target_pairs={{0,2},{2,0},{1,3},{3,1},{4,6},{6,4},{5,7},{7,5},{8,10},{10,8},{9,1... | collective-permute-start | bytes 98312 | tf_op jit(solution)/shard_map/ppermute | solution.py:423
  66.1 4.4 %collective-permute-start.17 = (f32[32,128]{1,0:T(8,128)S(1)}, f32[32,128]{1,0:T(8,128)S(1)}, u32[]{:S(2)}, u32[]{:S(2)}) collective-permute-start(f32[32,128]{1,0:T(8,128)S(1)} %get-tuple-element.58), channel_id=1, source_target_pairs={{0,1},{1,0},{2,3},{3,2},{4,5},{5,4},{6,7},{7,6},{8,9},{9,8},{10,11... | collective-permute-start | bytes 49160 | tf_op jit(solution)/shard_map/ppermute | solution.py:479
  70.6 6.5 %collective-permute-start.18 = (f32[16,128]{1,0:T(8,128)S(1)}, f32[16,128]{1,0:T(8,128)S(1)}, u32[]{:S(2)}, u32[]{:S(2)}) collective-permute-start(f32[16,128]{1,0:T(8,128)S(1)} %get-tuple-element.60), channel_id=1, source_target_pairs={{0,4},{4,0},{8,12},{12,8},{1,5},{5,1},{9,13},{13,9},{2,6},{6,2},{1... | collective-permute-start | bytes 24584 | tf_op jit(solution)/shard_map/ppermute | solution.py:487
  72.5 6.2 %collective-permute-start.19 = (f32[16,128]{1,0:T(8,128)S(1)}, f32[16,128]{1,0:T(8,128)S(1)}, u32[]{:S(2)}, u32[]{:S(2)}) collective-permute-start(f32[16,128]{1,0:T(8,128)S(1)} %get-tuple-element.61), channel_id=1, source_target_pairs={{0,8},{4,12},{8,0},{12,4},{1,9},{5,13},{9,1},{13,5},{2,10},{6,14},... | collective-permute-start | bytes 24584 | tf_op jit(solution)/shard_map/ppermute | solution.py:487
  77.1 5.4 %collective-permute-start.20 = (f32[16,128]{1,0:T(8,128)S(1)}, f32[16,128]{1,0:T(8,128)S(1)}, u32[]{:S(2)}, u32[]{:S(2)}) collective-permute-start(f32[16,128]{1,0:T(8,128)S(1)} %get-tuple-element.62), channel_id=1, source_target_pairs={{0,12},{4,8},{8,4},{12,0},{1,13},{5,9},{9,5},{13,1},{2,14},{6,10},... | collective-permute-start | bytes 24584 | tf_op jit(solution)/shard_map/ppermute | solution.py:487
  (2 other events, 3.5 us)
